TPU v7x, 32 devices: a whole 2x2x4 slice. The times are simulated.
32 devices in a mesh: dp: 8 (over z, x), blk: 4 (over y, core).
Axes of the slice: x: 2, y: 2, z: 4, core: 2. Of those that a mesh axis runs over, the one named last changes fastest.
Arguments:
- tokens: bfloat16 [8, 512, 1280], P('dp', 'blk')
- first_gain: float32 [1280], replicated, may hold values from 0.5 to 1.5
- first_shift: float32 [1280], replicated, may hold values from -3 to 3
- w_qkv: bfloat16 [1280, 3840], replicated, may hold values from -0.15625 to 0.15625
- w_out: bfloat16 [1280, 1280], replicated, may hold values from -2 to 2
- second_gain: float32 [1280], replicated, may hold values from 0.5 to 1.5
- second_shift: float32 [1280], replicated, may hold values from -3 to 3
- w_in: bfloat16 [1280, 5120], replicated, may hold values from -0.15625 to 0.15625
- w_down: bfloat16 [5120, 1280], replicated, may hold values from -0.078125 to 0.078125
- segment_ids: int32 [8, 512], P('dp', 'blk'), may hold values from 0 to 3, as said below
- cls_positions: int32 [8, 4], P('dp'), may hold values from 0 to 511, as said below
- out_grad: bfloat16 [8, 512, 1280], P('dp', 'blk'), may hold values from -6 to 6
Outputs:
- layer_out: bfloat16 [8, 512, 1280], P('dp', 'blk')
- tokens_grad: bfloat16 [8, 512, 1280], P('dp', 'blk')
- grad_qkv: float32 [1280, 3840], P(('dp', 'blk'))
- grad_out: float32 [1280, 1280], P(('dp', 'blk'))
- grad_in: float32 [1280, 5120], P(('dp', 'blk'))
- grad_down: float32 [5120, 1280], P(('dp', 'blk'))
- first_gain_grad: float32 [1280], P(('dp', 'blk'))
- first_shift_grad: float32 [1280], P(('dp', 'blk'))
- second_gain_grad: float32 [1280], P(('dp', 'blk'))
- second_shift_grad: float32 [1280], P(('dp', 'blk'))
- cls_mean: float32 [1280], P(('dp', 'blk'))
- cls_variance: float32 [1280], P(('dp', 'blk'))
Inputs may be any that keep to these rules, and one draw needn't show every extreme that they name: `segment_ids`: in each row the numbers never fall, every cell number has at least one token, and one cell of every row has exactly 256 tokens. `cls_positions`: the first position of each cell of the row, in cell order, consistent with segment_ids.
All inputs are finite; a program needn't handle non-finite values.
Results may differ from a plain program's by a relative error of at most 0.013.
Values may be sent and summed in bfloat16 or wider, within the bound.
A program may use at most 320 MiB of HBM per device.

v0:
```python
import jax
import jax.numpy as jnp
from jax import lax
from jax.sharding import PartitionSpec as P

H = 20


EPSILON = 1e-05


def shifted(block, axis, distance):
    devices = range(lax.axis_size(axis))
    route = [((i - distance) % len(devices), i) for i in devices]
    return lax.ppermute(block, axis, route)


def layer_norm(values, gain, shift):
    center = values - jnp.mean(values, axis=-1, keepdims=True)
    spread = jnp.mean(center * center, axis=-1, keepdims=True)
    return center * lax.rsqrt(spread + EPSILON) * gain + shift


def exact_gelu(values):
    return jax.nn.gelu(values, approximate=False)


def same_cells(query_cells, key_cells):
    return query_cells[:, :, None] == key_cells[:, None, :]


def forward_block(queries, key_part, value_part, query_cells, key_cells, totals, weights):
    scores = jnp.einsum("sqhd,skhd->shqk", queries, key_part, preferred_element_type=jnp.float32)
    exp_scores = jnp.where(same_cells(query_cells, key_cells)[:, None], jnp.exp(scores), 0.0)
    weights = weights + jnp.sum(exp_scores, axis=-1)
    totals = totals + jnp.einsum(
        "shqk,skhd->sqhd",
        exp_scores.astype(jnp.bfloat16),
        value_part,
        preferred_element_type=jnp.float32,
    )
    return (totals, weights)


def backward_block(queries, scaled, deltas, query_cells, key_part, value_part, key_cells):
    scores = jnp.einsum("sqhd,skhd->shqk", queries, key_part, preferred_element_type=jnp.float32)
    exp_scores = jnp.where(same_cells(query_cells, key_cells)[:, None], jnp.exp(scores), 0.0)
    grad_exp = jnp.einsum("sqhd,skhd->shqk", scaled, value_part, preferred_element_type=jnp.float32)
    grad_scores = (exp_scores * (grad_exp - deltas[..., None])).astype(jnp.bfloat16)
    grad_queries = jnp.einsum(
        "shqk,skhd->sqhd", grad_scores, key_part, preferred_element_type=jnp.float32
    )
    grad_keys = jnp.einsum(
        "shqk,sqhd->skhd", grad_scores, queries, preferred_element_type=jnp.float32
    )
    grad_values = jnp.einsum(
        "shqk,sqhd->skhd",
        exp_scores.astype(jnp.bfloat16),
        scaled,
        preferred_element_type=jnp.float32,
    )
    return (grad_queries, grad_keys, grad_values)


def on_device(
    tokens,
    first_gain,
    first_shift,
    w_qkv,
    w_out,
    second_gain,
    second_shift,
    w_in,
    w_down,
    segment_ids,
    cls_positions,
    out_grad,
):
    seqs_here, block_len, width = tokens.shape
    head_count = H
    head_size = width // head_count
    blocks = lax.axis_size("blk")
    head_shape = (seqs_here, block_len, head_count, head_size)
    flat_shape = (seqs_here, block_len, width)
    tokens_wide = tokens.astype(jnp.float32)
    normed_low = layer_norm(tokens_wide, first_gain, first_shift).astype(jnp.bfloat16)
    projected = jnp.dot(normed_low, w_qkv, preferred_element_type=jnp.float32)
    queries = (projected[..., :width] * 0.125).astype(jnp.bfloat16).reshape(head_shape)
    key_part = projected[..., width : 2 * width].astype(jnp.bfloat16).reshape(head_shape)
    value_part = projected[..., 2 * width :].astype(jnp.bfloat16).reshape(head_shape)
    totals = jnp.zeros(head_shape, jnp.float32)
    weights = jnp.zeros((seqs_here, head_count, block_len), jnp.float32)
    totals, weights = forward_block(
        queries, key_part, value_part, segment_ids, segment_ids, totals, weights
    )

    def forward_step(position, loop_state):
        moving, totals_in, weights_in = loop_state
        moving = shifted((moving[0], moving[1], moving[2]), "blk", 1)
        totals_out, weights_out = forward_block(
            queries, moving[0], moving[1], segment_ids, moving[2], totals_in, weights_in
        )
        return (moving, totals_out, weights_out)

    moved_state, totals, weights = lax.fori_loop(
        0, blocks - 1, forward_step, ((key_part, value_part, segment_ids), totals, weights)
    )
    weights_rows = jnp.swapaxes(weights, 1, 2)[..., None]
    attended = totals / weights_rows
    attended_low = attended.reshape(flat_shape).astype(jnp.bfloat16)
    residual = tokens_wide + jnp.dot(attended_low, w_out, preferred_element_type=jnp.float32)
    normed_two_low = layer_norm(residual, second_gain, second_shift).astype(jnp.bfloat16)
    hidden_pre = jnp.dot(normed_two_low, w_in, preferred_element_type=jnp.float32)
    hidden_low = exact_gelu(hidden_pre).astype(jnp.bfloat16)
    layer = residual + jnp.dot(hidden_low, w_down, preferred_element_type=jnp.float32)
    offset = lax.axis_index("blk") * block_len
    places = (
        lax.broadcasted_iota(jnp.int32, (seqs_here, cls_positions.shape[1], block_len), 2) + offset
    )
    chosen = jnp.sum((places == cls_positions[:, :, None]).astype(jnp.float32), axis=1)
    cell_sums = jnp.sum(chosen[..., None] * layer, axis=(0, 1))
    cell_squares = jnp.sum(chosen[..., None] * layer * layer, axis=(0, 1))
    count = cls_positions.shape[0] * cls_positions.shape[1] * lax.axis_size("dp")
    share = width // (lax.axis_size("dp") * blocks)
    moment_sums = lax.psum((cell_sums, cell_squares), ("dp", "blk"))
    rank = lax.axis_index("dp") * blocks + lax.axis_index("blk")
    sum_share = lax.dynamic_slice_in_dim(moment_sums[0], rank * share, share)
    square_share = lax.dynamic_slice_in_dim(moment_sums[1], rank * share, share)
    grad_layer = out_grad.astype(jnp.float32)
    grad_down = jnp.einsum("sbf,sbd->fd", hidden_low, out_grad, preferred_element_type=jnp.float32)
    grad_hidden = jnp.einsum("sbd,fd->sbf", out_grad, w_down, preferred_element_type=jnp.float32)
    grad_pre = jax.vjp(exact_gelu, hidden_pre)[1](grad_hidden)[0].astype(jnp.bfloat16)
    grad_in = jnp.einsum(
        "sbd,sbf->df", normed_two_low, grad_pre, preferred_element_type=jnp.float32
    )
    grad_normed_two = jnp.einsum("sbf,df->sbd", grad_pre, w_in, preferred_element_type=jnp.float32)
    unused_two, pull_two = jax.vjp(layer_norm, residual, second_gain, second_shift)
    residual_part, second_gain_grad, second_shift_grad = pull_two(grad_normed_two)
    grad_residual = grad_layer + residual_part
    grad_proj = grad_residual.astype(jnp.bfloat16)
    grad_out = jnp.einsum(
        "sbd,sbe->de", attended_low, grad_proj, preferred_element_type=jnp.float32
    )
    grad_attended = jnp.einsum(
        "sbe,de->sbd", grad_proj, w_out, preferred_element_type=jnp.float32
    ).reshape(head_shape)
    scaled = (grad_attended / weights_rows).astype(jnp.bfloat16)
    deltas = jnp.swapaxes(jnp.sum(grad_attended * attended, axis=-1), 1, 2) / weights

    def key_step(position, loop_state):
        moving, key_sums, query_sum = loop_state
        grad_queries, grad_keys, grad_values = backward_block(
            queries, scaled, deltas, segment_ids, moving[0], moving[1], moving[2]
        )
        query_next = query_sum + grad_queries
        keys_next = key_sums[0] + grad_keys
        values_next = key_sums[1] + grad_values
        moving = shifted((moving[0], moving[1], moving[2]), "blk", 1)
        key_sums = (
            shifted(keys_next.astype(jnp.bfloat16), "blk", 1).astype(keys_next.dtype),
            shifted(values_next.astype(jnp.bfloat16), "blk", 1).astype(values_next.dtype),
        )
        return (moving, key_sums, query_next)

    zero_heads = jnp.zeros(head_shape, jnp.float32)
    moved_back, key_sums, query_total = lax.fori_loop(
        0,
        blocks,
        key_step,
        ((key_part, value_part, segment_ids), (zero_heads, zero_heads), zero_heads),
    )
    keys_total, values_total = (key_sums[0], key_sums[1])
    grad_qkv_low = jnp.concatenate(
        [
            (query_total * 0.125).reshape(flat_shape),
            keys_total.reshape(flat_shape),
            values_total.reshape(flat_shape),
        ],
        axis=-1,
    ).astype(jnp.bfloat16)
    grad_qkv = jnp.einsum(
        "sbd,sbe->de", normed_low, grad_qkv_low, preferred_element_type=jnp.float32
    )
    grad_normed_one = jnp.einsum(
        "sbe,de->sbd", grad_qkv_low, w_qkv, preferred_element_type=jnp.float32
    )
    unused_one, pull_one = jax.vjp(layer_norm, tokens_wide, first_gain, first_shift)
    tokens_part, first_gain_grad, first_shift_grad = pull_one(grad_normed_one)
    tokens_grad = (grad_residual + tokens_part).astype(jnp.bfloat16)
    summed = (
        lax.psum_scatter(grad_qkv, ("dp", "blk"), scatter_dimension=0, tiled=True),
        lax.psum_scatter(grad_out, ("dp", "blk"), scatter_dimension=0, tiled=True),
        lax.psum_scatter(grad_in, ("dp", "blk"), scatter_dimension=0, tiled=True),
        lax.psum_scatter(grad_down, ("dp", "blk"), scatter_dimension=0, tiled=True),
        lax.psum_scatter(first_gain_grad, ("dp", "blk"), scatter_dimension=0, tiled=True),
        lax.psum_scatter(first_shift_grad, ("dp", "blk"), scatter_dimension=0, tiled=True),
        lax.psum_scatter(second_gain_grad, ("dp", "blk"), scatter_dimension=0, tiled=True),
        lax.psum_scatter(second_shift_grad, ("dp", "blk"), scatter_dimension=0, tiled=True),
    )
    cls_mean = sum_share / count
    cls_variance = square_share / count - cls_mean * cls_mean
    return (
        layer.astype(jnp.bfloat16),
        tokens_grad,
        summed[0],
        summed[1],
        summed[2],
        summed[3],
        summed[4],
        summed[5],
        summed[6],
        summed[7],
        cls_mean,
        cls_variance,
    )


def solution(mesh):
    placed = (
        P("dp", "blk", None),
        P(),
        P(),
        P(),
        P(),
        P(),
        P(),
        P(),
        P(),
        P("dp", "blk"),
        P("dp", None),
        P("dp", "blk", None),
    )
    return jax.shard_map(
        on_device,
        mesh=mesh,
        in_specs=placed,
        out_specs=(
            P("dp", "blk", None),
            P("dp", "blk", None),
            P(("dp", "blk"), None),
            P(("dp", "blk"), None),
            P(("dp", "blk"), None),
            P(("dp", "blk"), None),
            P(("dp", "blk")),
            P(("dp", "blk")),
            P(("dp", "blk")),
            P(("dp", "blk")),
            P(("dp", "blk")),
            P(("dp", "blk")),
        ),
        check_vma=False,
    )
```

profile of v0, /device:TPU:0, one launch (start us, length us, event | category | flops | bytes accessed | tf_op | source)
XLA Modules:
  0.0 1064.6 jit_solution(13084297685438267267)
XLA Ops:
  11.3 6.8 fusion.74
  19.0 1.9 copy.57
  20.8 1.9 copy.56
  22.7 1.7 copy.68
  24.4 1.7 copy.69
  26.1 1.9 fusion.44
  28.0 1.9 copy.59
  31.5 2.1 convolution_bitcast_fusion.7
  33.6 43.2 %while.39 = (s32[]{:T(128)}, bf16[1,128,20,64]{1,3,2,0:T(8,128)(2,1)}, bf16[1,128,20,64]{1,3,2,0:T(8,128)(2,1)}, s32[1,128]{1,0:T(1,128)S(1)}, f32[1,128,20,64]{...) while((s32[]{:T(128)}, ...), condition=%wide.region_5.6_spmd, body=%wide.region_3.5_spmd.sunk | while | flops 85377024 | bytes 12873997 | solution.py:105
  34.0 2.6 collective-permute-start.2
  36.7 4.4 collective-permute-done.2
  42.7 1.7 copy.80
  44.6 1.7 copy.81
  48.4 2.4 collective-permute-start.2
  50.9 4.4 collective-permute-done.2
  56.9 1.7 copy.80
  58.8 1.7 copy.81
  62.6 2.4 collective-permute-start.2
  65.1 4.4 collective-permute-done.2
  71.1 1.7 copy.80
  73.0 1.7 copy.81
  78.0 1.7 fusion.76
  80.0 6.7 fusion.70
  88.4 12.1 %add_convert_fusion = bf16[128,5120]{1,0:T(8,128)(2,1)S(1)} fusion(f32[128,5120]{1,0:T(8,128)S(1)} %fusion.70, bf16[5120,1280]{1,0:T(8,128)(2,1)} %param.24, bf16[1,128,1280]{2,1,0:T(8,128)(2,1)S(1)} %copy-done.20), kind=kOutput, calls=%fused_computation.38 | convolution fusion | flops 1724907520 | bytes 17367040 | tf_op jit(solution)/shard_map/sbd,fd->sbf/dot_general | solution.py:131
  100.4 9.7 fusion.45
  112.7 3.7 fusion.78
  116.8 2.0 fusion.77
  119.0 144.5 %while.40 = (s32[]{:T(128)}, bf16[1,128,20,64]{1,3,2,0:T(8,128)(2,1)}, bf16[1,128,20,64]{1,3,2,0:T(8,128)(2,1)}, s32[1,128]{1,0:T(1,128)S(1)}, f32[1,128,20,64]{...) while((s32[]{:T(128)}, ...), condition=%wide.region_12.13_spmd.clone, body=%wide.region_11.12_spmd.clone.sunk | while | flops 213008384 | bytes 26589632 | solution.py:166
  125.3 2.4 collective-permute-start.7
  129.1 6.8 collective-permute-done.6
  136.0 1.9 convert_element_type.211
  137.8 5.3 collective-permute-done.7
  144.0 11.4 %collective-permute-done.5 = s32[1,128]{1,0:T(1,128)S(1)} collective-permute-done((s32[1,128]{1,0:T(1,128)S(1)}, s32[1,128]{1,0:T(1,128)S(1)}, u32[]{:S(2)}, u32[]{:S(2)}) %collective-permute-start.5) | collective-permute-done | bytes 544 | tf_op jit(solution)/shard_map/while/body/eval_jaxpr/ppermute | solution.py:15
  160.4 2.1 fusion.130
  162.5 2.5 collective-permute-start.6
  166.0 2.5 collective-permute-start.7
  168.6 2.5 fusion.132
  172.5 1.9 convert_element_type.211
  174.3 5.7 collective-permute-done.7
  180.9 12.5 %collective-permute-done.5 = s32[1,128]{1,0:T(1,128)S(1)} collective-permute-done((s32[1,128]{1,0:T(1,128)S(1)}, s32[1,128]{1,0:T(1,128)S(1)}, u32[]{:S(2)}, u32[]{:S(2)}) %collective-permute-start.5) | collective-permute-done | bytes 544 | tf_op jit(solution)/shard_map/while/body/eval_jaxpr/ppermute | solution.py:15
  198.4 2.1 fusion.130
  200.6 1.7 collective-permute-start.6
  203.3 2.6 collective-permute-start.7
  206.0 2.5 fusion.132
  208.5 1.9 convert_element_type.211
  210.4 5.3 collective-permute-done.7
  216.6 12.7 %collective-permute-done.5 = s32[1,128]{1,0:T(1,128)S(1)} collective-permute-done((s32[1,128]{1,0:T(1,128)S(1)}, s32[1,128]{1,0:T(1,128)S(1)}, u32[]{:S(2)}, u32[]{:S(2)}) %collective-permute-start.5) | collective-permute-done | bytes 544 | tf_op jit(solution)/shard_map/while/body/eval_jaxpr/ppermute | solution.py:15
  234.3 2.1 fusion.130
  236.4 1.8 collective-permute-start.6
  239.2 2.7 collective-permute-start.7
  242.0 2.5 fusion.132
  244.5 1.9 convert_element_type.211
  246.3 4.9 collective-permute-done.7
  252.1 10.6 collective-permute-done.5
  267.0 8.2 fusion.49
  276.2 16.0 %fusion.54 = f32[5120,1280]{1,0:T(8,128)} fusion(bf16[1,128,1280]{2,1,0:T(8,128)(2,1)S(1)} %copy-done.21, f32[128,5120]{1,0:T(8,128)} %copy-done.19), kind=kOutput, calls=%fused_computation.99 | convolution fusion | flops 1720320000 | bytes 29163520 | tf_op jit(solution)/shard_map/sbf,sbd->fd/dot_general | solution.py:130
  293.9 12.6 %fusion.68 = f32[1280,5120]{1,0:T(8,128)} fusion(bf16[128,5120]{1,0:T(8,128)(2,1)S(1)} %copy-done.17, f32[1,128,1280]{2,1,0:T(8,128)S(1)} %copy-done.7, f32[1280]{0:T(1024)S(1)} %copy-done.24, f32[1280]{0:T(1024)S(1)} %copy-done.22, f32[128]{0:T(128)S(1)} %fusion.62, f32[128]{0:T(128)S(1)} %broadcast_multiply_fusion), kind=kOutput, calls=%fused_computation.124 | convolution fusion | flops 1678540800 | bytes 28191744 | tf_op jit(solution)/shard_map/sbd,sbf->df/dot_general | solution.py:133
  307.8 8.0 fusion.43
  317.0 12.5 %fusion.41 = (f32[1280]{0:T(1024)S(1)}, f32[1280]{0:T(1024)S(1)}, bf16[1,128,1280]{2,1,0:T(8,128)(2,1)}) fusion(f32[128]{0:T(128)S(1)} %convert_reduce_fusion.1, f32[1,128,1280]{2,1,0:T(8,128)} %copy-done.6, bf16[5120,1280]{1,0:T(8,128)(2,1)} %param.24, f32[128,5120]{1,0:T(8,128)} %copy-done.19), kind=kOutput, calls=%fused_computation.76 | convolution fusion | flops 1721300480 | bytes 16722432 | tf_op jit(solution)/shard_map/dot_general | solution.py:115
  329.5 49.0 %all-reduce.4 = (f32[1280]{0:T(1024)S(1)}, f32[1280]{0:T(1024)S(1)}, f32[1280]{0:T(1024)S(1)}, f32[1280]{0:T(1024)S(1)}, f32[1280]{0:T(1024)S(1)}, /*index=5*/f32[1280]{0:T(1024)S(1)}) all-reduce(f32[1280]{0:T(1024)S(1)} %get-tuple-element.176, f32[1280]{0:T(1024)S(1)} %reduce_sum.191, ...), channel_id=6, replica_groups=mesh['dp'=8,'blk'=4] {'dp','blk'}, use_global_device_ids=true, to_apply=%region_20.21.clone | all-reduce | flops 7680 | bytes 61440
  381.5 2.6 add_convert_fusion.1
  384.1 107.9 %reduce-scatter.5.cloned.1.call-done = f32[40,3840]{1,0:T(8,128)} async-done(((f32[1280,3840]{1,0:T(8,128)}), f32[40,3840]{1,0:T(8,128)}) %reduce-scatter.5.cloned.1.call-update) | async-done | bytes 614416 | tf_op jit(solution)/shard_map/reduce_scatter | solution.py:191
  491.9 281.9 %reduce-scatter.11.cloned.1.call-done = f32[160,1280]{1,0:T(8,128)} async-done(((f32[5120,1280]{1,0:T(8,128)}), f32[160,1280]{1,0:T(8,128)}) %reduce-scatter.11.cloned.1.call-update) | async-done | bytes 819216 | tf_op jit(solution)/shard_map/reduce_scatter | solution.py:194
  773.8 284.2 %reduce-scatter.9.cloned.1.call-done = f32[40,5120]{1,0:T(8,128)} async-done(((f32[1280,5120]{1,0:T(8,128)}), f32[40,5120]{1,0:T(8,128)}) %reduce-scatter.9.cloned.1.call-update) | async-done | bytes 819216 | tf_op jit(solution)/shard_map/reduce_scatter | solution.py:193
  (219 shorter events, 67.7 us)
Async XLA Ops:
  7.2 70.8 %copy-start = (bf16[1280,1280]{1,0:T(8,128)(2,1)S(1)}, bf16[1280,1280]{1,0:T(8,128)(2,1)}, u32[]{:S(2)}) copy-start(bf16[1280,1280]{1,0:T(8,128)(2,1)} %param.20) | copy-start | bytes 9830404
  7.2 376.9 %reduce-scatter.7.cloned.1.call-start = ((), (), s32[]{:S(2)}) async-start(), calls=%async_computation.5 | async-start | bytes 6758400 | tf_op jit(solution)/shard_map/reduce_scatter | solution.py:192
  26.1 7.4 copy-start.26
  33.6 7.6 collective-permute-start
  34.0 7.0 collective-permute-start.2
  36.7 7.9 collective-permute-start.1
  36.7 9.6 copy-start.2
  48.4 6.9 collective-permute-start
  48.4 6.8 collective-permute-start.2
  50.9 7.9 collective-permute-start.1
  50.9 9.6 copy-start.2
  62.6 6.9 collective-permute-start
  62.6 6.8 collective-permute-start.2
  65.0 7.9 collective-permute-start.1
  65.1 9.6 copy-start.2
  78.0 2.0 copy-start.22
  78.0 2.0 copy-start.24
  79.7 30.5 %copy-start.6 = (f32[1,128,1280]{2,1,0:T(8,128)}, f32[1,128,1280]{2,1,0:T(8,128)S(1)}, u32[]{:S(2)}) copy-start(f32[1,128,1280]{2,1,0:T(8,128)S(1)} %get-tuple-element.240) | copy-start | bytes 1966084
  80.0 8.4 copy-start.20
  86.7 1.7 copy-start.19
  100.4 9.7 copy-start.16
  111.0 0.8 copy-start.15
  116.5 375.5 %reduce-scatter.5.cloned.1.call-start = ((), (), s32[]{:S(2)}) async-start(), calls=%async_computation.4 | async-start | bytes 20275200 | tf_op jit(solution)/shard_map/reduce_scatter | solution.py:191
  116.8 2.1 copy-start.4
  120.0 3.1 copy-start.5
  122.5 1.7 copy-start.8
  124.2 11.7 %collective-permute-start.6 = (bf16[1,128,20,64]{1,3,2,0:T(8,128)(2,1)}, bf16[1,128,20,64]{1,3,2,0:T(8,128)(2,1)}, u32[]{:S(2)}, u32[]{:S(2)}) collective-permute-start(bf16[1,128,20,64]{1,3,2,0:T(8,128)(2,1)} %fusion.130), channel_id=1, source_target_pairs={{3,0},{0,1},{1,2},{2,3},{7,4},{4,5},{5,6},{6,7},{11,8},{8,9},{9,10... | collective-permute-start | bytes 983048 | tf_op jit(solution)/shard_map/while/body/eval_jaxpr/ppermute | solution.py:15
  125.3 17.9 %collective-permute-start.7 = (bf16[1,128,20,64]{1,3,2,0:T(8,128)(2,1)}, bf16[1,128,20,64]{1,3,2,0:T(8,128)(2,1)S(1)}, u32[]{:S(2)}, u32[]{:S(2)}) collective-permute-start(bf16[1,128,20,64]{1,3,2,0:T(8,128)(2,1)} %fusion.131), channel_id=1, source_target_pairs={{3,0},{0,1},{1,2},{2,3},{7,4},{4,5},{5,6},{6,7},{11,8},{8,9},{9,10... | collective-permute-start | bytes 983048 | tf_op jit(solution)/shard_map/while/body/eval_jaxpr/ppermute | solution.py:15
  127.7 27.8 %collective-permute-start.4 = (bf16[1,128,20,64]{1,3,2,0:T(8,128)(2,1)S(1)}, bf16[1,128,20,64]{1,3,2,0:T(8,128)(2,1)S(1)}, u32[]{:S(2)}, u32[]{:S(2)}) collective-permute-start(bf16[1,128,20,64]{1,3,2,0:T(8,128)(2,1)S(1)} %copy.94), channel_id=1, source_target_pairs={{3,0},{0,1},{1,2},{2,3},{7,4},{4,5},{5,6},{6,7},{11,8},{8,9},{9,10... | collective-permute-start | bytes 983048 | tf_op jit(solution)/shard_map/while/body/eval_jaxpr/ppermute | solution.py:15
  127.7 27.8 %collective-permute-start.3 = (bf16[1,128,20,64]{1,3,2,0:T(8,128)(2,1)S(1)}, bf16[1,128,20,64]{1,3,2,0:T(8,128)(2,1)S(1)}, u32[]{:S(2)}, u32[]{:S(2)}) collective-permute-start(bf16[1,128,20,64]{1,3,2,0:T(8,128)(2,1)S(1)} %copy.93), channel_id=1, source_target_pairs={{3,0},{0,1},{1,2},{2,3},{7,4},{4,5},{5,6},{6,7},{11,8},{8,9},{9,10... | collective-permute-start | bytes 983048 | tf_op jit(solution)/shard_map/while/body/eval_jaxpr/ppermute | solution.py:15
  127.7 27.7 %collective-permute-start.5 = (s32[1,128]{1,0:T(1,128)S(1)}, s32[1,128]{1,0:T(1,128)S(1)}, u32[]{:S(2)}, u32[]{:S(2)}) collective-permute-start(s32[1,128]{1,0:T(1,128)S(1)} %copy.95), channel_id=1, source_target_pairs={{3,0},{0,1},{1,2},{2,3},{7,4},{4,5},{5,6},{6,7},{11,8},{8,9},{9,10... | collective-permute-start | bytes 1544 | tf_op jit(solution)/shard_map/while/body/eval_jaxpr/ppermute | solution.py:15
  157.2 3.1 copy-start.5
  159.7 5.3 copy-start.8
  162.5 9.9 collective-permute-start.6
  166.0 14.0 %collective-permute-start.7 = (bf16[1,128,20,64]{1,3,2,0:T(8,128)(2,1)}, bf16[1,128,20,64]{1,3,2,0:T(8,128)(2,1)S(1)}, u32[]{:S(2)}, u32[]{:S(2)}) collective-permute-start(bf16[1,128,20,64]{1,3,2,0:T(8,128)(2,1)} %fusion.131), channel_id=1, source_target_pairs={{3,0},{0,1},{1,2},{2,3},{7,4},{4,5},{5,6},{6,7},{11,8},{8,9},{9,10... | collective-permute-start | bytes 983048 | tf_op jit(solution)/shard_map/while/body/eval_jaxpr/ppermute | solution.py:15
  168.5 24.9 %collective-permute-start.4 = (bf16[1,128,20,64]{1,3,2,0:T(8,128)(2,1)S(1)}, bf16[1,128,20,64]{1,3,2,0:T(8,128)(2,1)S(1)}, u32[]{:S(2)}, u32[]{:S(2)}) collective-permute-start(bf16[1,128,20,64]{1,3,2,0:T(8,128)(2,1)S(1)} %copy.94), channel_id=1, source_target_pairs={{3,0},{0,1},{1,2},{2,3},{7,4},{4,5},{5,6},{6,7},{11,8},{8,9},{9,10... | collective-permute-start | bytes 983048 | tf_op jit(solution)/shard_map/while/body/eval_jaxpr/ppermute | solution.py:15
  168.5 24.9 %collective-permute-start.3 = (bf16[1,128,20,64]{1,3,2,0:T(8,128)(2,1)S(1)}, bf16[1,128,20,64]{1,3,2,0:T(8,128)(2,1)S(1)}, u32[]{:S(2)}, u32[]{:S(2)}) collective-permute-start(bf16[1,128,20,64]{1,3,2,0:T(8,128)(2,1)S(1)} %copy.93), channel_id=1, source_target_pairs={{3,0},{0,1},{1,2},{2,3},{7,4},{4,5},{5,6},{6,7},{11,8},{8,9},{9,10... | collective-permute-start | bytes 983048 | tf_op jit(solution)/shard_map/while/body/eval_jaxpr/ppermute | solution.py:15
  168.6 24.9 %collective-permute-start.5 = (s32[1,128]{1,0:T(1,128)S(1)}, s32[1,128]{1,0:T(1,128)S(1)}, u32[]{:S(2)}, u32[]{:S(2)}) collective-permute-start(s32[1,128]{1,0:T(1,128)S(1)} %copy.95), channel_id=1, source_target_pairs={{3,0},{0,1},{1,2},{2,3},{7,4},{4,5},{5,6},{6,7},{11,8},{8,9},{9,10... | collective-permute-start | bytes 1544 | tf_op jit(solution)/shard_map/while/body/eval_jaxpr/ppermute | solution.py:15
  195.3 3.1 copy-start.5
  197.8 4.5 copy-start.8
  200.6 7.9 collective-permute-start.6
  203.3 12.4 %collective-permute-start.7 = (bf16[1,128,20,64]{1,3,2,0:T(8,128)(2,1)}, bf16[1,128,20,64]{1,3,2,0:T(8,128)(2,1)S(1)}, u32[]{:S(2)}, u32[]{:S(2)}) collective-permute-start(bf16[1,128,20,64]{1,3,2,0:T(8,128)(2,1)} %fusion.131), channel_id=1, source_target_pairs={{3,0},{0,1},{1,2},{2,3},{7,4},{4,5},{5,6},{6,7},{11,8},{8,9},{9,10... | collective-permute-start | bytes 983048 | tf_op jit(solution)/shard_map/while/body/eval_jaxpr/ppermute | solution.py:15
  205.9 23.4 %collective-permute-start.4 = (bf16[1,128,20,64]{1,3,2,0:T(8,128)(2,1)S(1)}, bf16[1,128,20,64]{1,3,2,0:T(8,128)(2,1)S(1)}, u32[]{:S(2)}, u32[]{:S(2)}) collective-permute-start(bf16[1,128,20,64]{1,3,2,0:T(8,128)(2,1)S(1)} %copy.94), channel_id=1, source_target_pairs={{3,0},{0,1},{1,2},{2,3},{7,4},{4,5},{5,6},{6,7},{11,8},{8,9},{9,10... | collective-permute-start | bytes 983048 | tf_op jit(solution)/shard_map/while/body/eval_jaxpr/ppermute | solution.py:15
  205.9 23.4 %collective-permute-start.3 = (bf16[1,128,20,64]{1,3,2,0:T(8,128)(2,1)S(1)}, bf16[1,128,20,64]{1,3,2,0:T(8,128)(2,1)S(1)}, u32[]{:S(2)}, u32[]{:S(2)}) collective-permute-start(bf16[1,128,20,64]{1,3,2,0:T(8,128)(2,1)S(1)} %copy.93), channel_id=1, source_target_pairs={{3,0},{0,1},{1,2},{2,3},{7,4},{4,5},{5,6},{6,7},{11,8},{8,9},{9,10... | collective-permute-start | bytes 983048 | tf_op jit(solution)/shard_map/while/body/eval_jaxpr/ppermute | solution.py:15
  206.0 23.4 %collective-permute-start.5 = (s32[1,128]{1,0:T(1,128)S(1)}, s32[1,128]{1,0:T(1,128)S(1)}, u32[]{:S(2)}, u32[]{:S(2)}) collective-permute-start(s32[1,128]{1,0:T(1,128)S(1)} %copy.95), channel_id=1, source_target_pairs={{3,0},{0,1},{1,2},{2,3},{7,4},{4,5},{5,6},{6,7},{11,8},{8,9},{9,10... | collective-permute-start | bytes 1544 | tf_op jit(solution)/shard_map/while/body/eval_jaxpr/ppermute | solution.py:15
  231.1 3.1 copy-start.5
  233.6 4.6 copy-start.8
  236.4 8.0 collective-permute-start.6
  239.2 12.0 %collective-permute-start.7 = (bf16[1,128,20,64]{1,3,2,0:T(8,128)(2,1)}, bf16[1,128,20,64]{1,3,2,0:T(8,128)(2,1)S(1)}, u32[]{:S(2)}, u32[]{:S(2)}) collective-permute-start(bf16[1,128,20,64]{1,3,2,0:T(8,128)(2,1)} %fusion.131), channel_id=1, source_target_pairs={{3,0},{0,1},{1,2},{2,3},{7,4},{4,5},{5,6},{6,7},{11,8},{8,9},{9,10... | collective-permute-start | bytes 983048 | tf_op jit(solution)/shard_map/while/body/eval_jaxpr/ppermute | solution.py:15
  241.9 20.8 %collective-permute-start.4 = (bf16[1,128,20,64]{1,3,2,0:T(8,128)(2,1)S(1)}, bf16[1,128,20,64]{1,3,2,0:T(8,128)(2,1)S(1)}, u32[]{:S(2)}, u32[]{:S(2)}) collective-permute-start(bf16[1,128,20,64]{1,3,2,0:T(8,128)(2,1)S(1)} %copy.94), channel_id=1, source_target_pairs={{3,0},{0,1},{1,2},{2,3},{7,4},{4,5},{5,6},{6,7},{11,8},{8,9},{9,10... | collective-permute-start | bytes 983048 | tf_op jit(solution)/shard_map/while/body/eval_jaxpr/ppermute | solution.py:15
  241.9 20.8 %collective-permute-start.3 = (bf16[1,128,20,64]{1,3,2,0:T(8,128)(2,1)S(1)}, bf16[1,128,20,64]{1,3,2,0:T(8,128)(2,1)S(1)}, u32[]{:S(2)}, u32[]{:S(2)}) collective-permute-start(bf16[1,128,20,64]{1,3,2,0:T(8,128)(2,1)S(1)} %copy.93), channel_id=1, source_target_pairs={{3,0},{0,1},{1,2},{2,3},{7,4},{4,5},{5,6},{6,7},{11,8},{8,9},{9,10... | collective-permute-start | bytes 983048 | tf_op jit(solution)/shard_map/while/body/eval_jaxpr/ppermute | solution.py:15
  241.9 20.7 %collective-permute-start.5 = (s32[1,128]{1,0:T(1,128)S(1)}, s32[1,128]{1,0:T(1,128)S(1)}, u32[]{:S(2)}, u32[]{:S(2)}) collective-permute-start(s32[1,128]{1,0:T(1,128)S(1)} %copy.95), channel_id=1, source_target_pairs={{3,0},{0,1},{1,2},{2,3},{7,4},{4,5},{5,6},{6,7},{11,8},{8,9},{9,10... | collective-permute-start | bytes 1544 | tf_op jit(solution)/shard_map/while/body/eval_jaxpr/ppermute | solution.py:15
  263.5 3.5 copy-start.10
  263.5 3.5 copy-start.23
  263.5 3.5 copy-start.25
  275.2 1.0 copy-start.21
  275.3 498.6 %reduce-scatter.11.cloned.1.call-start = ((), (), s32[]{:S(2)}) async-start(), calls=%async_computation.7 | async-start | bytes 27033600 | tf_op jit(solution)/shard_map/reduce_scatter | solution.py:194
  292.2 1.2 copy-start.7
  292.2 1.7 copy-start.17
  292.3 765.8 %reduce-scatter.9.cloned.1.call-start = ((), (), s32[]{:S(2)}) async-start(), calls=%async_computation.6 | async-start | bytes 27033600 | tf_op jit(solution)/shard_map/reduce_scatter | solution.py:193
  306.6 1.2 copy-start.13
  307.8 8.1 copy-start.27
  315.8 0.8 copy-start.14
  317.0 741.1 %copy-start.1 = (bf16[1280,1280]{1,0:T(8,128)(2,1)S(1)}, bf16[1280,1280]{1,0:T(8,128)(2,1)}, u32[]{:S(2)}) copy-start(bf16[1280,1280]{1,0:T(8,128)(2,1)} %param.20) | copy-start | bytes 9830404
  (13 other events, 10.3 us)
Sparse Core Ops, SparseCore 0:
  116.6 148.1 reduce-scatter.6
  275.4 216.5 reduce-scatter.4
  494.8 278.9 reduce-scatter.10
  776.6 281.4 reduce-scatter.8
where the time goes:
time: 1070 us; the launch traced here: 1060 us
  waiting for transfers between devices  764 us (71%)
  matrix products  141 us (13%)
  blocking collectives  49 us (5%)
  local copies, waits for them, and re-layouts  45 us (4%)
  other arithmetic  26 us (2%)
  starting transfers between devices  25.1 us (2%)
  between operations  14.2 us (1%)
    reduce_scatter x1, waiting for transfers between devices, on_device(): lax.psum_scatter(grad_in, ('dp', 'blk'), scatter_dimension=0, tiled=True)  284 us
    reduce_scatter x1, waiting for transfers between devices, on_device(): lax.psum_scatter(grad_down, ('dp', 'blk'), scatter_dimension=0, tiled=True)  282 us
    reduce_scatter x1, waiting for transfers between devices, on_device(): lax.psum_scatter(grad_qkv, ('dp', 'blk'), scatter_dimension=0, tiled=True)  108 us
    ppermute x29, waiting for transfers between devices, shifted(): return lax.ppermute(block, axis, route)  90 us
    unnamed x1, blocking collectives  49 us
    ppermute x29, starting transfers between devices, shifted(): return lax.ppermute(block, axis, route)  24.4 us
    while x65, local copies, waits for them, and re-layouts  24.1 us
  transfers between devices with their start and end apart: 33, of which 19 were waited for; matrix products, arithmetic and copies ran while one was open for 12% of the time, Pallas kernels for 0%

commit v1 on v0

--- a/solution.py
+++ b/solution.py
@@ -1,6 +1,8 @@
 import jax
 import jax.numpy as jnp
 from jax import lax
+from jax.experimental import pallas as pl
+from jax.experimental.pallas import tpu as pltpu
 from jax.sharding import PartitionSpec as P
 
 H = 20
@@ -60,6 +62,182 @@
         preferred_element_type=jnp.float32,
     )
     return (grad_queries, grad_keys, grad_values)
+
+
+MESH = pl.DeviceIdType.MESH
+F32 = jnp.float32
+BF16 = jnp.bfloat16
+NN = (((1,), (0,)), ((), ()))
+NT = (((1,), (1,)), ((), ()))
+
+
+def mm(left, right, dims=NN):
+    return lax.dot_general(left, right, dims, preferred_element_type=F32)
+
+
+def remote(src, dst, send, recv, target):
+    return pltpu.make_async_remote_copy(
+        src_ref=src, dst_ref=dst, send_sem=send, recv_sem=recv, device_id=target, device_id_type=MESH
+    )
+
+
+def greet(targets):
+    barrier = pltpu.get_barrier_semaphore()
+    for target in targets:
+        pl.semaphore_signal(barrier, inc=1, device_id=target, device_id_type=MESH)
+    pl.semaphore_wait(barrier, len(targets))
+
+
+def place():
+    dp, blk = lax.axis_index("dp"), lax.axis_index("blk")
+    return dp, blk, dp // 2, lax.rem(dp, 2), blk // 2, lax.rem(blk, 2)
+
+
+def ffn_grads_kernel(
+    x_ref, g_ref, win_ref, wdown_ref, down_ref, in_ref,
+    gx, gg, wi, wd, xt, gp, ht, part_in, part_dn, sib_in, sib_dn, ysend_in, ysend_dn, yrecv_in, yrecv_dn, slab, slab_in,
+    wsem, gsend, grecv, ssend, srecv, ysend, yrecv, qsend, qrecv,
+):
+    dp, blk, z, x, y, c = place()
+    width = x_ref.shape[1]
+    tokens = x_ref.shape[0]
+    cut = wi.shape[1]
+    owned = down_ref.shape[0]
+    rows = in_ref.shape[0]
+    load_in = pltpu.make_async_copy(win_ref.at[:, pl.ds(pl.multiple_of(dp * cut, cut), cut)], wi, wsem.at[0])
+    load_dn = pltpu.make_async_copy(wdown_ref.at[pl.ds(pl.multiple_of(dp * cut, cut), cut), :], wd, wsem.at[1])
+    load_in.start()
+    load_dn.start()
+    gx[0] = x_ref[...]
+    gg[0] = g_ref[...]
+    sibling = (dp, 2 * y + (1 - c))
+    ypeer = (dp, 2 * (1 - y) + c)
+    xpeer = (2 * z + (1 - x), blk)
+    greet([(lax.rem(dp + k, 8), blk) for k in range(1, 8)] + [sibling, ypeer])
+
+    def gather(slot, target_slot, target):
+        return (
+            remote(gx.at[slot], gx.at[target_slot], gsend.at[0, target_slot], grecv.at[0, target_slot], target),
+            remote(gg.at[slot], gg.at[target_slot], gsend.at[1, target_slot], grecv.at[1, target_slot], target),
+        )
+
+    for k in range(1, 4):
+        for copy in gather(0, k, (2 * lax.rem(z + k, 4) + x, blk)):
+            copy.start()
+    for copy in gather(0, 4, xpeer):
+        copy.start()
+    load_in.wait()
+    load_dn.wait()
+
+    def make(slot):
+        xs = gx[slot]
+        place_at = pl.ds(pl.multiple_of(slot * tokens, tokens), tokens)
+        xt[:, place_at] = xs.T
+        pre = mm(xs, wi[...])
+        cdf = 0.5 * (1.0 + lax.erf(pre * 0.7071067811865476))
+        ht[:, place_at] = (pre * cdf).astype(BF16).T
+        slope = cdf + pre * (0.3989422804014327 * jnp.exp(-0.5 * pre * pre))
+        gp[place_at, :] = (mm(gg[slot], wd[...], NT) * slope).astype(BF16)
+
+    make(0)
+
+    @pl.loop(1, 4)
+    def _(slot):
+        for copy in gather(slot, slot, xpeer):
+            copy.wait_recv()
+        for copy in gather(slot, slot + 4, xpeer):
+            copy.start()
+        make(slot)
+
+    @pl.loop(4, 8)
+    def _(slot):
+        for copy in gather(slot, slot, xpeer):
+            copy.wait_recv()
+        make(slot)
+
+    @pl.loop(0, 4)
+    def _(pair):
+        made = mm(xt[pl.ds(pl.multiple_of(pair * 2 * owned, 2 * owned), 2 * owned), :], gp[...])
+        for half in range(2):
+            for q in range(4):
+                at = half * owned + q * rows
+                part_in[q, 2 * pair + half] = made[at : at + rows].astype(BF16)
+
+    to_sibling = []
+    for kind, part, landing in ((0, part_in, sib_in), (1, part_dn, sib_dn)):
+        for yy in range(2):
+            away = part.at[2 * yy + (1 - c)]
+            to_sibling.append(remote(away, landing.at[yy], ssend.at[kind, yy], srecv.at[kind, yy], sibling))
+    to_sibling[0].start()
+    to_sibling[1].start()
+    every = gg[...].reshape(8 * tokens, width)
+
+    @pl.loop(0, 4)
+    def _(q):
+        part_dn[q] = mm(ht[pl.ds(pl.multiple_of(q * owned, owned), owned), :], every).astype(BF16)
+
+    to_sibling[2].start()
+    to_sibling[3].start()
+    over = 2 * (1 - y) + c
+    mine = 2 * y + c
+    for copy in to_sibling:
+        copy.wait()
+    ysend_in[...] = (part_in[over].astype(F32) + sib_in[1 - y].astype(F32)).astype(BF16)
+    ysend_dn[...] = (part_dn[over].astype(F32) + sib_dn[1 - y].astype(F32)).astype(BF16)
+    to_y = (
+        remote(ysend_in, yrecv_in, ysend.at[0], yrecv.at[0], ypeer),
+        remote(ysend_dn, yrecv_dn, ysend.at[1], yrecv.at[1], ypeer),
+    )
+    for copy in to_y:
+        copy.start()
+    to_y[0].wait()
+    slab[...] = (part_in[mine].astype(F32) + sib_in[y].astype(F32) + yrecv_in[...].astype(F32)).astype(BF16)
+    to_q = []
+    for k in range(1, 8):
+        target = lax.rem(dp + k, 8)
+        to_q.append(remote(slab.at[target], slab_in.at[dp], qsend.at[k], qrecv.at[k], (target, blk)))
+        to_q[-1].start()
+    slab_in[dp] = slab[dp]
+    to_y[1].wait()
+    down_ref[...] = part_dn[mine].astype(F32) + sib_dn[y].astype(F32) + yrecv_dn[...].astype(F32)
+    for copy in to_q:
+        copy.wait()
+    for s in range(8):
+        in_ref[:, s * cut : (s + 1) * cut] = slab_in[s].astype(F32)
+    for k in range(1, 4):
+        for copy in gather(0, k, xpeer):
+            copy.wait_send()
+    for k in range(0, 4):
+        for copy in gather(k, 4 + k, xpeer):
+            copy.wait_send()
+
+
+def ffn_grads(normed, grad, w_in, w_down):
+    tokens, width = normed.shape
+    inner = w_in.shape[1]
+    cut, owned, rows = inner // 8, inner // 32, width // 32
+    v = pltpu.VMEM
+    dma = pltpu.SemaphoreType.DMA
+    flops = 2 * 8 * tokens * width * cut * 4
+    return pl.pallas_call(
+        ffn_grads_kernel,
+        out_shape=(jax.ShapeDtypeStruct((owned, width), F32), jax.ShapeDtypeStruct((rows, inner), F32)),
+        in_specs=[pl.BlockSpec(memory_space=v)] * 2 + [pl.BlockSpec(memory_space=pl.ANY)] * 2,
+        out_specs=(pl.BlockSpec(memory_space=v),) * 2,
+        scratch_shapes=[
+            v((8, tokens, width), BF16), v((8, tokens, width), BF16),
+            v((width, cut), BF16), v((cut, width), BF16),
+            v((width, 8 * tokens), BF16), v((8 * tokens, cut), BF16), v((cut, 8 * tokens), BF16),
+            v((4, 8, rows, cut), BF16), v((4, owned, width), BF16),
+            v((2, 8, rows, cut), BF16), v((2, owned, width), BF16),
+            v((8, rows, cut), BF16), v((owned, width), BF16),
+            v((8, rows, cut), BF16), v((owned, width), BF16),
+            v((8, rows, cut), BF16), v((8, rows, cut), BF16),
+            dma((2,)), dma((2, 8)), dma((2, 8)), dma((2, 2)), dma((2, 2)), dma((2,)), dma((2,)), dma((8,)), dma((8,)),
+        ],
+        compiler_params=pltpu.CompilerParams(collective_id=1, has_side_effects=True, vmem_limit_bytes=60 * 2**20),
+        cost_estimate=pl.CostEstimate(flops=flops, bytes_accessed=8 * 2**20, transcendentals=0),
+    )(normed, grad, w_in, w_down)
 
 
 def on_device(
@@ -127,12 +305,17 @@
     sum_share = lax.dynamic_slice_in_dim(moment_sums[0], rank * share, share)
     square_share = lax.dynamic_slice_in_dim(moment_sums[1], rank * share, share)
     grad_layer = out_grad.astype(jnp.float32)
-    grad_down = jnp.einsum("sbf,sbd->fd", hidden_low, out_grad, preferred_element_type=jnp.float32)
     grad_hidden = jnp.einsum("sbd,fd->sbf", out_grad, w_down, preferred_element_type=jnp.float32)
     grad_pre = jax.vjp(exact_gelu, hidden_pre)[1](grad_hidden)[0].astype(jnp.bfloat16)
-    grad_in = jnp.einsum(
-        "sbd,sbf->df", normed_two_low, grad_pre, preferred_element_type=jnp.float32
-    )
+    if lax.axis_size("dp") == 8 and blocks == 4 and seqs_here == 1:
+        grad_down, grad_in = ffn_grads(normed_two_low[0], out_grad[0], w_in, w_down)
+    else:
+        grad_down = jnp.einsum("sbf,sbd->fd", hidden_low, out_grad, preferred_element_type=jnp.float32)
+        grad_in = jnp.einsum(
+            "sbd,sbf->df", normed_two_low, grad_pre, preferred_element_type=jnp.float32
+        )
+        grad_in = lax.psum_scatter(grad_in, ("dp", "blk"), scatter_dimension=0, tiled=True)
+        grad_down = lax.psum_scatter(grad_down, ("dp", "blk"), scatter_dimension=0, tiled=True)
     grad_normed_two = jnp.einsum("sbf,df->sbd", grad_pre, w_in, preferred_element_type=jnp.float32)
     unused_two, pull_two = jax.vjp(layer_norm, residual, second_gain, second_shift)
     residual_part, second_gain_grad, second_shift_grad = pull_two(grad_normed_two)
@@ -190,8 +373,8 @@
     summed = (
         lax.psum_scatter(grad_qkv, ("dp", "blk"), scatter_dimension=0, tiled=True),
         lax.psum_scatter(grad_out, ("dp", "blk"), scatter_dimension=0, tiled=True),
-        lax.psum_scatter(grad_in, ("dp", "blk"), scatter_dimension=0, tiled=True),
-        lax.psum_scatter(grad_down, ("dp", "blk"), scatter_dimension=0, tiled=True),
+        grad_in,
+        grad_down,
         lax.psum_scatter(first_gain_grad, ("dp", "blk"), scatter_dimension=0, tiled=True),
         lax.psum_scatter(first_shift_grad, ("dp", "blk"), scatter_dimension=0, tiled=True),
         lax.psum_scatter(second_gain_grad, ("dp", "blk"), scatter_dimension=0, tiled=True),

time: 1070 us -> 523 us (0.49)
  waiting for transfers between devices: 764 us -> 104 us
  Pallas kernels: 0 us -> 144 us
  matrix products: 141 us -> 111 us
    reduce_scatter x2 -> x0, waiting for transfers between devices: 566 us -> none  [the longest x1 284 us: on_device(): lax.psum_scatter(grad_in, ('dp', 'blk'), scatter_dimension=0, tiled=True)]
    pallas_call x0 -> x1, Pallas kernels: none -> 144 us  [ffn_grads(): pl.pallas_call(ffn_grads_kernel, out_shape=(jax.ShapeDtypeStruct((owned,...]
    reduce_scatter x1, waiting for transfers between devices: 108 us -> 14.8 us  [on_device(): lax.psum_scatter(grad_qkv, ('dp', 'blk'), scatter_dimension=0, tiled=True)]
    dot_general x3 -> x0, matrix products: 40.7 us -> none  [the longest x1 16 us: on_device(): jnp.einsum('sbf,sbd->fd', hidden_low, out_grad, preferred_element_type=jn...]
  transfers between devices with their start and end apart: 33 -> 31, of which waited for: 19 -> 17; matrix products, arithmetic and copies ran while one was open for 12% -> 19% of each run, Pallas kernels for 0% -> 28%
where the time goes in v1:
time: 523 us; the launch traced here: 521 us
  Pallas kernels  144 us (28%)
  matrix products  111 us (21%)
  waiting for transfers between devices  104 us (20%)
  blocking collectives  49.4 us (9%)
  local copies, waits for them, and re-layouts  44.3 us (8%)
  other arithmetic  28.9 us (6%)
  starting transfers between devices  25 us (5%)
  between operations  14.4 us (3%)
    pallas_call x1, Pallas kernels, ffn_grads(): pl.pallas_call(ffn_grads_kernel, out_shape=(jax.ShapeDtypeStruct((owned,...  144 us
    ppermute x29, waiting for transfers between devices, shifted(): return lax.ppermute(block, axis, route)  89.4 us
    unnamed x1, blocking collectives  49.4 us
    ppermute x29, starting transfers between devices, shifted(): return lax.ppermute(block, axis, route)  24.9 us
    while x65, local copies, waits for them, and re-layouts  24.1 us
    dot_general x1, matrix products, on_device(): jnp.einsum('sbf,df->sbd', grad_pre, w_in, preferred_element_type=jnp.floa...  19.9 us
    reduce_scatter x1, waiting for transfers between devices, on_device(): lax.psum_scatter(grad_qkv, ('dp', 'blk'), scatter_dimension=0, tiled=True)  14.8 us
    unnamed x48, local copies, waits for them, and re-layouts  13.7 us
  transfers between devices with their start and end apart: 31, of which 17 were waited for; matrix products, arithmetic and copies ran while one was open for 19% of the time, Pallas kernels for 28%

profile of v1, /device:TPU:0, one launch (start us, length us, event | category | flops | bytes accessed | tf_op | source)
XLA Modules:
  0.0 521.4 jit_solution(15570087037355946240)
XLA Ops:
  11.3 6.8 %fusion.81 = (bf16[1,128,3840]{2,1,0:T(8,128)(2,1)S(1)}, f32[1,128,3840]{2,1,0:T(8,128)}) fusion(bf16[1280,3840]{1,0:T(8,128)(2,1)} %param.19, bf16[1,128,1280]{2,1,0:T(8,128)(2,1)} %param.16, f32[1280]{0:T(1024)} %param.18, f32[1280]{0:T(1024)} %param.17, f32[128]{0:T(128)S(1)} %fusion.60, f32[128]{0:T(128)S(1)} %broadcast_multiply_fusion.1), kind=kOutput, calls=%fused_computation.133 | convolution fusion | flops 1259765760 | bytes 13118464 | tf_op jit(solution)/shard_map/dot_general | solution.py:265
  19.0 1.9 copy.57
  20.8 1.9 copy.56
  22.7 1.7 copy.68
  24.4 1.7 copy.69
  26.1 1.9 fusion.49
  28.0 1.9 copy.59
  29.9 1.6 fusion.82
  31.5 2.1 convolution_bitcast_fusion.7
  33.6 43.2 %while.39 = (s32[]{:T(128)}, bf16[1,128,20,64]{1,3,2,0:T(8,128)(2,1)}, bf16[1,128,20,64]{1,3,2,0:T(8,128)(2,1)}, s32[1,128]{1,0:T(1,128)S(1)}, f32[1,128,20,64]{...) while((s32[]{:T(128)}, ...), condition=%wide.region_5.6_spmd, body=%wide.region_3.5_spmd.sunk | while | flops 85377024 | bytes 12873997 | solution.py:283
  34.0 2.6 collective-permute-start.2
  36.7 4.4 collective-permute-done.2
  42.7 1.7 copy.80
  44.6 1.7 copy.81
  48.4 2.4 collective-permute-start.2
  50.9 4.4 collective-permute-done.2
  56.9 1.7 copy.80
  58.8 1.7 copy.81
  62.6 2.4 collective-permute-start.2
  65.1 4.4 collective-permute-done.2
  71.1 1.7 copy.80
  72.9 1.7 copy.81
  78.0 1.8 fusion.83
  81.6 8.1 %fusion.86 = f32[128,5120]{1,0:T(8,128)} fusion(bf16[128,1280]{1,0:T(8,128)(2,1)S(1)} %fusion.57.x_ref, bf16[1280,5120]{1,0:T(8,128)(2,1)} %win_ref.1), kind=kOutput, calls=%fused_computation.136 | convolution fusion | flops 1677721600 | bytes 16056320 | tf_op jit(solution)/shard_map/dot_general | solution.py:291
  89.7 19.9 %fusion.50 = (f32[1280]{0:T(1024)S(1)}, f32[128]{0:T(128)S(1)}, f32[128,1280]{1,0:T(8,128)}) fusion(f32[1,128,1280]{2,1,0:T(8,128)} %copy-done.10, f32[128]{0:T(128)S(1)} %fusion.61, f32[128]{0:T(128)S(1)} %broadcast_multiply_fusion, f32[1280]{0:T(1024)S(1)} %copy-done.22, bf16[1280,5120]{1,0:T(8,128)(2,1)} %win_ref.1, f32[128,5120]{1,0:T(8,128)} %fusion.86, ...), kind=kOutput, calls=%fused_computation.87 | convolution fusion | flops 3403774464 | bytes 30486016 | tf_op jit(solution)/shard_map/sbf,df->sbd/dot_general | solution.py:319
  109.7 1.6 fusion.79
  114.0 3.8 fusion.88
  117.9 2.0 fusion.87
  120.1 144.6 %while.40 = (s32[]{:T(128)}, bf16[1,128,20,64]{1,3,2,0:T(8,128)(2,1)}, bf16[1,128,20,64]{1,3,2,0:T(8,128)(2,1)}, s32[1,128]{1,0:T(1,128)S(1)}, f32[1,128,20,64]{...) while((s32[]{:T(128)}, ...), condition=%wide.region_12.13_spmd.clone, body=%wide.region_11.12_spmd.clone.sunk | while | flops 213008384 | bytes 26589632 | solution.py:349
  126.6 2.4 collective-permute-start.7
  130.4 6.9 %collective-permute-done.6 = bf16[1,128,20,64]{1,3,2,0:T(8,128)(2,1)} collective-permute-done((bf16[1,128,20,64]{1,3,2,0:T(8,128)(2,1)}, bf16[1,128,20,64]{1,3,2,0:T(8,128)(2,1)}, u32[]{:S(2)}, u32[]{:S(2)}) %collective-permute-start.6) | collective-permute-done | bytes 327712 | tf_op jit(solution)/shard_map/while/body/eval_jaxpr/ppermute | solution.py:17
  137.3 1.9 convert_element_type.211
  139.2 5.2 %collective-permute-done.7 = bf16[1,128,20,64]{1,3,2,0:T(8,128)(2,1)S(1)} collective-permute-done((bf16[1,128,20,64]{1,3,2,0:T(8,128)(2,1)}, bf16[1,128,20,64]{1,3,2,0:T(8,128)(2,1)S(1)}, u32[]{:S(2)}, u32[]{:S(2)}) %collective-permute-start.7) | collective-permute-done | bytes 327712 | tf_op jit(solution)/shard_map/while/body/eval_jaxpr/ppermute | solution.py:17
  145.4 11.4 %collective-permute-done.5 = s32[1,128]{1,0:T(1,128)S(1)} collective-permute-done((s32[1,128]{1,0:T(1,128)S(1)}, s32[1,128]{1,0:T(1,128)S(1)}, u32[]{:S(2)}, u32[]{:S(2)}) %collective-permute-start.5) | collective-permute-done | bytes 544 | tf_op jit(solution)/shard_map/while/body/eval_jaxpr/ppermute | solution.py:17
  161.7 2.1 fusion.139
  163.8 2.5 collective-permute-start.6
  167.3 2.5 collective-permute-start.7
  169.9 2.5 fusion.141
  173.8 1.9 convert_element_type.211
  175.7 5.6 %collective-permute-done.7 = bf16[1,128,20,64]{1,3,2,0:T(8,128)(2,1)S(1)} collective-permute-done((bf16[1,128,20,64]{1,3,2,0:T(8,128)(2,1)}, bf16[1,128,20,64]{1,3,2,0:T(8,128)(2,1)S(1)}, u32[]{:S(2)}, u32[]{:S(2)}) %collective-permute-start.7) | collective-permute-done | bytes 327712 | tf_op jit(solution)/shard_map/while/body/eval_jaxpr/ppermute | solution.py:17
  182.2 12.5 %collective-permute-done.5 = s32[1,128]{1,0:T(1,128)S(1)} collective-permute-done((s32[1,128]{1,0:T(1,128)S(1)}, s32[1,128]{1,0:T(1,128)S(1)}, u32[]{:S(2)}, u32[]{:S(2)}) %collective-permute-start.5) | collective-permute-done | bytes 544 | tf_op jit(solution)/shard_map/while/body/eval_jaxpr/ppermute | solution.py:17
  199.7 2.1 fusion.139
  201.8 1.7 collective-permute-start.6
  204.5 2.7 collective-permute-start.7
  207.3 2.5 fusion.141
  209.7 1.9 convert_element_type.211
  211.6 5.4 %collective-permute-done.7 = bf16[1,128,20,64]{1,3,2,0:T(8,128)(2,1)S(1)} collective-permute-done((bf16[1,128,20,64]{1,3,2,0:T(8,128)(2,1)}, bf16[1,128,20,64]{1,3,2,0:T(8,128)(2,1)S(1)}, u32[]{:S(2)}, u32[]{:S(2)}) %collective-permute-start.7) | collective-permute-done | bytes 327712 | tf_op jit(solution)/shard_map/while/body/eval_jaxpr/ppermute | solution.py:17
  217.9 12.4 %collective-permute-done.5 = s32[1,128]{1,0:T(1,128)S(1)} collective-permute-done((s32[1,128]{1,0:T(1,128)S(1)}, s32[1,128]{1,0:T(1,128)S(1)}, u32[]{:S(2)}, u32[]{:S(2)}) %collective-permute-start.5) | collective-permute-done | bytes 544 | tf_op jit(solution)/shard_map/while/body/eval_jaxpr/ppermute | solution.py:17
  235.3 2.1 fusion.139
  237.5 1.8 collective-permute-start.6
  240.3 3.1 collective-permute-start.7
  243.5 2.5 fusion.141
  245.9 1.9 convert_element_type.211
  247.8 4.6 collective-permute-done.7
  253.3 10.5 %collective-permute-done.5 = s32[1,128]{1,0:T(1,128)S(1)} collective-permute-done((s32[1,128]{1,0:T(1,128)S(1)}, s32[1,128]{1,0:T(1,128)S(1)}, u32[]{:S(2)}, u32[]{:S(2)}) %collective-permute-start.5) | collective-permute-done | bytes 544 | tf_op jit(solution)/shard_map/while/body/eval_jaxpr/ppermute | solution.py:17
  268.3 8.3 %fusion.54 = f32[1280,3840]{1,0:T(8,128)} fusion(bf16[128,1280]{0,1:T(8,128)(2,1)S(1)} %bitcast.226, bf16[128,1280]{0,1:T(8,128)(2,1)S(1)} %bitcast.224, bf16[128,1280]{0,1:T(8,128)(2,1)S(1)} %bitcast.228, bf16[1,128,1280]{2,1,0:T(8,128)(2,1)S(1)} %copy-done.8, f32[1280]{0:T(1024)S(1)} %copy-done.20, f32[1280]{0:T(1024)S(1)} %copy-done.19, ...), kind=kOutput, calls=%fused_computation.99 | convolution fusion | flops 1262223360 | bytes 20982784 | tf_op jit(solution)/shard_map/sbd,sbe->de/dot_general | solution.py:364
  276.6 143.9 %shard_map.214 = (f32[160,1280]{1,0:T(8,128)}, f32[40,5120]{1,0:T(8,128)}) custom-call(bf16[128,1280]{1,0:T(8,128)(2,1)} %copy-done.16, bf16[128,1280]{1,0:T(8,128)(2,1)} %bitcast.222, bf16[1280,5120]{1,0:T(8,128)(2,1)} %win_ref.1, bf16[5120,1280]{1,0:T(8,128)(2,1)} %wdown_ref.1), custom_call_target="tpu_custom_call" | custom-call | flops 6710886400 | bytes 8388608 | tf_op jit(solution)/shard_map/pallas_call | solution.py:222
  420.6 7.2 %fusion.48 = (f32[128]{0:T(128)S(1)}, f32[128,1280]{1,0:T(8,128)S(1)}) fusion(bf16[1,128,1280]{2,1,0:T(8,128)(2,1)S(1)} %copy-done.8, f32[1280]{0:T(1024)S(1)} %copy-done.19, f32[128]{0:T(128)S(1)} %broadcast_multiply_fusion.1, bf16[1280,3840]{1,0:T(8,128)(2,1)} %param.19, bf16[128,1280]{0,1:T(8,128)(2,1)S(1)} %bitcast.227, ...), kind=kOutput, calls=%fused_computation.83 | convolution fusion | flops 1262059392 | bytes 11802624 | tf_op jit(solution)/shard_map/sbe,de->sbd/dot_general | solution.py:367
  428.5 12.1 %fusion.46 = (f32[1280]{0:T(1024)S(1)}, f32[1280]{0:T(1024)S(1)}, bf16[1,128,1280]{2,1,0:T(8,128)(2,1)}) fusion(f32[128]{0:T(128)S(1)} %convert_reduce_fusion.1, f32[1,128,1280]{2,1,0:T(8,128)S(1)} %copy-done.11, bf16[5120,1280]{1,0:T(8,128)(2,1)} %wdown_ref.1, f32[128,5120]{1,0:T(8,128)} %fusion.86), kind=kOutput, calls=%fused_computation.81 | convolution fusion | flops 1721300480 | bytes 16722432 | tf_op jit(solution)/shard_map/dot_general | solution.py:293
  440.6 49.4 %all-reduce.4 = (f32[1280]{0:T(1024)S(1)}, f32[1280]{0:T(1024)S(1)}, f32[1280]{0:T(1024)S(1)}, f32[1280]{0:T(1024)S(1)}, f32[1280]{0:T(1024)S(1)}, /*index=5*/f32[1280]{0:T(1024)S(1)}) all-reduce(f32[1280]{0:T(1024)S(1)} %get-tuple-element.180, f32[1280]{0:T(1024)S(1)} %reduce_sum.191, ...), channel_id=4, replica_groups=mesh['dp'=8,'blk'=4] {'dp','blk'}, use_global_device_ids=true, to_apply=%region_18.19.clone | all-reduce | flops 7680 | bytes 61440
  492.9 2.7 add_convert_fusion.2
  495.6 14.8 %reduce-scatter.3.cloned.1.call-done = f32[40,3840]{1,0:T(8,128)} async-done(((f32[1280,3840]{1,0:T(8,128)}), f32[40,3840]{1,0:T(8,128)}) %reduce-scatter.3.cloned.1.call-update) | async-done | bytes 614416 | tf_op jit(solution)/shard_map/reduce_scatter | solution.py:374
  510.4 2.1 copy.108
  512.5 2.1 copy.109
  (208 shorter events, 61.7 us)
Async XLA Ops:
  7.2 70.8 %copy-start = (bf16[1280,1280]{1,0:T(8,128)(2,1)S(1)}, bf16[1280,1280]{1,0:T(8,128)(2,1)}, u32[]{:S(2)}) copy-start(bf16[1280,1280]{1,0:T(8,128)(2,1)} %param.20) | copy-start | bytes 9830404
  7.2 488.4 %reduce-scatter.5.cloned.1.call-start = ((), (), s32[]{:S(2)}) async-start(), calls=%async_computation.3 | async-start | bytes 6758400 | tf_op jit(solution)/shard_map/reduce_scatter | solution.py:375
  26.1 7.4 %copy-start.21 = (s32[1,128]{1,0:T(1,128)S(1)}, s32[1,128]{1,0:T(1,128)}, u32[]{:S(2)}) copy-start(s32[1,128]{1,0:T(1,128)} %param.25) | copy-start | bytes 1540
  33.6 7.6 %collective-permute-start = (bf16[1,128,20,64]{1,3,2,0:T(8,128)(2,1)}, bf16[1,128,20,64]{1,3,2,0:T(8,128)(2,1)}, u32[]{:S(2)}, u32[]{:S(2)}) collective-permute-start(bf16[1,128,20,64]{1,3,2,0:T(8,128)(2,1)} %get-tuple-element.383), channel_id=1, source_target_pairs={{3,0},{0,1},{1,2},{2,3},{7,4},{4,5},{5,6},{6,7},{11,8},{8,9},{9,10... | collective-permute-start | bytes 983048 | tf_op jit(solution)/shard_map/while/body/eval_jaxpr/ppermute | solution.py:17
  34.0 7.0 %collective-permute-start.2 = (s32[1,128]{1,0:T(1,128)S(1)}, s32[1,128]{1,0:T(1,128)S(1)}, u32[]{:S(2)}, u32[]{:S(2)}) collective-permute-start(s32[1,128]{1,0:T(1,128)S(1)} %get-tuple-element.385), channel_id=1, source_target_pairs={{3,0},{0,1},{1,2},{2,3},{7,4},{4,5},{5,6},{6,7},{11,8},{8,9},{9,10... | collective-permute-start | bytes 1544 | tf_op jit(solution)/shard_map/while/body/eval_jaxpr/ppermute | solution.py:17
  36.7 7.9 %collective-permute-start.1 = (bf16[1,128,20,64]{1,3,2,0:T(8,128)(2,1)}, bf16[1,128,20,64]{1,3,2,0:T(8,128)(2,1)}, u32[]{:S(2)}, u32[]{:S(2)}) collective-permute-start(bf16[1,128,20,64]{1,3,2,0:T(8,128)(2,1)} %get-tuple-element.384), channel_id=1, source_target_pairs={{3,0},{0,1},{1,2},{2,3},{7,4},{4,5},{5,6},{6,7},{11,8},{8,9},{9,10... | collective-permute-start | bytes 983048 | tf_op jit(solution)/shard_map/while/body/eval_jaxpr/ppermute | solution.py:17
  36.7 9.6 %copy-start.2 = (f32[1,128,20,64]{1,3,2,0:T(8,128)S(1)}, f32[1,128,20,64]{1,3,2,0:T(8,128)}, u32[]{:S(2)}) copy-start(f32[1,128,20,64]{1,3,2,0:T(8,128)} %get-tuple-element.386) | copy-start | bytes 1966084 | tf_op jit(solution)/shard_map/while
  47.6 0.8 copy-start.3
  48.4 6.9 %collective-permute-start = (bf16[1,128,20,64]{1,3,2,0:T(8,128)(2,1)}, bf16[1,128,20,64]{1,3,2,0:T(8,128)(2,1)}, u32[]{:S(2)}, u32[]{:S(2)}) collective-permute-start(bf16[1,128,20,64]{1,3,2,0:T(8,128)(2,1)} %get-tuple-element.383), channel_id=1, source_target_pairs={{3,0},{0,1},{1,2},{2,3},{7,4},{4,5},{5,6},{6,7},{11,8},{8,9},{9,10... | collective-permute-start | bytes 983048 | tf_op jit(solution)/shard_map/while/body/eval_jaxpr/ppermute | solution.py:17
  48.4 6.8 %collective-permute-start.2 = (s32[1,128]{1,0:T(1,128)S(1)}, s32[1,128]{1,0:T(1,128)S(1)}, u32[]{:S(2)}, u32[]{:S(2)}) collective-permute-start(s32[1,128]{1,0:T(1,128)S(1)} %get-tuple-element.385), channel_id=1, source_target_pairs={{3,0},{0,1},{1,2},{2,3},{7,4},{4,5},{5,6},{6,7},{11,8},{8,9},{9,10... | collective-permute-start | bytes 1544 | tf_op jit(solution)/shard_map/while/body/eval_jaxpr/ppermute | solution.py:17
  50.8 7.9 %collective-permute-start.1 = (bf16[1,128,20,64]{1,3,2,0:T(8,128)(2,1)}, bf16[1,128,20,64]{1,3,2,0:T(8,128)(2,1)}, u32[]{:S(2)}, u32[]{:S(2)}) collective-permute-start(bf16[1,128,20,64]{1,3,2,0:T(8,128)(2,1)} %get-tuple-element.384), channel_id=1, source_target_pairs={{3,0},{0,1},{1,2},{2,3},{7,4},{4,5},{5,6},{6,7},{11,8},{8,9},{9,10... | collective-permute-start | bytes 983048 | tf_op jit(solution)/shard_map/while/body/eval_jaxpr/ppermute | solution.py:17
  50.9 9.6 %copy-start.2 = (f32[1,128,20,64]{1,3,2,0:T(8,128)S(1)}, f32[1,128,20,64]{1,3,2,0:T(8,128)}, u32[]{:S(2)}) copy-start(f32[1,128,20,64]{1,3,2,0:T(8,128)} %get-tuple-element.386) | copy-start | bytes 1966084 | tf_op jit(solution)/shard_map/while
  61.8 0.8 copy-start.3
  62.6 6.9 %collective-permute-start = (bf16[1,128,20,64]{1,3,2,0:T(8,128)(2,1)}, bf16[1,128,20,64]{1,3,2,0:T(8,128)(2,1)}, u32[]{:S(2)}, u32[]{:S(2)}) collective-permute-start(bf16[1,128,20,64]{1,3,2,0:T(8,128)(2,1)} %get-tuple-element.383), channel_id=1, source_target_pairs={{3,0},{0,1},{1,2},{2,3},{7,4},{4,5},{5,6},{6,7},{11,8},{8,9},{9,10... | collective-permute-start | bytes 983048 | tf_op jit(solution)/shard_map/while/body/eval_jaxpr/ppermute | solution.py:17
  62.6 6.8 %collective-permute-start.2 = (s32[1,128]{1,0:T(1,128)S(1)}, s32[1,128]{1,0:T(1,128)S(1)}, u32[]{:S(2)}, u32[]{:S(2)}) collective-permute-start(s32[1,128]{1,0:T(1,128)S(1)} %get-tuple-element.385), channel_id=1, source_target_pairs={{3,0},{0,1},{1,2},{2,3},{7,4},{4,5},{5,6},{6,7},{11,8},{8,9},{9,10... | collective-permute-start | bytes 1544 | tf_op jit(solution)/shard_map/while/body/eval_jaxpr/ppermute | solution.py:17
  65.0 7.9 %collective-permute-start.1 = (bf16[1,128,20,64]{1,3,2,0:T(8,128)(2,1)}, bf16[1,128,20,64]{1,3,2,0:T(8,128)(2,1)}, u32[]{:S(2)}, u32[]{:S(2)}) collective-permute-start(bf16[1,128,20,64]{1,3,2,0:T(8,128)(2,1)} %get-tuple-element.384), channel_id=1, source_target_pairs={{3,0},{0,1},{1,2},{2,3},{7,4},{4,5},{5,6},{6,7},{11,8},{8,9},{9,10... | collective-permute-start | bytes 983048 | tf_op jit(solution)/shard_map/while/body/eval_jaxpr/ppermute | solution.py:17
  65.1 9.6 %copy-start.2 = (f32[1,128,20,64]{1,3,2,0:T(8,128)S(1)}, f32[1,128,20,64]{1,3,2,0:T(8,128)}, u32[]{:S(2)}) copy-start(f32[1,128,20,64]{1,3,2,0:T(8,128)} %get-tuple-element.386) | copy-start | bytes 1966084 | tf_op jit(solution)/shard_map/while
  75.9 0.8 copy-start.3
  78.0 2.1 copy-start.14
  78.0 2.7 copy-start.22
  78.0 2.7 copy-start.23
  79.8 0.8 copy-start.10
  109.6 4.3 copy-start.15
  111.3 0.9 copy-start.13
  117.8 392.6 %reduce-scatter.3.cloned.1.call-start = ((), (), s32[]{:S(2)}) async-start(), calls=%async_computation.2 | async-start | bytes 20275200 | tf_op jit(solution)/shard_map/reduce_scatter | solution.py:374
  117.9 2.1 copy-start.4
  121.3 3.1 copy-start.5
  123.8 1.7 copy-start.6
  125.5 11.8 %collective-permute-start.6 = (bf16[1,128,20,64]{1,3,2,0:T(8,128)(2,1)}, bf16[1,128,20,64]{1,3,2,0:T(8,128)(2,1)}, u32[]{:S(2)}, u32[]{:S(2)}) collective-permute-start(bf16[1,128,20,64]{1,3,2,0:T(8,128)(2,1)} %fusion.139), channel_id=1, source_target_pairs={{3,0},{0,1},{1,2},{2,3},{7,4},{4,5},{5,6},{6,7},{11,8},{8,9},{9,10... | collective-permute-start | bytes 983048 | tf_op jit(solution)/shard_map/while/body/eval_jaxpr/ppermute | solution.py:17
  126.6 17.9 %collective-permute-start.7 = (bf16[1,128,20,64]{1,3,2,0:T(8,128)(2,1)}, bf16[1,128,20,64]{1,3,2,0:T(8,128)(2,1)S(1)}, u32[]{:S(2)}, u32[]{:S(2)}) collective-permute-start(bf16[1,128,20,64]{1,3,2,0:T(8,128)(2,1)} %fusion.140), channel_id=1, source_target_pairs={{3,0},{0,1},{1,2},{2,3},{7,4},{4,5},{5,6},{6,7},{11,8},{8,9},{9,10... | collective-permute-start | bytes 983048 | tf_op jit(solution)/shard_map/while/body/eval_jaxpr/ppermute | solution.py:17
  129.0 27.8 %collective-permute-start.4 = (bf16[1,128,20,64]{1,3,2,0:T(8,128)(2,1)S(1)}, bf16[1,128,20,64]{1,3,2,0:T(8,128)(2,1)S(1)}, u32[]{:S(2)}, u32[]{:S(2)}) collective-permute-start(bf16[1,128,20,64]{1,3,2,0:T(8,128)(2,1)S(1)} %copy.94), channel_id=1, source_target_pairs={{3,0},{0,1},{1,2},{2,3},{7,4},{4,5},{5,6},{6,7},{11,8},{8,9},{9,10... | collective-permute-start | bytes 983048 | tf_op jit(solution)/shard_map/while/body/eval_jaxpr/ppermute | solution.py:17
  129.0 27.8 %collective-permute-start.3 = (bf16[1,128,20,64]{1,3,2,0:T(8,128)(2,1)S(1)}, bf16[1,128,20,64]{1,3,2,0:T(8,128)(2,1)S(1)}, u32[]{:S(2)}, u32[]{:S(2)}) collective-permute-start(bf16[1,128,20,64]{1,3,2,0:T(8,128)(2,1)S(1)} %copy.93), channel_id=1, source_target_pairs={{3,0},{0,1},{1,2},{2,3},{7,4},{4,5},{5,6},{6,7},{11,8},{8,9},{9,10... | collective-permute-start | bytes 983048 | tf_op jit(solution)/shard_map/while/body/eval_jaxpr/ppermute | solution.py:17
  129.0 27.7 %collective-permute-start.5 = (s32[1,128]{1,0:T(1,128)S(1)}, s32[1,128]{1,0:T(1,128)S(1)}, u32[]{:S(2)}, u32[]{:S(2)}) collective-permute-start(s32[1,128]{1,0:T(1,128)S(1)} %copy.95), channel_id=1, source_target_pairs={{3,0},{0,1},{1,2},{2,3},{7,4},{4,5},{5,6},{6,7},{11,8},{8,9},{9,10... | collective-permute-start | bytes 1544 | tf_op jit(solution)/shard_map/while/body/eval_jaxpr/ppermute | solution.py:17
  156.7 0.8 copy-start.9
  158.5 3.1 copy-start.5
  161.0 5.3 %copy-start.6 = (f32[1,128,20,64]{1,3,2,0:T(8,128)S(1)}, f32[1,128,20,64]{1,3,2,0:T(8,128)}, u32[]{:S(2)}) copy-start(f32[1,128,20,64]{1,3,2,0:T(8,128)} %get-tuple-element.418) | copy-start | bytes 1966084 | tf_op jit(solution)/shard_map/while
  163.8 9.9 %collective-permute-start.6 = (bf16[1,128,20,64]{1,3,2,0:T(8,128)(2,1)}, bf16[1,128,20,64]{1,3,2,0:T(8,128)(2,1)}, u32[]{:S(2)}, u32[]{:S(2)}) collective-permute-start(bf16[1,128,20,64]{1,3,2,0:T(8,128)(2,1)} %fusion.139), channel_id=1, source_target_pairs={{3,0},{0,1},{1,2},{2,3},{7,4},{4,5},{5,6},{6,7},{11,8},{8,9},{9,10... | collective-permute-start | bytes 983048 | tf_op jit(solution)/shard_map/while/body/eval_jaxpr/ppermute | solution.py:17
  167.3 13.9 %collective-permute-start.7 = (bf16[1,128,20,64]{1,3,2,0:T(8,128)(2,1)}, bf16[1,128,20,64]{1,3,2,0:T(8,128)(2,1)S(1)}, u32[]{:S(2)}, u32[]{:S(2)}) collective-permute-start(bf16[1,128,20,64]{1,3,2,0:T(8,128)(2,1)} %fusion.140), channel_id=1, source_target_pairs={{3,0},{0,1},{1,2},{2,3},{7,4},{4,5},{5,6},{6,7},{11,8},{8,9},{9,10... | collective-permute-start | bytes 983048 | tf_op jit(solution)/shard_map/while/body/eval_jaxpr/ppermute | solution.py:17
  169.8 24.9 %collective-permute-start.4 = (bf16[1,128,20,64]{1,3,2,0:T(8,128)(2,1)S(1)}, bf16[1,128,20,64]{1,3,2,0:T(8,128)(2,1)S(1)}, u32[]{:S(2)}, u32[]{:S(2)}) collective-permute-start(bf16[1,128,20,64]{1,3,2,0:T(8,128)(2,1)S(1)} %copy.94), channel_id=1, source_target_pairs={{3,0},{0,1},{1,2},{2,3},{7,4},{4,5},{5,6},{6,7},{11,8},{8,9},{9,10... | collective-permute-start | bytes 983048 | tf_op jit(solution)/shard_map/while/body/eval_jaxpr/ppermute | solution.py:17
  169.8 24.9 %collective-permute-start.3 = (bf16[1,128,20,64]{1,3,2,0:T(8,128)(2,1)S(1)}, bf16[1,128,20,64]{1,3,2,0:T(8,128)(2,1)S(1)}, u32[]{:S(2)}, u32[]{:S(2)}) collective-permute-start(bf16[1,128,20,64]{1,3,2,0:T(8,128)(2,1)S(1)} %copy.93), channel_id=1, source_target_pairs={{3,0},{0,1},{1,2},{2,3},{7,4},{4,5},{5,6},{6,7},{11,8},{8,9},{9,10... | collective-permute-start | bytes 983048 | tf_op jit(solution)/shard_map/while/body/eval_jaxpr/ppermute | solution.py:17
  169.9 24.8 %collective-permute-start.5 = (s32[1,128]{1,0:T(1,128)S(1)}, s32[1,128]{1,0:T(1,128)S(1)}, u32[]{:S(2)}, u32[]{:S(2)}) collective-permute-start(s32[1,128]{1,0:T(1,128)S(1)} %copy.95), channel_id=1, source_target_pairs={{3,0},{0,1},{1,2},{2,3},{7,4},{4,5},{5,6},{6,7},{11,8},{8,9},{9,10... | collective-permute-start | bytes 1544 | tf_op jit(solution)/shard_map/while/body/eval_jaxpr/ppermute | solution.py:17
  194.7 0.8 copy-start.9
  196.5 3.1 copy-start.5
  199.1 4.5 copy-start.6
  201.8 7.9 %collective-permute-start.6 = (bf16[1,128,20,64]{1,3,2,0:T(8,128)(2,1)}, bf16[1,128,20,64]{1,3,2,0:T(8,128)(2,1)}, u32[]{:S(2)}, u32[]{:S(2)}) collective-permute-start(bf16[1,128,20,64]{1,3,2,0:T(8,128)(2,1)} %fusion.139), channel_id=1, source_target_pairs={{3,0},{0,1},{1,2},{2,3},{7,4},{4,5},{5,6},{6,7},{11,8},{8,9},{9,10... | collective-permute-start | bytes 983048 | tf_op jit(solution)/shard_map/while/body/eval_jaxpr/ppermute | solution.py:17
  204.5 12.4 %collective-permute-start.7 = (bf16[1,128,20,64]{1,3,2,0:T(8,128)(2,1)}, bf16[1,128,20,64]{1,3,2,0:T(8,128)(2,1)S(1)}, u32[]{:S(2)}, u32[]{:S(2)}) collective-permute-start(bf16[1,128,20,64]{1,3,2,0:T(8,128)(2,1)} %fusion.140), channel_id=1, source_target_pairs={{3,0},{0,1},{1,2},{2,3},{7,4},{4,5},{5,6},{6,7},{11,8},{8,9},{9,10... | collective-permute-start | bytes 983048 | tf_op jit(solution)/shard_map/while/body/eval_jaxpr/ppermute | solution.py:17
  207.2 23.2 %collective-permute-start.4 = (bf16[1,128,20,64]{1,3,2,0:T(8,128)(2,1)S(1)}, bf16[1,128,20,64]{1,3,2,0:T(8,128)(2,1)S(1)}, u32[]{:S(2)}, u32[]{:S(2)}) collective-permute-start(bf16[1,128,20,64]{1,3,2,0:T(8,128)(2,1)S(1)} %copy.94), channel_id=1, source_target_pairs={{3,0},{0,1},{1,2},{2,3},{7,4},{4,5},{5,6},{6,7},{11,8},{8,9},{9,10... | collective-permute-start | bytes 983048 | tf_op jit(solution)/shard_map/while/body/eval_jaxpr/ppermute | solution.py:17
  207.2 23.2 %collective-permute-start.3 = (bf16[1,128,20,64]{1,3,2,0:T(8,128)(2,1)S(1)}, bf16[1,128,20,64]{1,3,2,0:T(8,128)(2,1)S(1)}, u32[]{:S(2)}, u32[]{:S(2)}) collective-permute-start(bf16[1,128,20,64]{1,3,2,0:T(8,128)(2,1)S(1)} %copy.93), channel_id=1, source_target_pairs={{3,0},{0,1},{1,2},{2,3},{7,4},{4,5},{5,6},{6,7},{11,8},{8,9},{9,10... | collective-permute-start | bytes 983048 | tf_op jit(solution)/shard_map/while/body/eval_jaxpr/ppermute | solution.py:17
  207.2 23.1 %collective-permute-start.5 = (s32[1,128]{1,0:T(1,128)S(1)}, s32[1,128]{1,0:T(1,128)S(1)}, u32[]{:S(2)}, u32[]{:S(2)}) collective-permute-start(s32[1,128]{1,0:T(1,128)S(1)} %copy.95), channel_id=1, source_target_pairs={{3,0},{0,1},{1,2},{2,3},{7,4},{4,5},{5,6},{6,7},{11,8},{8,9},{9,10... | collective-permute-start | bytes 1544 | tf_op jit(solution)/shard_map/while/body/eval_jaxpr/ppermute | solution.py:17
  232.2 3.1 copy-start.5
  234.7 4.5 copy-start.6
  237.5 8.5 %collective-permute-start.6 = (bf16[1,128,20,64]{1,3,2,0:T(8,128)(2,1)}, bf16[1,128,20,64]{1,3,2,0:T(8,128)(2,1)}, u32[]{:S(2)}, u32[]{:S(2)}) collective-permute-start(bf16[1,128,20,64]{1,3,2,0:T(8,128)(2,1)} %fusion.139), channel_id=1, source_target_pairs={{3,0},{0,1},{1,2},{2,3},{7,4},{4,5},{5,6},{6,7},{11,8},{8,9},{9,10... | collective-permute-start | bytes 983048 | tf_op jit(solution)/shard_map/while/body/eval_jaxpr/ppermute | solution.py:17
  240.3 12.2 %collective-permute-start.7 = (bf16[1,128,20,64]{1,3,2,0:T(8,128)(2,1)}, bf16[1,128,20,64]{1,3,2,0:T(8,128)(2,1)S(1)}, u32[]{:S(2)}, u32[]{:S(2)}) collective-permute-start(bf16[1,128,20,64]{1,3,2,0:T(8,128)(2,1)} %fusion.140), channel_id=1, source_target_pairs={{3,0},{0,1},{1,2},{2,3},{7,4},{4,5},{5,6},{6,7},{11,8},{8,9},{9,10... | collective-permute-start | bytes 983048 | tf_op jit(solution)/shard_map/while/body/eval_jaxpr/ppermute | solution.py:17
  243.4 20.5 %collective-permute-start.4 = (bf16[1,128,20,64]{1,3,2,0:T(8,128)(2,1)S(1)}, bf16[1,128,20,64]{1,3,2,0:T(8,128)(2,1)S(1)}, u32[]{:S(2)}, u32[]{:S(2)}) collective-permute-start(bf16[1,128,20,64]{1,3,2,0:T(8,128)(2,1)S(1)} %copy.94), channel_id=1, source_target_pairs={{3,0},{0,1},{1,2},{2,3},{7,4},{4,5},{5,6},{6,7},{11,8},{8,9},{9,10... | collective-permute-start | bytes 983048 | tf_op jit(solution)/shard_map/while/body/eval_jaxpr/ppermute | solution.py:17
  243.4 20.5 %collective-permute-start.3 = (bf16[1,128,20,64]{1,3,2,0:T(8,128)(2,1)S(1)}, bf16[1,128,20,64]{1,3,2,0:T(8,128)(2,1)S(1)}, u32[]{:S(2)}, u32[]{:S(2)}) collective-permute-start(bf16[1,128,20,64]{1,3,2,0:T(8,128)(2,1)S(1)} %copy.93), channel_id=1, source_target_pairs={{3,0},{0,1},{1,2},{2,3},{7,4},{4,5},{5,6},{6,7},{11,8},{8,9},{9,10... | collective-permute-start | bytes 983048 | tf_op jit(solution)/shard_map/while/body/eval_jaxpr/ppermute | solution.py:17
  243.4 20.4 %collective-permute-start.5 = (s32[1,128]{1,0:T(1,128)S(1)}, s32[1,128]{1,0:T(1,128)S(1)}, u32[]{:S(2)}, u32[]{:S(2)}) collective-permute-start(s32[1,128]{1,0:T(1,128)S(1)} %copy.95), channel_id=1, source_target_pairs={{3,0},{0,1},{1,2},{2,3},{7,4},{4,5},{5,6},{6,7},{11,8},{8,9},{9,10... | collective-permute-start | bytes 1544 | tf_op jit(solution)/shard_map/while/body/eval_jaxpr/ppermute | solution.py:17
  264.7 3.5 copy-start.8
  264.7 3.5 copy-start.19
  264.7 3.5 copy-start.20
  276.6 143.9 %copy-start.18 = (f32[128,1280]{1,0:T(8,128)S(1)}, f32[128,1280]{1,0:T(8,128)}, u32[]{:S(2)}) copy-start(f32[128,1280]{1,0:T(8,128)} %get-tuple-element.246) | copy-start | bytes 1966084
  420.6 7.4 %copy-start.24 = (s32[1,4]{1,0:T(1,128)S(1)}, s32[1,4]{1,0:T(1,128)}, u32[]{:S(2)}) copy-start(s32[1,4]{1,0:T(1,128)} %param.26) | copy-start | bytes 52
  420.6 7.8 %copy-start.11 = (f32[1,128,1280]{2,1,0:T(8,128)S(1)}, f32[1,128,1280]{2,1,0:T(8,128)}, u32[]{:S(2)}) copy-start(f32[1,128,1280]{2,1,0:T(8,128)} %copy-done.10) | copy-start | bytes 1966084
  427.9 12.7 %copy-start.12 = (f32[128,1280]{1,0:T(8,128)}, f32[128,1280]{1,0:T(8,128)S(1)}, u32[]{:S(2)}) copy-start(f32[128,1280]{1,0:T(8,128)S(1)} %get-tuple-element.248) | copy-start | bytes 1966084
  492.9 21.6 %copy-start.1 = (bf16[1280,1280]{1,0:T(8,128)(2,1)S(1)}, bf16[1280,1280]{1,0:T(8,128)(2,1)}, u32[]{:S(2)}) copy-start(bf16[1280,1280]{1,0:T(8,128)(2,1)} %param.20) | copy-start | bytes 9830404
  (8 other events, 6.0 us)
Sparse Core Ops, SparseCore 0:
  117.9 148.1 reduce-scatter.4
  276.7 233.5 reduce-scatter.2

commit v2 on v0

--- a/solution.py
+++ b/solution.py
@@ -1,6 +1,8 @@
 import jax
 import jax.numpy as jnp
 from jax import lax
+from jax.experimental import pallas as pl
+from jax.experimental.pallas import tpu as pltpu
 from jax.sharding import PartitionSpec as P
 
 H = 20
@@ -62,7 +64,7 @@
     return (grad_queries, grad_keys, grad_values)
 
 
-def on_device(
+def on_device_general(
     tokens,
     first_gain,
     first_shift,
@@ -215,6 +217,626 @@
     )
 
 
+MESH = pl.DeviceIdType.MESH
+F32 = jnp.float32
+BF16 = jnp.bfloat16
+NN = (((1,), (0,)), ((), ()))
+NT = (((1,), (1,)), ((), ()))
+
+
+def mm(left, right, dims=NN):
+    return lax.dot_general(left, right, dims, preferred_element_type=F32)
+
+
+def remote(src, dst, send, recv, target):
+    return pltpu.make_async_remote_copy(
+        src_ref=src, dst_ref=dst, send_sem=send, recv_sem=recv, device_id=target, device_id_type=MESH
+    )
+
+
+def greet(targets):
+    barrier = pltpu.get_barrier_semaphore()
+    for target in targets:
+        pl.semaphore_signal(barrier, inc=1, device_id=target, device_id_type=MESH)
+    pl.semaphore_wait(barrier, len(targets))
+
+
+def place():
+    dp, blk = lax.axis_index("dp"), lax.axis_index("blk")
+    return dp, blk, dp // 2, lax.rem(dp, 2), blk // 2, lax.rem(blk, 2)
+
+
+def ffn_grads_kernel(
+    x_ref, g_ref, win_ref, wdown_ref, down_ref, in_ref,
+    gx, gg, wi, wd, xt, gp, ht, part_in, part_dn, sib_in, sib_dn, ysend_in, ysend_dn, yrecv_in, yrecv_dn, slab, slab_in,
+    wsem, gsend, grecv, ssend, srecv, ysend, yrecv, qsend, qrecv,
+):
+    dp, blk, z, x, y, c = place()
+    width = x_ref.shape[1]
+    tokens = x_ref.shape[0]
+    cut = wi.shape[1]
+    owned = down_ref.shape[0]
+    rows = in_ref.shape[0]
+    load_in = pltpu.make_async_copy(win_ref.at[:, pl.ds(pl.multiple_of(dp * cut, cut), cut)], wi, wsem.at[0])
+    load_dn = pltpu.make_async_copy(wdown_ref.at[pl.ds(pl.multiple_of(dp * cut, cut), cut), :], wd, wsem.at[1])
+    load_in.start()
+    load_dn.start()
+    gx[0] = x_ref[...]
+    gg[0] = g_ref[...]
+    sibling = (dp, 2 * y + (1 - c))
+    ypeer = (dp, 2 * (1 - y) + c)
+    xpeer = (2 * z + (1 - x), blk)
+    greet([(lax.rem(dp + k, 8), blk) for k in range(1, 8)] + [sibling, ypeer])
+
+    def gather(slot, target_slot, target):
+        return (
+            remote(gx.at[slot], gx.at[target_slot], gsend.at[0, target_slot], grecv.at[0, target_slot], target),
+            remote(gg.at[slot], gg.at[target_slot], gsend.at[1, target_slot], grecv.at[1, target_slot], target),
+        )
+
+    for k in range(1, 4):
+        for copy in gather(0, k, (2 * lax.rem(z + k, 4) + x, blk)):
+            copy.start()
+    for copy in gather(0, 4, xpeer):
+        copy.start()
+    load_in.wait()
+    load_dn.wait()
+
+    def make(slot):
+        xs = gx[slot]
+        place_at = pl.ds(pl.multiple_of(slot * tokens, tokens), tokens)
+        xt[:, place_at] = xs.T
+        pre = mm(xs, wi[...])
+        cdf = 0.5 * (1.0 + lax.erf(pre * 0.7071067811865476))
+        ht[:, place_at] = (pre * cdf).astype(BF16).T
+        slope = cdf + pre * (0.3989422804014327 * jnp.exp(-0.5 * pre * pre))
+        gp[place_at, :] = (mm(gg[slot], wd[...], NT) * slope).astype(BF16)
+
+    make(0)
+
+    @pl.loop(1, 4)
+    def _(slot):
+        for copy in gather(slot, slot, xpeer):
+            copy.wait_recv()
+        for copy in gather(slot, slot + 4, xpeer):
+            copy.start()
+        make(slot)
+
+    @pl.loop(4, 8)
+    def _(slot):
+        for copy in gather(slot, slot, xpeer):
+            copy.wait_recv()
+        make(slot)
+
+    @pl.loop(0, 4)
+    def _(pair):
+        made = mm(xt[pl.ds(pl.multiple_of(pair * 2 * owned, 2 * owned), 2 * owned), :], gp[...])
+        for half in range(2):
+            for q in range(4):
+                at = half * owned + q * rows
+                part_in[q, 2 * pair + half] = made[at : at + rows].astype(BF16)
+
+    to_sibling = []
+    for kind, part, landing in ((0, part_in, sib_in), (1, part_dn, sib_dn)):
+        for yy in range(2):
+            away = part.at[2 * yy + (1 - c)]
+            to_sibling.append(remote(away, landing.at[yy], ssend.at[kind, yy], srecv.at[kind, yy], sibling))
+    to_sibling[0].start()
+    to_sibling[1].start()
+    every = gg[...].reshape(8 * tokens, width)
+
+    @pl.loop(0, 4)
+    def _(q):
+        part_dn[q] = mm(ht[pl.ds(pl.multiple_of(q * owned, owned), owned), :], every).astype(BF16)
+
+    to_sibling[2].start()
+    to_sibling[3].start()
+    over = 2 * (1 - y) + c
+    mine = 2 * y + c
+    for copy in to_sibling:
+        copy.wait()
+    ysend_in[...] = (part_in[over].astype(F32) + sib_in[1 - y].astype(F32)).astype(BF16)
+    ysend_dn[...] = (part_dn[over].astype(F32) + sib_dn[1 - y].astype(F32)).astype(BF16)
+    to_y = (
+        remote(ysend_in, yrecv_in, ysend.at[0], yrecv.at[0], ypeer),
+        remote(ysend_dn, yrecv_dn, ysend.at[1], yrecv.at[1], ypeer),
+    )
+    for copy in to_y:
+        copy.start()
+    to_y[0].wait()
+    slab[...] = (part_in[mine].astype(F32) + sib_in[y].astype(F32) + yrecv_in[...].astype(F32)).astype(BF16)
+    to_q = []
+    for k in range(1, 8):
+        target = lax.rem(dp + k, 8)
+        to_q.append(remote(slab.at[target], slab_in.at[dp], qsend.at[k], qrecv.at[k], (target, blk)))
+        to_q[-1].start()
+    slab_in[dp] = slab[dp]
+    to_y[1].wait()
+    down_ref[...] = part_dn[mine].astype(F32) + sib_dn[y].astype(F32) + yrecv_dn[...].astype(F32)
+    for copy in to_q:
+        copy.wait()
+    for s in range(8):
+        in_ref[:, s * cut : (s + 1) * cut] = slab_in[s].astype(F32)
+    for k in range(1, 4):
+        for copy in gather(0, k, xpeer):
+            copy.wait_send()
+    for k in range(0, 4):
+        for copy in gather(k, 4 + k, xpeer):
+            copy.wait_send()
+
+
+def ffn_grads(normed, grad, w_in, w_down):
+    tokens, width = normed.shape
+    inner = w_in.shape[1]
+    cut, owned, rows = inner // 8, inner // 32, width // 32
+    v = pltpu.VMEM
+    dma = pltpu.SemaphoreType.DMA
+    flops = 2 * 8 * tokens * width * cut * 4
+    return pl.pallas_call(
+        ffn_grads_kernel,
+        out_shape=(jax.ShapeDtypeStruct((owned, width), F32), jax.ShapeDtypeStruct((rows, inner), F32)),
+        in_specs=[pl.BlockSpec(memory_space=v)] * 2 + [pl.BlockSpec(memory_space=pl.ANY)] * 2,
+        out_specs=(pl.BlockSpec(memory_space=v),) * 2,
+        scratch_shapes=[
+            v((8, tokens, width), BF16), v((8, tokens, width), BF16),
+            v((width, cut), BF16), v((cut, width), BF16),
+            v((width, 8 * tokens), BF16), v((8 * tokens, cut), BF16), v((cut, 8 * tokens), BF16),
+            v((4, 8, rows, cut), BF16), v((4, owned, width), BF16),
+            v((2, 8, rows, cut), BF16), v((2, owned, width), BF16),
+            v((8, rows, cut), BF16), v((owned, width), BF16),
+            v((8, rows, cut), BF16), v((owned, width), BF16),
+            v((8, rows, cut), BF16), v((8, rows, cut), BF16),
+            dma((2,)), dma((2, 8)), dma((2, 8)), dma((2, 2)), dma((2, 2)), dma((2,)), dma((2,)), dma((8,)), dma((8,)),
+        ],
+        compiler_params=pltpu.CompilerParams(collective_id=1, has_side_effects=True, vmem_limit_bytes=60 * 2**20),
+        cost_estimate=pl.CostEstimate(flops=flops, bytes_accessed=8 * 2**20, transcendentals=0),
+    )(normed, grad, w_in, w_down)
+
+
+TN = (((0,), (0,)), ((), ()))
+
+
+def neighbours(dp, y, c):
+    return (dp, 2 * y + (1 - c)), (dp, 2 * (1 - y) + c), (dp, 2 * (1 - y) + (1 - c))
+
+
+def row_gather(kind, mine, rows, y, c, sibling, ypeer, send, recv):
+    at = rows.at[y, pl.ds(pl.multiple_of(c * mine, mine), mine), :]
+    over = rows.at[1 - y, pl.ds(pl.multiple_of(c * mine, mine), mine), :]
+    return (
+        remote(at, at, send.at[kind, 0], recv.at[kind, 0], sibling),
+        remote(at, at, send.at[kind, 1], recv.at[kind, 1], ypeer),
+        remote(over, over, send.at[kind, 2], recv.at[kind, 2], sibling),
+    )
+
+
+def norm_rows(values, gain, shift):
+    center = values - jnp.mean(values, axis=-1, keepdims=True)
+    spread = jnp.mean(center * center, axis=-1, keepdims=True)
+    return center * lax.rsqrt(spread + EPSILON) * gain + shift
+
+
+def half_of(pair, head):
+    lanes = lax.broadcasted_iota(jnp.int32, pair.shape, 1) // 64
+    return jnp.where(lanes == head, pair, jnp.zeros_like(pair))
+
+
+def attend_kernel(
+    tok_ref, gain_ref, shift_ref, segq_ref, segk_ref, wqkv_ref, row_ref, qkv_ref, att_ref, own_ref,
+    rows, wbuf, low, landing, wsem, gsend, grecv, asend, arecv,
+):
+    dp, blk, z, x, y, c = place()
+    tokens, width = tok_ref.shape
+    row_len = 4 * tokens
+    first = 5 * y + 3 * c
+    pairs = 3 - c
+
+    def load(j, t):
+        source = wqkv_ref.at[:, pl.ds(pl.multiple_of(t * width + (first + j) * 128, 128), 128)]
+        return pltpu.make_async_copy(source, wbuf.at[j, :, pl.ds(t * 128, 128)], wsem.at[j, t])
+
+    @pl.loop(0, pairs)
+    def _(j):
+        for t in range(3):
+            load(j, t).start()
+
+    rows[y, pl.ds(pl.multiple_of(c * tokens, tokens), tokens), :] = tok_ref[...]
+    sibling, ypeer, diag = neighbours(dp, y, c)
+    greet([sibling, ypeer, diag])
+    moves = row_gather(0, tokens, rows, y, c, sibling, ypeer, gsend, grecv)
+    moves[0].start()
+    moves[1].start()
+
+    @pl.loop(0, pairs)
+    def _(j):
+        for t in range(3):
+            load(j, t).wait()
+
+    def project(chip):
+        at = pl.ds(pl.multiple_of(chip * 2 * tokens, 2 * tokens), 2 * tokens)
+        row_ref[at, :] = norm_rows(rows[chip].astype(F32), gain_ref[...], shift_ref[...]).astype(BF16)
+
+        @pl.loop(0, pairs)
+        def _(j):
+            made = mm(row_ref[at, :], wbuf[j])
+            qkv_ref[j, at, 0:128] = (made[:, 0:128] * 0.125).astype(BF16)
+            qkv_ref[j, at, 128:384] = made[:, 128:384].astype(BF16)
+
+    @pl.loop(0, 2)
+    def _(step):
+        @pl.when(step == 0)
+        def _():
+            moves[0].wait_recv()
+
+        @pl.when(step == 1)
+        def _():
+            moves[1].wait_recv()
+            moves[2].start()
+            moves[2].wait_recv()
+
+        project(y + step - 2 * y * step)
+
+    @pl.when(c == 1)
+    def _():
+        low[2] = jnp.zeros_like(low[2])
+        qkv_ref[2] = jnp.zeros_like(qkv_ref[2])
+        att_ref[2] = jnp.zeros_like(att_ref[2])
+
+    @pl.loop(0, pairs)
+    def _(j):
+        @pl.loop(0, 2)
+        def _(part):
+            at = pl.ds(pl.multiple_of(part * 2 * tokens, 2 * tokens), 2 * tokens)
+            same = segq_ref[at, :] == segk_ref[...]
+            pair = jnp.zeros((2 * tokens, 128), F32)
+            for head in range(2):
+                scores = mm(half_of(qkv_ref[j, at, 0:128], head), qkv_ref[j, :, 128:256], NT)
+                weigh = jnp.where(same, jnp.exp(scores), 0.0)
+                total = jnp.sum(weigh, axis=-1, keepdims=True)
+                pair = pair + half_of(mm(weigh.astype(BF16), qkv_ref[j, :, 256:384]) / total, head)
+            att_ref[j, at, :] = pair
+            low[j, at, :] = pair.astype(BF16)
+
+    def rows_of(b):
+        return pl.ds(pl.multiple_of(b * tokens, tokens), tokens)
+
+    out = []
+    for r, target in ((1, sibling), (2, ypeer), (3, diag)):
+        out.append(remote(low.at[:, rows_of(target[1]), :], landing.at[r], asend.at[r], arecv.at[r], target))
+        out[-1].start()
+    landing[0] = low[:, rows_of(blk), :]
+    for copy in out:
+        copy.wait()
+    spread_pairs(landing, own_ref, y, c, 1)
+    for move in moves:
+        move.wait_send()
+
+
+def spread_pairs(landing, out, y, c, kinds):
+    for yy in range(2):
+        for cc in range(2):
+            slot = 2 * (y + yy - 2 * y * yy) + (c + cc - 2 * c * cc)
+            for j in range(3 - cc):
+                p = 5 * yy + 3 * cc + j
+                for t in range(kinds):
+                    at = t * (out.shape[1] // kinds) + 128 * p
+                    out[:, at : at + 128] = landing[slot, j, :, 128 * t : 128 * t + 128].astype(out.dtype)
+
+
+def attend(tokens, gain, shift, segq, segk, w_qkv):
+    count, width = tokens.shape
+    row_len = 4 * count
+    v = pltpu.VMEM
+    dma = pltpu.SemaphoreType.DMA
+    return pl.pallas_call(
+        attend_kernel,
+        out_shape=(
+            jax.ShapeDtypeStruct((row_len, width), BF16),
+            jax.ShapeDtypeStruct((3, row_len, 384), BF16),
+            jax.ShapeDtypeStruct((3, row_len, 128), F32),
+            jax.ShapeDtypeStruct((count, width), BF16),
+        ),
+        in_specs=[pl.BlockSpec(memory_space=v)] * 5 + [pl.BlockSpec(memory_space=pl.ANY)],
+        out_specs=(pl.BlockSpec(memory_space=v),) * 4,
+        scratch_shapes=[
+            v((2, 2 * count, width), BF16), v((3, width, 384), BF16),
+            v((3, row_len, 128), BF16), v((4, 3, count, 128), BF16),
+            dma((3, 3)), dma((1, 3)), dma((1, 3)), dma((4,)), dma((4,)),
+        ],
+        compiler_params=pltpu.CompilerParams(collective_id=2, has_side_effects=True, vmem_limit_bytes=48 * 2**20),
+        cost_estimate=pl.CostEstimate(flops=2 * row_len * width * 1152, bytes_accessed=8 * 2**20, transcendentals=0),
+    )(tokens, gain, shift, segq, segk, w_qkv)
+
+
+def attend_back_kernel(
+    proj_ref, mine_ref, row_ref, qkv_ref, att_ref, segq_ref, segk_ref, wout_ref, gqkv_ref, gout_ref, low_ref,
+    grow, arow, wo, turned, aturned, gatt, low, keys, values, part, xin, zout, zin, full, fin, landing,
+    wsem, gsend, grecv, xsend, xrecv, zsend, zrecv, fsend, frecv, asend, arecv,
+):
+    dp, blk, z, x, y, c = place()
+    tokens, width = proj_ref.shape
+    row_len = 4 * tokens
+    first = 5 * y + 3 * c
+    pairs = 3 - c
+    share = width // 8
+    cut = share // 4
+
+    @pl.loop(0, pairs)
+    def _(j):
+        source = wout_ref.at[pl.ds(pl.multiple_of((first + j) * 128, 128), 128), :]
+        pltpu.make_async_copy(source, wo.at[j], wsem.at[j]).start()
+
+    own_rows = pl.ds(pl.multiple_of(c * tokens, tokens), tokens)
+    grow[y, own_rows, :] = proj_ref[...]
+    arow[y, own_rows, :] = mine_ref[...]
+    sibling, ypeer, diag = neighbours(dp, y, c)
+    xpeer = (2 * z + (1 - x), blk)
+    zpeers = [(2 * lax.rem(z + k, 4) + x, blk) for k in range(1, 4)]
+    greet([sibling, ypeer, diag, xpeer] + zpeers)
+    moves = row_gather(0, tokens, grow, y, c, sibling, ypeer, gsend, grecv)
+    amoves = row_gather(1, tokens, arow, y, c, sibling, ypeer, gsend, grecv)
+    for copy in (moves[0], moves[1], amoves[0], amoves[1]):
+        copy.start()
+    for b in range(4):
+        turned[:, b * tokens : (b + 1) * tokens] = row_ref[b * tokens : (b + 1) * tokens, :].T
+    moves[1].wait_recv()
+    moves[2].start()
+
+    @pl.loop(0, pairs)
+    def _(j):
+        source = wout_ref.at[pl.ds(pl.multiple_of((first + j) * 128, 128), 128), :]
+        pltpu.make_async_copy(source, wo.at[j], wsem.at[j]).wait()
+
+    moves[0].wait_recv()
+    moves[2].wait_recv()
+    every = grow[...].reshape(row_len, width)
+
+    @pl.loop(0, pairs)
+    def _(j):
+        gatt[j] = mm(grow[...].reshape(row_len, width), wo[j], NT)
+
+    amoves[1].wait_recv()
+    amoves[2].start()
+    amoves[0].wait_recv()
+    amoves[2].wait_recv()
+    for b in range(4):
+        aturned[:, b * tokens : (b + 1) * tokens] = arow[b // 2, (b % 2) * tokens : (b % 2 + 1) * tokens, :].T
+
+    def to_x(s):
+        return remote(part.at[s, 1 - x], xin.at[s], xsend.at[s], xrecv.at[s], xpeer)
+
+    def to_z(s, k):
+        target = lax.rem(z + k, 4)
+        return remote(zout.at[s, target], zin.at[s, k - 1], zsend.at[s, k - 1], zrecv.at[s, k - 1], zpeers[k - 1])
+
+    def to_blk(s, r, target):
+        return remote(full.at[s, target[1]], fin.at[r, s], fsend.at[r, s], frecv.at[r, s], target)
+
+    def to_low(j, r, target):
+        there = pl.ds(pl.multiple_of(target[1] * tokens, tokens), tokens)
+        return remote(low.at[j, there, :], landing.at[r, j], asend.at[r, j], arecv.at[r, j], target)
+
+    others = ((1, sibling), (2, ypeer), (3, diag))
+
+    def add_x(s):
+        to_x(s).wait()
+        for k in range(4):
+            zout[s, k] = (part[s, x, k].astype(F32) + xin[s, k].astype(F32)).astype(BF16)
+        for k in range(1, 4):
+            to_z(s, k).start()
+
+    def add_z(s):
+        for k in range(1, 4):
+            to_z(s, k).wait()
+        total = zout[s, z].astype(F32)
+        for k in range(3):
+            total = total + zin[s, k].astype(F32)
+        for b in range(4):
+            full[s, b] = total[b * cut : (b + 1) * cut]
+        for r, target in others:
+            to_blk(s, r, target).start()
+        fin[0, s] = full[s, blk]
+
+    def weight_part(s, left, right):
+        @pl.loop(0, 4)
+        def _(zz):
+            at = pl.ds(pl.multiple_of(zz * 2 * share, 2 * share), 2 * share)
+            made = mm(left[at, :], right)
+            part[s, 0, zz] = made[:share].astype(BF16)
+            part[s, 1, zz] = made[share:].astype(BF16)
+
+    @pl.when(c == 0)
+    def _():
+        weight_part(0, aturned, grow[:, :, pl.ds(pl.multiple_of(first * 128, 128), 384)].reshape(row_len, 384))
+
+    @pl.when(c == 1)
+    def _():
+        right = grow[:, :, pl.ds(pl.multiple_of(first * 128, 128), 256)].reshape(row_len, 256)
+        weight_part(0, aturned, jnp.concatenate([right, jnp.zeros((row_len, 128), BF16)], axis=1))
+
+    to_x(0).start()
+
+    @pl.loop(0, pairs)
+    def _(j):
+        keys[...] = jnp.zeros_like(keys)
+        values[...] = jnp.zeros_like(values)
+
+        @pl.loop(0, 2)
+        def _(half):
+            at = pl.ds(pl.multiple_of(half * 2 * tokens, 2 * tokens), 2 * tokens)
+            same = segq_ref[at, :] == segk_ref[...]
+            queries_grad = jnp.zeros((2 * tokens, 128), F32)
+            for head in range(2):
+                query = half_of(qkv_ref[j, at, 0:128], head)
+                key = half_of(qkv_ref[j, :, 128:256], head)
+                grad = half_of(gatt[j, at, :], head)
+                weigh = jnp.where(same, jnp.exp(mm(query, key, NT)), 0.0)
+                total = jnp.sum(weigh, axis=-1, keepdims=True)
+                scaled = (grad / total).astype(BF16)
+                delta = jnp.sum(grad * att_ref[j, at, :], axis=-1, keepdims=True) / total
+                spread = mm(scaled, qkv_ref[j, :, 256:384], NT)
+                score = (weigh * (spread - delta)).astype(BF16)
+                queries_grad = queries_grad + mm(score, key)
+                keys[...] += mm(score, query, TN)
+                values[...] += mm(weigh.astype(BF16), scaled, TN)
+            low[j, at, 0:128] = (queries_grad * 0.125).astype(BF16)
+
+        low[j, :, 128:256] = keys[...].astype(BF16)
+        low[j, :, 256:384] = values[...].astype(BF16)
+        for r, target in others:
+            to_low(j, r, target).start()
+        weight_part(j + 1, turned, low[j])
+        to_x(j + 1).start()
+        add_x(j)
+
+        @pl.when(j > 0)
+        def _():
+            add_z(j - 1)
+
+    add_x(pairs)
+    add_z(pairs - 1)
+    add_z(pairs)
+
+    @pl.loop(0, pairs)
+    def _(j):
+        landing[0, j] = low[j, pl.ds(pl.multiple_of(blk * tokens, tokens), tokens), :]
+        for r, target in others:
+            to_low(j, r, target).wait_send()
+
+    @pl.loop(0, pairs + 1)
+    def _(s):
+        for r, target in others:
+            to_blk(s, r, target).wait_send()
+
+    for r, target, count in ((1, sibling, 2 + c), (2, ypeer, 3 - c), (3, diag, 2 + c)):
+        @pl.loop(0, count)
+        def _(j):
+            to_low(j, r, target).wait_recv()
+
+        @pl.loop(0, count + 1)
+        def _(s):
+            to_blk(s, r, target).wait_recv()
+
+    spread_pairs(landing, low_ref, y, c, 3)
+    for yy in range(2):
+        for cc in range(2):
+            slot = 2 * (y + yy - 2 * y * yy) + (c + cc - 2 * c * cc)
+            p = 5 * yy + 3 * cc
+            wide = 128 * (3 - cc)
+            gout_ref[:, 128 * p : 128 * p + wide] = fin[slot, 0, :, :wide]
+            for j in range(3 - cc):
+                for t in range(3):
+                    at = t * width + 128 * (p + j)
+                    gqkv_ref[:, at : at + 128] = fin[slot, j + 1, :, 128 * t : 128 * t + 128]
+    for move in moves + amoves:
+        move.wait_send()
+
+
+def attend_back(proj, mine, rows, qkv, att, segq, segk, w_out):
+    count, width = proj.shape
+    row_len, share = 4 * count, width // 8
+    v = pltpu.VMEM
+    dma = pltpu.SemaphoreType.DMA
+    return pl.pallas_call(
+        attend_back_kernel,
+        out_shape=(
+            jax.ShapeDtypeStruct((share // 4, 3 * width), F32),
+            jax.ShapeDtypeStruct((share // 4, width), F32),
+            jax.ShapeDtypeStruct((count, 3 * width), BF16),
+        ),
+        in_specs=[pl.BlockSpec(memory_space=v)] * 7 + [pl.BlockSpec(memory_space=pl.ANY)],
+        out_specs=(pl.BlockSpec(memory_space=v),) * 3,
+        scratch_shapes=[
+            v((2, 2 * count, width), BF16), v((2, 2 * count, width), BF16), v((3, 128, width), BF16),
+            v((width, row_len), BF16), v((width, row_len), BF16), v((3, row_len, 128), F32),
+            v((3, row_len, 384), BF16), v((row_len, 128), F32), v((row_len, 128), F32),
+            v((4, 2, 4, share, 384), BF16), v((4, 4, share, 384), BF16), v((4, 4, share, 384), BF16),
+            v((4, 3, share, 384), BF16), v((4, 4, share // 4, 384), F32), v((4, 4, share // 4, 384), F32),
+            v((4, 3, count, 384), BF16),
+            dma((3,)), dma((2, 3)), dma((2, 3)), dma((4,)), dma((4,)), dma((4, 3)), dma((4, 3)),
+            dma((4, 4)), dma((4, 4)), dma((4, 3)), dma((4, 3)),
+        ],
+        compiler_params=pltpu.CompilerParams(collective_id=3, has_side_effects=True, vmem_limit_bytes=60 * 2**20),
+        cost_estimate=pl.CostEstimate(flops=20 * 2**30, bytes_accessed=16 * 2**20, transcendentals=0),
+    )(proj, mine, rows, qkv, att, segq, segk, w_out)
+
+
+def on_device(
+    tokens,
+    first_gain,
+    first_shift,
+    w_qkv,
+    w_out,
+    second_gain,
+    second_shift,
+    w_in,
+    w_down,
+    segment_ids,
+    cls_positions,
+    out_grad,
+):
+    tokens, out_grad = tokens[0], out_grad[0]
+    block_len, width = tokens.shape
+    blocks = lax.axis_size("blk")
+    row_len = block_len * blocks
+    tokens_wide = tokens.astype(F32)
+    places = lax.broadcasted_iota(jnp.int32, (row_len, cls_positions.shape[1]), 0)
+    row_cells = jnp.sum((places >= cls_positions).astype(jnp.int32), axis=1)
+    segq, segk = row_cells[:, None], row_cells[None, :]
+    rows, qkv, att, attended_low = attend(
+        tokens, first_gain[None], first_shift[None], segq, segk, w_qkv
+    )
+    residual = tokens_wide + jnp.dot(attended_low, w_out, preferred_element_type=F32)
+    normed_two_low = layer_norm(residual, second_gain, second_shift).astype(BF16)
+    hidden_pre = jnp.dot(normed_two_low, w_in, preferred_element_type=F32)
+    hidden_low = exact_gelu(hidden_pre).astype(BF16)
+    layer = residual + jnp.dot(hidden_low, w_down, preferred_element_type=F32)
+    offset = lax.axis_index("blk") * block_len
+    spots = lax.broadcasted_iota(jnp.int32, (cls_positions.shape[1], block_len), 1) + offset
+    chosen = jnp.sum((spots == cls_positions[0][:, None]).astype(F32), axis=0)
+    cell_sums = jnp.sum(chosen[:, None] * layer, axis=0)
+    cell_squares = jnp.sum(chosen[:, None] * layer * layer, axis=0)
+    count = cls_positions.shape[0] * cls_positions.shape[1] * lax.axis_size("dp")
+    grad_hidden = mm(out_grad, w_down, NT)
+    grad_pre = jax.vjp(exact_gelu, hidden_pre)[1](grad_hidden)[0].astype(BF16)
+    grad_down, grad_in = ffn_grads(normed_two_low, out_grad, w_in, w_down)
+    grad_normed_two = mm(grad_pre, w_in, NT)
+    unused_two, pull_two = jax.vjp(layer_norm, residual, second_gain, second_shift)
+    residual_part, second_gain_grad, second_shift_grad = pull_two(grad_normed_two)
+    grad_residual = out_grad.astype(F32) + residual_part
+    grad_proj = grad_residual.astype(BF16)
+    grad_qkv, grad_out, grad_qkv_low = attend_back(
+        grad_proj, attended_low, rows, qkv, att, segq, segk, w_out
+    )
+    grad_normed_one = mm(grad_qkv_low, w_qkv, NT)
+    unused_one, pull_one = jax.vjp(layer_norm, tokens_wide, first_gain, first_shift)
+    tokens_part, first_gain_grad, first_shift_grad = pull_one(grad_normed_one)
+    tokens_grad = (grad_residual + tokens_part).astype(BF16)
+    sums = lax.psum(
+        jnp.stack([first_gain_grad, first_shift_grad, second_gain_grad, second_shift_grad, cell_sums, cell_squares]),
+        ("dp", "blk"),
+    )
+    share = width // (lax.axis_size("dp") * blocks)
+    rank = lax.axis_index("dp") * blocks + lax.axis_index("blk")
+    mine = lax.dynamic_slice_in_dim(sums, rank * share, share, axis=1)
+    cls_mean = mine[4] / count
+    cls_variance = mine[5] / count - cls_mean * cls_mean
+    return (
+        layer.astype(BF16)[None],
+        tokens_grad[None],
+        grad_qkv,
+        grad_out,
+        grad_in,
+        grad_down,
+        mine[0],
+        mine[1],
+        mine[2],
+        mine[3],
+        cls_mean,
+        cls_variance,
+    )
+
+
 def solution(mesh):
     placed = (
         P("dp", "blk", None),
@@ -230,8 +852,9 @@
         P("dp", None),
         P("dp", "blk", None),
     )
+    small = mesh.shape["dp"] == 8 and mesh.shape["blk"] == 4
     return jax.shard_map(
-        on_device,
+        on_device if small else on_device_general,
         mesh=mesh,
         in_specs=placed,
         out_specs=(

time: 1070 us -> 324 us (0.30)
  waiting for transfers between devices: 764 us -> 0 us
  Pallas kernels: 0 us -> 224 us
  matrix products: 141 us -> 41.6 us
  local copies, waits for them, and re-layouts: 45 us -> 9.14 us
  starting transfers between devices: 25.1 us -> 0 us
  other arithmetic: 26 us -> 5.2 us
  between operations: 14.2 us -> 0.99 us
    reduce_scatter x4 -> x0, waiting for transfers between devices: 674 us -> none  [the longest x1 284 us: on_device(): lax.psum_scatter(grad_in, ('dp', 'blk'), scatter_dimension=0, tiled=True)]
    pallas_call x0 -> x3, Pallas kernels: none -> 224 us  [the longest x1 120 us: ffn_grads(): pl.pallas_call(ffn_grads_kernel, out_shape=(jax.ShapeDtypeStruct((owned,...]
    dot_general x40 -> x5, matrix products: 141 us -> 41.6 us  [the longest x2 26.1 us: mm(): return lax.dot_general(left, right, dims, preferred_element_type=F32)]
    ppermute x29 -> x0, waiting for transfers between devices: 90 us -> none  [shifted(): return lax.ppermute(block, axis, route)]
    unnamed x1 -> x0, blocking collectives: 49 us -> none
    psum x0 -> x1, blocking collectives: none -> 43 us  [on_device(): lax.psum(jnp.stack([first_gain_grad, first_shift_grad, second_gain_grad,...]
    ppermute x29 -> x0, starting transfers between devices: 24.4 us -> none  [shifted(): return lax.ppermute(block, axis, route)]
    while x65 -> x0, local copies, waits for them, and re-layouts: 24.1 us -> none
  transfers between devices with their start and end apart: 33 -> 0, of which waited for: 19 -> 0; matrix products, arithmetic and copies ran while one was open for 12% -> 0% of each run, Pallas kernels for 0% -> 0%
where the time goes in v2:
time: 324 us
  Pallas kernels  224 us (69%)
  blocking collectives  43 us (13%)
  matrix products  41.6 us (13%)
  local copies, waits for them, and re-layouts  9.14 us (3%)
  other arithmetic  5.2 us (2%)
    pallas_call x1, Pallas kernels, ffn_grads(): pl.pallas_call(ffn_grads_kernel, out_shape=(jax.ShapeDtypeStruct((owned,...  120 us
    pallas_call x1, Pallas kernels, attend_back(): pl.pallas_call(attend_back_kernel, out_shape=(jax.ShapeDtypeStruct((share...  81.4 us
    psum x1, blocking collectives, on_device(): lax.psum(jnp.stack([first_gain_grad, first_shift_grad, second_gain_grad,...  43 us
    dot_general x2, matrix products, mm(): return lax.dot_general(left, right, dims, preferred_element_type=F32)  26.1 us
    pallas_call x1, Pallas kernels, attend(): pl.pallas_call(attend_kernel, out_shape=(jax.ShapeDtypeStruct((row_len, w...  23.1 us
    dot_general x1, matrix products, on_device(): layer = residual + jnp.dot(hidden_low, w_down, preferred_element_type=F32)  7.98 us
    unnamed x48, local copies, waits for them, and re-layouts  6.9 us
    dot_general x1, matrix products, on_device(): hidden_pre = jnp.dot(normed_two_low, w_in, preferred_element_type=F32)  6.74 us

profile of v2, /device:TPU:0, one launch (start us, length us, event | category | flops | bytes accessed | tf_op | source)
XLA Modules:
  0.0 324.1 jit_solution(7011683271296645289)
XLA Ops:
  0.7 0.7 convert_reduce_fusion.2
  1.4 0.7 broadcast_in_dim.20.gain_ref
  2.1 0.7 broadcast_in_dim.21.shift_ref
  2.8 0.7 convert_reduce_fusion.1
  3.5 0.0 copy-start.4
  3.5 0.1 copy.25.segq_ref
  3.7 0.0 copy-start.2
  3.7 0.0 copy-start
  3.7 1.1 copy-done
  4.8 23.1 %shard_map.202 = (bf16[512,1280]{1,0:T(8,128)(2,1)S(1)}, bf16[3,512,384]{2,1,0:T(8,128)(2,1)S(1)}, f32[3,512,128]{2,1,0:T(8,128)S(1)}, bf16[128,1280]{1,0:T(8,128)(2,1)S(1)}) custom-call(bf16[128,1280]{1,0:T(8,128)(2,1)S(1)} %bitcast.51, f32[1,1280]{1,0:T(1,128)S(1)} %broadcast_in_dim.20.gain_ref, f32[1,1280]{1,0:T(1,128)S(1)} %broadcast_in_dim.21.shift_ref, ...), custom_call_target="tpu_custom_call" | custom-call | flops 1509949440 | bytes 8388608 | tf_op jit(solution)/shard_map/pallas_call | solution.py:531
  27.9 0.0 copy-done.4
  27.9 0.0 copy-done.2
  27.9 0.0 copy-start.3
  27.9 0.0 copy-start.5
  27.9 0.0 copy-start.6
  27.9 0.0 copy-start.7
  28.0 0.0 copy-done.9
  28.0 0.0 copy-start.16
  28.0 0.0 copy-start.17
  28.0 0.7 fusion.39
  28.7 0.2 multiply_reduce_fusion.3
  28.9 0.0 copy-done.3
  28.9 0.2 copy-done.5
  29.1 0.4 copy-done.6
  29.5 0.2 copy-done.7
  29.7 0.0 copy-done.16
  29.7 0.0 copy-done.17
  29.7 0.2 add_convert_fusion.3.x_ref
  29.9 0.0 copy-start.8
  29.9 0.0 slice-start.2
  29.9 0.0 slice-start.3
  30.0 6.7 %fusion.42 = f32[128,5120]{1,0:T(8,128)S(1)} fusion(bf16[128,1280]{1,0:T(8,128)(2,1)S(1)} %add_convert_fusion.3.x_ref, bf16[1280,5120]{1,0:T(8,128)(2,1)} %win_ref.1), kind=kOutput, calls=%fused_computation.79 | convolution fusion | flops 1677721600 | bytes 16056320 | tf_op jit(solution)/shard_map/dot_general | solution.py:791
  36.7 0.0 copy-done.8
  36.7 0.0 slice-done
  36.7 0.0 slice-done.1
  36.7 0.0 slice-done.2
  36.7 0.5 slice-done.3
  37.2 8.0 %fusion.15 = (f32[1280]{0:T(1024)S(1)}, f32[1280]{0:T(1024)S(1)}, bf16[1,128,1280]{2,1,0:T(8,128)(2,1)}) fusion(f32[128]{0:T(128)S(1)} %convert_reduce_fusion.2, f32[128,1280]{1,0:T(8,128)S(1)} %get-tuple-element.52, bf16[5120,1280]{1,0:T(8,128)(2,1)S(1)} %bitcast.56, f32[128,5120]{1,0:T(8,128)S(1)} %fusion.42), kind=kOutput, calls=%fused_computation.34 | convolution fusion | flops 1721300480 | bytes 16722432 | tf_op jit(solution)/shard_map/dot_general | solution.py:793
  45.2 0.0 copy-done.11
  45.2 0.0 copy-done.10
  45.2 18.7 %multiply_reduce_fusion.1 = (f32[1280]{0:T(1024)S(1)}, f32[128]{0:T(128)S(1)}, f32[1280]{0:T(1024)S(1)}, f32[128,1280]{1,0:T(8,128)S(1)}) fusion(f32[128,1280]{1,0:T(8,128)S(1)} %get-tuple-element.52, f32[128]{0:T(128)S(1)} %fusion.22, f32[128]{0:T(128)S(1)} %broadcast_multiply_fusion.1, f32[1280]{0:T(1024)S(1)} %copy-done.16, ...), kind=kOutput, calls=%fused_computation.39 | convolution fusion | flops 3403937024 | bytes 30491136 | tf_op jit(solution)/shard_map/dot_general | solution.py:228
  63.9 0.3 fusion.38
  64.2 0.0 copy-done.1
  64.2 0.1 convert_reduce_fusion
  64.3 0.9 fusion.20.proj_ref
  65.2 81.4 %shard_map.203 = (f32[40,3840]{1,0:T(8,128)}, f32[40,1280]{1,0:T(8,128)}, bf16[128,3840]{1,0:T(8,128)(2,1)}) custom-call(bf16[128,1280]{1,0:T(8,128)(2,1)} %fusion.20.proj_ref, bf16[128,1280]{1,0:T(8,128)(2,1)} %copy-done.3, bf16[512,1280]{1,0:T(8,128)(2,1)} %copy-done.5, bf16[3,512,384]{2,1,0:T(8,128)(2,1)} %copy-done.6, f32[3,512,128]{2,1,0:T(8,128)} %copy-done.7, ...), custom_call_target="tpu_custom_call" | custom-call | flops 21474836480 | bytes 16777216 | tf_op jit(solution)/shard_map/pallas_call | solution.py:740
  146.6 0.0 copy-done.15
  146.6 7.5 %fusion.37 = (f32[1280]{0:T(1024)S(1)}, f32[128]{0:T(128)S(1)}, f32[128]{0:T(128)S(1)}, f32[128,1280]{1,0:T(8,128)S(1)}) fusion(f32[1280]{0:T(1024)S(1)} %copy-done.15, f32[128]{0:T(128)S(1)} %get-tuple-element.56, bf16[1,128,1280]{2,1,0:T(8,128)(2,1)S(1)} %copy-done.1, bf16[128,3840]{1,0:T(8,128)(2,1)} %get-tuple-element.25, bf16[1280,3840]{1,0:T(8,128)(2,1)} %wqkv_ref.1), kind=kOutput, calls=%fused_computation.76 | convolution fusion | flops 1259600384 | bytes 11808256 | tf_op jit(solution)/shard_map/dot_general | solution.py:228
  154.1 0.4 fusion.19
  154.5 1.1 fusion.21
  155.6 119.8 %shard_map.204 = (f32[160,1280]{1,0:T(8,128)}, f32[40,5120]{1,0:T(8,128)}) custom-call(bf16[128,1280]{1,0:T(8,128)(2,1)} %copy-done.8, bf16[128,1280]{1,0:T(8,128)(2,1)} %bitcast.57, bf16[1280,5120]{1,0:T(8,128)(2,1)} %win_ref.1, bf16[5120,1280]{1,0:T(8,128)(2,1)} %wdown_ref.1), custom_call_target="tpu_custom_call" | custom-call | flops 6710886400 | bytes 8388608 | tf_op jit(solution)/shard_map/pallas_call | solution.py:375
  275.3 0.0 copy-start.12
  275.4 0.1 stack.15
  275.5 43.0 %psum.7 = f32[6,1280]{1,0:T(8,128)S(1)} all-reduce(f32[6,1280]{1,0:T(8,128)S(1)} %stack.15), channel_id=1, replica_groups=mesh['dp'=8,'blk'=4] {'dp','blk'}, use_global_device_ids=true, to_apply=%region_16.0 | all-reduce | flops 7680 | bytes 61440 | tf_op jit(solution)/shard_map/psum | solution.py:815
  318.5 0.1 constant_dynamic-slice_fusion
  318.5 0.5 slice_bitcast_fusion
  319.1 0.5 bitcast_subtract_fusion
  319.6 0.0 copy-done.13
  319.6 0.8 copy.31
  320.4 0.0 copy-done.14
  320.4 0.7 copy.32
  321.1 2.1 copy.33
  323.2 0.0 copy-done.12
  323.2 0.9 copy.34
  (23 shorter events, 0.1 us)
Async XLA Ops:
  3.5 24.4 %copy-start.4 = (s32[512]{0:T(512)}, s32[512]{0:T(512)S(1)}, u32[]{:S(2)}) copy-start(s32[512]{0:T(512)S(1)} %convert_reduce_fusion.1) | copy-start | bytes 6148
  3.7 24.2 %copy-start.2 = (s32[512,1]{1,0:T(8,128)}, s32[512,1]{1,0:T(8,128)S(1)}, u32[]{:S(2)}) copy-start(s32[512,1]{1,0:T(8,128)S(1)} %copy.25.segq_ref) | copy-start | bytes 6148
  3.7 1.1 copy-start
  4.8 23.2 %copy-start.9 = (bf16[1280,1280]{1,0:T(8,128)(2,1)S(1)}, bf16[1280,1280]{1,0:T(8,128)(2,1)}, u32[]{:S(2)}) copy-start(bf16[1280,1280]{1,0:T(8,128)(2,1)} %wout_ref.1) | copy-start | bytes 9830404
  4.8 31.9 %slice-start = ((s8[13107200]{0:T(1024)(128)(4,1)}), s8[4194304]{0:T(1024)(128)(4,1)S(1)}, s32[]{:S(2)}) async-start(s8[13107200]{0:T(1024)(128)(4,1)} %bitcast.55), calls=%async_computation | async-start | bytes 8388608
  4.8 31.9 %slice-start.1 = ((s8[13107200]{0:T(1024)(128)(4,1)}), s8[524288]{0:T(1024)(128)(4,1)S(1)}, s32[]{:S(2)}) async-start(s8[13107200]{0:T(1024)(128)(4,1)} %bitcast.55), calls=%async_computation.1 | async-start | bytes 1048576
  27.9 1.0 copy-start.3
  27.9 1.2 copy-start.5
  27.9 1.6 copy-start.6
  27.9 1.8 copy-start.7
  28.0 1.8 copy-start.16
  28.0 1.8 copy-start.17
  29.9 6.8 %copy-start.8 = (bf16[128,1280]{1,0:T(8,128)(2,1)}, bf16[128,1280]{1,0:T(8,128)(2,1)S(1)}, u32[]{:S(2)}) copy-start(bf16[128,1280]{1,0:T(8,128)(2,1)S(1)} %add_convert_fusion.3.x_ref) | copy-start | bytes 983044
  29.9 6.8 %slice-start.2 = ((s8[13107200]{0:T(1024)(128)(4,1)}), s8[4194304]{0:T(1024)(128)(4,1)S(1)}, s32[]{:S(2)}) async-start(s8[13107200]{0:T(1024)(128)(4,1)} %bitcast.55), calls=%async_computation.2 | async-start | bytes 8388608
  29.9 7.3 %slice-start.3 = ((s8[13107200]{0:T(1024)(128)(4,1)}), s8[4194304]{0:T(1024)(128)(4,1)S(1)}, s32[]{:S(2)}) async-start(s8[13107200]{0:T(1024)(128)(4,1)} %bitcast.55), calls=%async_computation.3 | async-start | bytes 8388608
  37.2 8.0 %copy-start.11 = (f32[128,5120]{1,0:T(8,128)}, f32[128,5120]{1,0:T(8,128)S(1)}, u32[]{:S(2)}) copy-start(f32[128,5120]{1,0:T(8,128)S(1)} %fusion.42) | copy-start | bytes 7864324
  37.2 8.0 %copy-start.10 = (bf16[1,128,1280]{2,1,0:T(8,128)(2,1)S(1)}, bf16[1,128,1280]{2,1,0:T(8,128)(2,1)}, u32[]{:S(2)}) copy-start(bf16[1,128,1280]{2,1,0:T(8,128)(2,1)} %param.22) | copy-start | bytes 983044
  45.2 19.0 %copy-start.1 = (bf16[1,128,1280]{2,1,0:T(8,128)(2,1)S(1)}, bf16[1,128,1280]{2,1,0:T(8,128)(2,1)}, u32[]{:S(2)}) copy-start(bf16[1,128,1280]{2,1,0:T(8,128)(2,1)} %param.12) | copy-start | bytes 983044
  65.2 81.4 %copy-start.15 = (f32[1280]{0:T(1024)S(1)}, f32[1280]{0:T(1024)}, u32[]{:S(2)}) copy-start(f32[1280]{0:T(1024)} %param.13) | copy-start | bytes 15364
  155.6 164.0 %copy-start.13 = (f32[40,3840]{1,0:T(8,128)S(1)}, f32[40,3840]{1,0:T(8,128)}, u32[]{:S(2)}) copy-start(f32[40,3840]{1,0:T(8,128)} %get-tuple-element.71) | copy-start | bytes 1843204
  155.6 164.9 %copy-start.14 = (f32[40,1280]{1,0:T(8,128)S(1)}, f32[40,1280]{1,0:T(8,128)}, u32[]{:S(2)}) copy-start(f32[40,1280]{1,0:T(8,128)} %get-tuple-element.72) | copy-start | bytes 614404
  275.3 47.9 %copy-start.12 = (f32[160,1280]{1,0:T(8,128)S(1)}, f32[160,1280]{1,0:T(8,128)}, u32[]{:S(2)}) copy-start(f32[160,1280]{1,0:T(8,128)} %get-tuple-element.74) | copy-start | bytes 2457604

commit v3 on v0

--- a/solution.py
+++ b/solution.py
@@ -1,6 +1,8 @@
 import jax
 import jax.numpy as jnp
 from jax import lax
+from jax.experimental import pallas as pl
+from jax.experimental.pallas import tpu as pltpu
 from jax.sharding import PartitionSpec as P
 
 H = 20
@@ -62,7 +64,7 @@
     return (grad_queries, grad_keys, grad_values)
 
 
-def on_device(
+def on_device_general(
     tokens,
     first_gain,
     first_shift,
@@ -215,6 +217,776 @@
     )
 
 
+MESH = pl.DeviceIdType.MESH
+F32 = jnp.float32
+BF16 = jnp.bfloat16
+NN = (((1,), (0,)), ((), ()))
+NT = (((1,), (1,)), ((), ()))
+TN = (((0,), (0,)), ((), ()))
+
+
+def mm(left, right, dims=NN):
+    return lax.dot_general(left, right, dims, preferred_element_type=F32)
+
+
+def remote(src, dst, send, recv, target):
+    return pltpu.make_async_remote_copy(
+        src_ref=src, dst_ref=dst, send_sem=send, recv_sem=recv, device_id=target, device_id_type=MESH
+    )
+
+
+def greet(targets):
+    barrier = pltpu.get_barrier_semaphore()
+    for target in targets:
+        pl.semaphore_signal(barrier, inc=1, device_id=target, device_id_type=MESH)
+    pl.semaphore_wait(barrier, len(targets))
+
+
+def place():
+    dp, blk = lax.axis_index("dp"), lax.axis_index("blk")
+    return dp, blk, dp // 2, lax.rem(dp, 2), blk // 2, lax.rem(blk, 2)
+
+
+def piece(index, size):
+    return pl.ds(pl.multiple_of(index * size, size), size)
+
+
+def flip(mine, other):
+    return mine + other - 2 * mine * other
+
+
+class RowGather:
+    def __init__(self, rows, size, y, c, sibling, ypeer, send, recv):
+        near, far = rows.at[y, piece(c, size)], rows.at[1 - y, piece(c, size)]
+        self.core = remote(near, near, send.at[0], recv.at[0], sibling)
+        self.over = remote(near, near, send.at[1], recv.at[1], ypeer)
+        self.last = remote(far, far, send.at[2], recv.at[2], sibling)
+
+    def start(self):
+        self.over.start()
+        self.core.start()
+
+    def forward(self):
+        self.over.wait_recv()
+        self.last.start()
+
+    def arrive(self):
+        self.core.wait_recv()
+        self.last.wait_recv()
+
+    def drain(self):
+        for copy in (self.core, self.over, self.last):
+            copy.wait_send()
+
+
+class DpGather:
+    def __init__(self, slots, z, x, blk, send, recv):
+        self.slots, self.z, self.x, self.send, self.recv = slots, z, x, send, recv
+        self.targets = ((2 * (z + 1) + x, blk), (2 * (z - 1) + x, blk), (2 * z + 1 - x, blk))
+
+    def hop(self, kind, zz):
+        slot = self.slots.at[self.x, zz]
+        return remote(slot, slot, self.send.at[kind, zz], self.recv.at[self.x, zz], self.targets[kind])
+
+    def up(self, zz):
+        @pl.when(self.z < 3)
+        def _():
+            self.hop(0, zz).start()
+
+        self.hop(2, zz).start()
+
+    def down(self, zz):
+        @pl.when(self.z > 0)
+        def _():
+            self.hop(1, zz).start()
+
+    def start(self):
+        self.up(self.z)
+        self.down(self.z)
+
+    def forward(self, step):
+        below, above = self.z - step, self.z + step
+
+        @pl.when(below >= 0)
+        def _():
+            self.hop(0, below).wait_recv()
+            self.up(below)
+
+        @pl.when(above <= 3)
+        def _():
+            self.hop(1, above).wait_recv()
+            self.down(above)
+            self.hop(2, above).start()
+
+    def arrive(self):
+        for zz in range(4):
+            slot = self.slots.at[1 - self.x, zz]
+            remote(slot, slot, self.send.at[2, zz], self.recv.at[1 - self.x, zz], self.targets[2]).wait_recv()
+
+    def drain(self):
+        for zz in range(4):
+            self.hop(2, zz).wait_send()
+
+            @pl.when((self.z < 3) & (zz <= self.z))
+            def _():
+                self.hop(0, zz).wait_send()
+
+            @pl.when((self.z > 0) & (zz >= self.z))
+            def _():
+                self.hop(1, zz).wait_send()
+
+
+def centered(values):
+    center = values - jnp.mean(values, axis=-1, keepdims=True)
+    spread = jnp.mean(center * center, axis=-1, keepdims=True)
+    scale = lax.rsqrt(spread + EPSILON)
+    return center * scale, scale
+
+
+def norm_back(grad, unit, scale):
+    return scale * (
+        grad - jnp.mean(grad, axis=-1, keepdims=True) - unit * jnp.mean(grad * unit, axis=-1, keepdims=True)
+    )
+
+
+def half_of(pair, head):
+    lanes = lax.broadcasted_iota(jnp.int32, pair.shape, 1) // 64
+    return jnp.where(lanes == head, pair, jnp.zeros_like(pair))
+
+
+def cells_at(cls_ref, places):
+    found = jnp.zeros(places.shape, jnp.int32)
+    for n in range(cls_ref.shape[1]):
+        found = found + (places >= cls_ref[0, n]).astype(jnp.int32)
+    return found
+
+
+def same_cell(cls_ref, start, count, row_len):
+    mine = lax.broadcasted_iota(jnp.int32, (count, 1), 0) + start
+    other = lax.broadcasted_iota(jnp.int32, (1, row_len), 1)
+    return cells_at(cls_ref, mine) == cells_at(cls_ref, other)
+
+
+def gelu_parts(pre):
+    cdf = 0.5 * (1.0 + lax.erf(pre * 0.7071067811865476))
+    return cdf, cdf + pre * (0.3989422804014327 * jnp.exp(-0.5 * pre * pre))
+
+
+def attend_kernel(
+    cls_ref, tok_ref, grad_ref, gain_ref, shift_ref, wqkv_ref,
+    turned_ref, qkv_ref, att_ref, aturned_ref, own_ref, grads_ref,
+    rows, normed, wbuf, low, wsem, gsend, grecv, asend, arecv, dsend, drecv,
+):
+    dp, blk, z, x, y, c = place()
+    tokens, width = tok_ref.shape
+    row_len = 4 * tokens
+    first = 5 * y + 3 * c
+    pairs = 3 - c
+    both = 2 * tokens
+
+    def load(j, t):
+        source = wqkv_ref.at[:, pl.ds(pl.multiple_of(t * width + (first + j) * 128, 128), 128)]
+        return pltpu.make_async_copy(source, wbuf.at[j, :, pl.ds(t * 128, 128)], wsem.at[j, t])
+
+    @pl.loop(0, pairs)
+    def _(j):
+        for t in range(3):
+            load(j, t).start()
+
+    rows[y, piece(c, tokens), :] = tok_ref[...]
+    grads_ref[x, z] = grad_ref[...]
+    sibling, ypeer, diag = (dp, 2 * y + 1 - c), (dp, 2 * (1 - y) + c), (dp, 2 * (1 - y) + 1 - c)
+    greet([sibling, ypeer, diag] + [(2 * lax.rem(z + k, 4) + x, blk) for k in (1, 3)] + [(2 * z + 1 - x, blk)])
+    row = RowGather(rows, tokens, y, c, sibling, ypeer, gsend, grecv)
+    row.start()
+    grads = DpGather(grads_ref, z, x, blk, dsend, drecv)
+    grads.start()
+
+    @pl.loop(0, pairs)
+    def _(j):
+        for t in range(3):
+            load(j, t).wait()
+
+    @pl.loop(0, 2)
+    def _(step):
+        @pl.when(step == 0)
+        def _():
+            row.core.wait_recv()
+
+        @pl.when(step == 1)
+        def _():
+            row.forward()
+            row.last.wait_recv()
+            grads.forward(1)
+
+        chip = flip(y, step)
+        at = piece(chip, both)
+        normed[at, :] = (centered(rows[chip].astype(F32))[0] * gain_ref[...] + shift_ref[...]).astype(BF16)
+
+        @pl.loop(0, pairs)
+        def _(j):
+            made = mm(normed[at, :], wbuf[j])
+            qkv_ref[j, at, 0:128] = (made[:, 0:128] * 0.125).astype(BF16)
+            qkv_ref[j, at, 128:384] = made[:, 128:384].astype(BF16)
+
+    @pl.when(c == 1)
+    def _():
+        qkv_ref[2] = jnp.zeros_like(qkv_ref[2])
+        att_ref[2] = jnp.zeros_like(att_ref[2])
+
+    def to_blk(j, r, target):
+        return remote(low.at[0, j], low.at[r, j], asend.at[r, j], arecv.at[r, j], target)
+
+    others = ((1, sibling), (2, ypeer), (3, diag))
+
+    @pl.loop(0, pairs)
+    def _(j):
+        @pl.loop(0, 2)
+        def _(part):
+            at = piece(part, both)
+            same = same_cell(cls_ref, part * both, both, row_len)
+            pair = jnp.zeros((both, 128), F32)
+            for head in range(2):
+                scores = mm(half_of(qkv_ref[j, at, 0:128], head), qkv_ref[j, :, 128:256], NT)
+                weigh = jnp.where(same, jnp.exp(scores), 0.0)
+                total = jnp.sum(weigh, axis=-1, keepdims=True)
+                pair = pair + half_of(mm(weigh.astype(BF16), qkv_ref[j, :, 256:384]) / total, head)
+            att_ref[j, at, :] = pair
+            low[0, j, at, :] = pair.astype(BF16)
+
+        for r, target in others:
+            to_blk(j, r, target).start()
+
+        @pl.when(j == 0)
+        def _():
+            grads.forward(2)
+
+    for b in range(4):
+        at = slice(b * tokens, (b + 1) * tokens)
+        turned_ref[:, at] = normed[at, :].T
+    grads.forward(3)
+
+    @pl.loop(0, pairs)
+    def _(j):
+        for r, target in others:
+            to_blk(j, r, target).wait_send()
+
+    for r, target, count in ((1, sibling, 2 + c), (2, ypeer, pairs), (3, diag, 2 + c)):
+
+        @pl.loop(0, count)
+        def _(j):
+            to_blk(j, r, target).wait_recv()
+
+    for p in range(10):
+        yy, cc = p // 5, (p % 5) // 3
+        j = p % 5 - 3 * cc
+        slot = 2 * flip(y, yy) + flip(c, cc)
+        aturned_ref[128 * p : 128 * p + 128, :] = low[slot, j].T
+        own_ref[:, 128 * p : 128 * p + 128] = low[slot, j, piece(blk, tokens), :]
+    row.drain()
+    grads.arrive()
+    grads.drain()
+
+
+def attend(cls_positions, tokens, grad, gain, shift, w_qkv):
+    count, width = tokens.shape
+    row_len = 4 * count
+    v = pltpu.VMEM
+    dma = pltpu.SemaphoreType.DMA
+    return pl.pallas_call(
+        attend_kernel,
+        out_shape=(
+            jax.ShapeDtypeStruct((width, row_len), BF16),
+            jax.ShapeDtypeStruct((3, row_len, 384), BF16),
+            jax.ShapeDtypeStruct((3, row_len, 128), F32),
+            jax.ShapeDtypeStruct((width, row_len), BF16),
+            jax.ShapeDtypeStruct((count, width), BF16),
+            jax.ShapeDtypeStruct((2, 4, count, width), BF16),
+        ),
+        in_specs=[pl.BlockSpec(memory_space=pltpu.SMEM)]
+        + [pl.BlockSpec(memory_space=v)] * 4
+        + [pl.BlockSpec(memory_space=pl.ANY)],
+        out_specs=(pl.BlockSpec(memory_space=v),) * 6,
+        scratch_shapes=[
+            v((2, 2 * count, width), BF16), v((row_len, width), BF16), v((3, width, 384), BF16),
+            v((4, 3, row_len, 128), BF16),
+            dma((3, 3)), dma((3,)), dma((3,)), dma((4, 3)), dma((4, 3)), dma((3, 4)), dma((2, 4)),
+        ],
+        compiler_params=pltpu.CompilerParams(collective_id=1, has_side_effects=True, vmem_limit_bytes=48 * 2**20),
+        cost_estimate=pl.CostEstimate(flops=2 * row_len * width * 1152, bytes_accessed=8 * 2**20, transcendentals=0),
+    )(cls_positions, tokens, grad, gain, shift, w_qkv)
+
+
+def rest_kernel(
+    cls_ref, tok_ref, own_ref, qkv_ref, att_ref, turned_ref, aturned_ref, gg,
+    gain1_ref, gain2_ref, shift2_ref, wout_ref, win_ref, wdown_ref, wqkv_ref,
+    layer_ref, tgrad_ref, gqkv_ref, gout_ref, in_ref, down_ref, sums_ref,
+    st_in, st_dn, wi, wd, wo, gx, gp, ht, part_in, part_dn, sib_in, sib_dn, ysend_in, ysend_dn, yrecv_in, yrecv_dn,
+    slab, slab_in, residual, unit, gnorm, grow, gatt, low, keys, values, part, xin, zout, zin, full, fin, landing,
+    sums, sbuf, sbox, tbox,
+    wsem, ssem, osem, gsend, grecv, dsend, drecv, sibs, sibr, ysend, yrecv, qsend, qrecv,
+    xsend, xrecv, zsend, zrecv, fsend, frecv, asend, arecv, usend, urecv, tsend, trecv,
+):
+    dp, blk, z, x, y, c = place()
+    tokens, width = tok_ref.shape
+    row_len, both = 4 * tokens, 2 * tokens
+    first, pairs = 5 * y + 3 * c, 3 - c
+    cut, owned, rows = wi.shape[1], down_ref.shape[0], in_ref.shape[0]
+    share = width // 8
+    block = st_in.shape[2]
+    steps = win_ref.shape[1] // block
+    depth = st_in.shape[0]
+    sibling, ypeer, diag = (dp, 2 * y + 1 - c), (dp, 2 * (1 - y) + c), (dp, 2 * (1 - y) + 1 - c)
+    xpeer = (2 * z + 1 - x, blk)
+    zpeers = [(2 * lax.rem(z + k, 4) + x, blk) for k in range(1, 4)]
+    others = ((1, sibling), (2, ypeer), (3, diag))
+
+    def stream_in(i):
+        slot = lax.rem(i, depth)
+        return pltpu.make_async_copy(win_ref.at[:, piece(i, block)], st_in.at[slot], ssem.at[0, slot])
+
+    def stream_dn(i):
+        slot = lax.rem(i, depth)
+        return pltpu.make_async_copy(wdown_ref.at[piece(i, block), :], st_dn.at[slot], ssem.at[1, slot])
+
+    tails = ((0, block), (1, block), (2, width - 2 * block))
+
+    def load_out(i, size):
+        return pltpu.make_async_copy(
+            wout_ref.at[pl.ds(i * block, size), :], st_dn.at[i, pl.ds(0, size), :], ssem.at[1, i]
+        )
+
+    for i, size in tails:
+        load_out(i, size).start()
+    for i in range(depth - 1):
+        stream_in(i).start()
+
+    def load_rows(j):
+        return pltpu.make_async_copy(wout_ref.at[piece(first + j, 128), :], wo.at[j], osem.at[j])
+
+    @pl.loop(0, pairs)
+    def _(j):
+        load_rows(j).start()
+
+    greet([sibling, ypeer, diag] + [(lax.rem(dp + k, 8), blk) for k in range(1, 8)])
+
+    made = tok_ref[...].astype(F32)
+    for i, size in tails:
+        load_out(i, size).wait()
+        made = made + mm(own_ref[:, i * block : i * block + size], st_dn[i, :size, :])
+    for i in range(depth - 1):
+        stream_dn(i).start()
+    residual[...] = made
+    made, scale2 = centered(made)
+    unit[...] = made
+    gx[x, z] = (made * gain2_ref[...] + shift2_ref[...]).astype(BF16)
+    normed = DpGather(gx, z, x, blk, dsend, drecv)
+    normed.start()
+    gnorm[...] = jnp.zeros_like(gnorm)
+
+    @pl.loop(0, steps)
+    def _(i):
+        slot = lax.rem(i, depth)
+
+        @pl.when(i + depth - 1 < steps)
+        def _():
+            stream_in(i + depth - 1).start()
+            stream_dn(i + depth - 1).start()
+
+        stream_in(i).wait()
+        stream_dn(i).wait()
+        pre = mm(gx[x, z], st_in[slot])
+        cdf, slope = gelu_parts(pre)
+        grad = (mm(gg[x, z], st_dn[slot], NT) * slope).astype(BF16)
+        residual[...] += mm((pre * cdf).astype(BF16), st_dn[slot])
+        gnorm[...] += mm(grad, st_in[slot], NT)
+
+        @pl.when(i == 4)
+        def _():
+            normed.forward(1)
+
+        @pl.when(i == 8)
+        def _():
+            normed.forward(2)
+
+    load_in = pltpu.make_async_copy(win_ref.at[:, piece(dp, cut)], wi, wsem.at[0])
+    load_dn = pltpu.make_async_copy(wdown_ref.at[piece(dp, cut), :], wd, wsem.at[1])
+    load_in.start()
+    load_dn.start()
+    layer = residual[...]
+    layer_ref[...] = layer.astype(BF16)
+    sums[...] = jnp.zeros_like(sums)
+    spots = lax.broadcasted_iota(jnp.int32, (tokens, 1), 0) + blk * tokens
+    chosen = jnp.zeros((tokens, 1), F32)
+    for n in range(cls_ref.shape[1]):
+        chosen = chosen + (spots == cls_ref[0, n]).astype(F32)
+    sums[4:5, :] = jnp.sum(chosen * layer, axis=0, keepdims=True)
+    sums[5:6, :] = jnp.sum(chosen * layer * layer, axis=0, keepdims=True)
+    grad = gnorm[...]
+    sums[2:3, :] = jnp.sum(grad * unit[...], axis=0, keepdims=True)
+    sums[3:4, :] = jnp.sum(grad, axis=0, keepdims=True)
+    made = gg[x, z].astype(F32) + norm_back(grad * gain2_ref[...], unit[...], scale2)
+    residual[...] = made
+    grow[y, piece(c, tokens), :] = made.astype(BF16)
+    row = RowGather(grow, tokens, y, c, sibling, ypeer, gsend, grecv)
+    row.start()
+    load_in.wait()
+    load_dn.wait()
+
+    def make(xx):
+        @pl.loop(0, 2)
+        def _(half):
+            at = piece(2 * xx + half, both)
+            pre = mm(gx[xx, piece(half, 2)].reshape(both, width), wi[...])
+            cdf, slope = gelu_parts(pre)
+            ht[:, at] = (pre * cdf).astype(BF16).T
+            gp[at, :] = (mm(gg[xx, piece(half, 2)].reshape(both, width), wd[...], NT) * slope).astype(BF16)
+
+    normed.forward(3)
+    row.forward()
+    make(x)
+    row.arrive()
+
+    @pl.loop(0, pairs)
+    def _(j):
+        load_rows(j).wait()
+        gatt[j] = mm(grow[...].reshape(row_len, width), wo[j], NT)
+
+    def to_x(s):
+        return remote(part.at[s, 1 - x], xin.at[s], xsend.at[s], xrecv.at[s], xpeer)
+
+    def to_z(s, k):
+        target = lax.rem(z + k, 4)
+        return remote(zout.at[s, target], zin.at[s, k - 1], zsend.at[s, k - 1], zrecv.at[s, k - 1], zpeers[k - 1])
+
+    def to_blk(s, r, target):
+        return remote(full.at[s, target[1]], fin.at[r, s], fsend.at[r, s], frecv.at[r, s], target)
+
+    def to_low(j, r, target):
+        return remote(low.at[j, piece(target[1], tokens), :], landing.at[r, j], asend.at[r, j], arecv.at[r, j], target)
+
+    def add_x(s):
+        to_x(s).wait()
+        for k in range(4):
+            zout[s, k] = (part[s, x, k].astype(F32) + xin[s, k].astype(F32)).astype(BF16)
+        for k in range(1, 4):
+            to_z(s, k).start()
+
+    def add_z(s):
+        for k in range(1, 4):
+            to_z(s, k).wait()
+        total = zout[s, z].astype(F32)
+        for k in range(3):
+            total = total + zin[s, k].astype(F32)
+        for b in range(4):
+            full[s, b] = total[b * rows : (b + 1) * rows]
+        for r, target in others:
+            to_blk(s, r, target).start()
+        fin[0, s] = full[s, blk]
+
+    def weight_part(s, left, right):
+        @pl.loop(0, 4)
+        def _(zz):
+            made = mm(left[piece(zz, 2 * share), :], right)
+            part[s, 0, zz] = made[:share].astype(BF16)
+            part[s, 1, zz] = made[share:].astype(BF16)
+
+    @pl.when(c == 0)
+    def _():
+        weight_part(0, aturned_ref, grow[:, :, pl.ds(pl.multiple_of(first * 128, 128), 384)].reshape(row_len, 384))
+
+    @pl.when(c == 1)
+    def _():
+        right = grow[:, :, pl.ds(pl.multiple_of(first * 128, 128), 256)].reshape(row_len, 256)
+        weight_part(0, aturned_ref, jnp.concatenate([right, jnp.zeros((row_len, 128), BF16)], axis=1))
+
+    to_x(0).start()
+
+    to_sibling = []
+    for kind, source, box in ((0, part_in, sib_in), (1, part_dn, sib_dn)):
+        for yy in range(2):
+            away = source.at[2 * yy + (1 - c)]
+            to_sibling.append(remote(away, box.at[yy], sibs.at[kind, yy], sibr.at[kind, yy], sibling))
+    to_y = (
+        remote(ysend_in, yrecv_in, ysend.at[0], yrecv.at[0], ypeer),
+        remote(ysend_dn, yrecv_dn, ysend.at[1], yrecv.at[1], ypeer),
+    )
+
+    @pl.loop(0, pairs)
+    def _(j):
+        keys[...] = jnp.zeros_like(keys)
+        values[...] = jnp.zeros_like(values)
+
+        @pl.loop(0, 2)
+        def _(half):
+            at = piece(half, both)
+            same = same_cell(cls_ref, half * both, both, row_len)
+            queries_grad = jnp.zeros((both, 128), F32)
+            for head in range(2):
+                query = half_of(qkv_ref[j, at, 0:128], head)
+                key = half_of(qkv_ref[j, :, 128:256], head)
+                grad = half_of(gatt[j, at, :], head)
+                weigh = jnp.where(same, jnp.exp(mm(query, key, NT)), 0.0)
+                total = jnp.sum(weigh, axis=-1, keepdims=True)
+                scaled = (grad / total).astype(BF16)
+                delta = jnp.sum(grad * att_ref[j, at, :], axis=-1, keepdims=True) / total
+                spread = mm(scaled, qkv_ref[j, :, 256:384], NT)
+                score = (weigh * (spread - delta)).astype(BF16)
+                queries_grad = queries_grad + mm(score, key)
+                keys[...] += mm(score, query, TN)
+                values[...] += mm(weigh.astype(BF16), scaled, TN)
+            low[j, at, 0:128] = (queries_grad * 0.125).astype(BF16)
+
+        low[j, :, 128:256] = keys[...].astype(BF16)
+        low[j, :, 256:384] = values[...].astype(BF16)
+        for r, target in others:
+            to_low(j, r, target).start()
+        weight_part(j + 1, turned_ref, low[j])
+        to_x(j + 1).start()
+
+        @pl.when(j == 0)
+        def _():
+            normed.arrive()
+            make(1 - x)
+
+            @pl.loop(0, 2)
+            def _(half):
+                left = gx[:, :, :, piece(half, width // 2)].reshape(8 * tokens, width // 2)
+                made = mm(left, gp[...], TN)
+                for n in range(4):
+                    for q in range(4):
+                        at = n * share + q * rows
+                        part_in[q, 4 * half + n] = made[at : at + rows].astype(BF16)
+
+            to_sibling[0].start()
+            to_sibling[1].start()
+            every = gg[...].reshape(8 * tokens, width)
+
+            @pl.loop(0, 4)
+            def _(q):
+                part_dn[q] = mm(ht[piece(q, owned), :], every).astype(BF16)
+
+            to_sibling[2].start()
+            to_sibling[3].start()
+
+        add_x(j)
+
+        @pl.when(j > 0)
+        def _():
+            add_z(j - 1)
+
+        @pl.when(j == 1)
+        def _():
+            for copy in to_sibling:
+                copy.wait()
+            over = 2 * (1 - y) + c
+            ysend_in[...] = (part_in[over].astype(F32) + sib_in[1 - y].astype(F32)).astype(BF16)
+            to_y[0].start()
+            ysend_dn[...] = (part_dn[over].astype(F32) + sib_dn[1 - y].astype(F32)).astype(BF16)
+            to_y[1].start()
+
+    @pl.loop(0, pairs)
+    def _(j):
+        landing[0, j] = low[j, piece(blk, tokens), :]
+        for r, target in others:
+            to_low(j, r, target).wait_send()
+
+    for r, target, count in ((1, sibling, 2 + c), (2, ypeer, pairs), (3, diag, 2 + c)):
+
+        @pl.loop(0, count)
+        def _(j):
+            to_low(j, r, target).wait_recv()
+
+    def stream_qkv(p, t):
+        slot = lax.rem(p, depth)
+        source = wqkv_ref.at[:, pl.ds(pl.multiple_of(t * width + p * 128, 128), 128)]
+        return pltpu.make_async_copy(source, st_in.at[slot, :, pl.ds(t * 128, 128)], wsem.at[2 + 3 * slot + t])
+
+    for p in range(depth - 1):
+        for t in range(3):
+            stream_qkv(p, t).start()
+    gnorm[...] = jnp.zeros_like(gnorm)
+    mine = 2 * y + c
+    to_q = []
+    for k in range(1, 8):
+        target = lax.rem(dp + k, 8)
+        to_q.append(remote(slab.at[target], slab_in.at[dp], qsend.at[k], qrecv.at[k], (target, blk)))
+
+    @pl.loop(0, 10)
+    def _(p):
+        @pl.when(p + depth - 1 < 10)
+        def _():
+            for t in range(3):
+                stream_qkv(p + depth - 1, t).start()
+
+        for t in range(3):
+            stream_qkv(p, t).wait()
+        yy, pp = p // 5, lax.rem(p, 5)
+        cc = pp // 3
+        slot = 2 * flip(y, yy) + flip(c, cc)
+        gnorm[...] += mm(landing[slot, pp - 3 * cc], st_in[lax.rem(p, depth), :, 0:384], NT)
+
+        @pl.when(p == 3)
+        def _():
+            add_x(pairs)
+
+        @pl.when(p == 6)
+        def _():
+            to_y[0].wait()
+            total = part_in[mine].astype(F32) + sib_in[y].astype(F32) + yrecv_in[...].astype(F32)
+            slab[...] = total.astype(BF16)
+            for copy in to_q:
+                copy.start()
+            slab_in[dp] = slab[dp]
+
+    grad = gnorm[...]
+    made, scale1 = centered(tok_ref[...].astype(F32))
+    sums[0:1, :] = jnp.sum(grad * made, axis=0, keepdims=True)
+    sums[1:2, :] = jnp.sum(grad, axis=0, keepdims=True)
+    sbuf[...] = jnp.zeros_like(sbuf)
+    for k in range(8):
+        sbuf[k, :, 0:share] = sums[:, k * share : (k + 1) * share]
+    to_u = []
+    for k in range(1, 8):
+        target = lax.rem(dp + k, 8)
+        to_u.append(remote(sbuf.at[target], sbox.at[dp], usend.at[k], urecv.at[k], (target, blk)))
+        to_u[-1].start()
+    sbox[dp] = sbuf[dp]
+    tgrad_ref[...] = (residual[...] + norm_back(grad * gain1_ref[...], made, scale1)).astype(BF16)
+    add_z(pairs - 1)
+    for copy in to_u:
+        copy.wait()
+    tbox[0] = jnp.sum(sbox[...], axis=0)
+    to_t = [remote(tbox.at[0], tbox.at[r], tsend.at[r], trecv.at[r], target) for r, target in others]
+    for copy in to_t:
+        copy.start()
+    to_y[1].wait()
+    down_ref[...] = part_dn[mine].astype(F32) + sib_dn[y].astype(F32) + yrecv_dn[...].astype(F32)
+    for copy in to_q:
+        copy.wait()
+    for s in range(8):
+        in_ref[:, s * cut : (s + 1) * cut] = slab_in[s].astype(F32)
+    add_z(pairs)
+    for copy in to_t:
+        copy.wait()
+    sums_ref[...] = (tbox[0] + tbox[1]) + (tbox[2] + tbox[3])
+
+    @pl.loop(0, pairs + 1)
+    def _(s):
+        for r, target in others:
+            to_blk(s, r, target).wait_send()
+
+    for r, target, count in ((1, sibling, 2 + c), (2, ypeer, pairs), (3, diag, 2 + c)):
+
+        @pl.loop(0, count + 1)
+        def _(s):
+            to_blk(s, r, target).wait_recv()
+
+    for yy in range(2):
+        for cc in range(2):
+            slot = 2 * flip(y, yy) + flip(c, cc)
+            p = 5 * yy + 3 * cc
+            wide = 128 * (3 - cc)
+            gout_ref[:, 128 * p : 128 * p + wide] = fin[slot, 0, :, :wide]
+            for j in range(3 - cc):
+                for t in range(3):
+                    at = t * width + 128 * (p + j)
+                    gqkv_ref[:, at : at + 128] = fin[slot, j + 1, :, 128 * t : 128 * t + 128]
+    row.drain()
+    normed.drain()
+
+
+def rest(cls_positions, tokens, own, qkv, att, turned, aturned, grads, gain1, gain2, shift2, w_out, w_in, w_down, w_qkv):
+    count, width = tokens.shape
+    inner = w_in.shape[1]
+    row_len, share = 4 * count, width // 8
+    cut, owned, rows = inner // 8, inner // 32, width // 32
+    block, depth = 512, 3
+    v = pltpu.VMEM
+    dma = pltpu.SemaphoreType.DMA
+    return pl.pallas_call(
+        rest_kernel,
+        out_shape=(
+            jax.ShapeDtypeStruct((count, width), BF16),
+            jax.ShapeDtypeStruct((count, width), BF16),
+            jax.ShapeDtypeStruct((rows, 3 * width), F32),
+            jax.ShapeDtypeStruct((rows, width), F32),
+            jax.ShapeDtypeStruct((rows, inner), F32),
+            jax.ShapeDtypeStruct((owned, width), F32),
+            jax.ShapeDtypeStruct((8, 256), F32),
+        ),
+        in_specs=[pl.BlockSpec(memory_space=pltpu.SMEM)]
+        + [pl.BlockSpec(memory_space=v)] * 10
+        + [pl.BlockSpec(memory_space=pl.ANY)] * 4,
+        out_specs=(pl.BlockSpec(memory_space=v),) * 7,
+        scratch_shapes=[
+            v((depth, width, block), BF16), v((depth, block, width), BF16),
+            v((width, cut), BF16), v((cut, width), BF16), v((3, 128, width), BF16),
+            v((2, 4, count, width), BF16), v((8 * count, cut), BF16), v((cut, 8 * count), BF16),
+            v((4, 8, rows, cut), BF16), v((4, owned, width), BF16),
+            v((2, 8, rows, cut), BF16), v((2, owned, width), BF16),
+            v((8, rows, cut), BF16), v((owned, width), BF16), v((8, rows, cut), BF16), v((owned, width), BF16),
+            v((8, rows, cut), BF16), v((8, rows, cut), BF16),
+            v((count, width), F32), v((count, width), F32), v((count, width), F32),
+            v((2, 2 * count, width), BF16), v((3, row_len, 128), F32), v((3, row_len, 384), BF16),
+            v((row_len, 128), F32), v((row_len, 128), F32),
+            v((4, 2, 4, share, 384), BF16), v((4, 4, share, 384), BF16), v((4, 4, share, 384), BF16),
+            v((4, 3, share, 384), BF16), v((4, 4, share // 4, 384), F32), v((4, 4, share // 4, 384), F32),
+            v((4, 3, count, 384), BF16),
+            v((8, width), F32), v((8, 8, 256), F32), v((8, 8, 256), F32), v((4, 8, 256), F32),
+            dma((2 + 3 * depth,)), dma((2, depth)), dma((3,)), dma((3,)), dma((3,)), dma((3, 4)), dma((2, 4)),
+            dma((2, 2)), dma((2, 2)), dma((2,)), dma((2,)), dma((8,)), dma((8,)),
+            dma((4,)), dma((4,)), dma((4, 3)), dma((4, 3)), dma((4, 4)), dma((4, 4)), dma((4, 3)), dma((4, 3)),
+            dma((8,)), dma((8,)), dma((4,)), dma((4,)),
+        ],
+        compiler_params=pltpu.CompilerParams(collective_id=2, has_side_effects=True, vmem_limit_bytes=64 * 2**20),
+        cost_estimate=pl.CostEstimate(flops=40 * 2**30, bytes_accessed=50 * 2**20, transcendentals=0),
+    )(cls_positions, tokens, own, qkv, att, turned, aturned, grads, gain1, gain2, shift2, w_out, w_in, w_down, w_qkv)
+
+
+def on_device(
+    tokens,
+    first_gain,
+    first_shift,
+    w_qkv,
+    w_out,
+    second_gain,
+    second_shift,
+    w_in,
+    w_down,
+    segment_ids,
+    cls_positions,
+    out_grad,
+):
+    tokens, out_grad = tokens[0], out_grad[0]
+    turned, qkv, att, aturned, own, grads = attend(
+        cls_positions, tokens, out_grad, first_gain[None], first_shift[None], w_qkv
+    )
+    layer, tokens_grad, grad_qkv, grad_out, grad_in, grad_down, sums = rest(
+        cls_positions, tokens, own, qkv, att, turned, aturned, grads,
+        first_gain[None], second_gain[None], second_shift[None], w_out, w_in, w_down, w_qkv,
+    )
+    count = cls_positions.shape[0] * cls_positions.shape[1] * lax.axis_size("dp")
+    share = tokens.shape[1] // (lax.axis_size("dp") * lax.axis_size("blk"))
+    mine = lax.dynamic_slice_in_dim(sums, lax.axis_index("blk") * share, share, axis=1)
+    cls_mean = mine[4] / count
+    cls_variance = mine[5] / count - cls_mean * cls_mean
+    return (
+        layer[None],
+        tokens_grad[None],
+        grad_qkv,
+        grad_out,
+        grad_in,
+        grad_down,
+        mine[0],
+        mine[1],
+        mine[2],
+        mine[3],
+        cls_mean,
+        cls_variance,
+    )
+
+
 def solution(mesh):
     placed = (
         P("dp", "blk", None),
@@ -230,8 +1002,9 @@
         P("dp", None),
         P("dp", "blk", None),
     )
+    small = mesh.shape["dp"] == 8 and mesh.shape["blk"] == 4
     return jax.shard_map(
-        on_device,
+        on_device if small else on_device_general,
         mesh=mesh,
         in_specs=placed,
         out_specs=(

time: 1070 us -> 183 us (0.17)
  waiting for transfers between devices: 764 us -> 0 us
  Pallas kernels: 0 us -> 160 us
  matrix products: 141 us -> 0 us
  blocking collectives: 49 us -> 0 us
  other arithmetic: 26 us -> 0.52 us
  starting transfers between devices: 25.1 us -> 0 us
  local copies, waits for them, and re-layouts: 45 us -> 20.2 us
  between operations: 14.2 us -> 0.71 us
    reduce_scatter x4 -> x0, waiting for transfers between devices: 674 us -> none  [the longest x1 284 us: on_device(): lax.psum_scatter(grad_in, ('dp', 'blk'), scatter_dimension=0, tiled=True)]
    pallas_call x0 -> x2, Pallas kernels: none -> 160 us  [the longest x1 116 us: rest(): pl.pallas_call(rest_kernel, out_shape=(jax.ShapeDtypeStruct((count, width...]
    dot_general x40 -> x0, matrix products: 141 us -> none  [the longest x1 16 us: on_device(): jnp.einsum('sbf,sbd->fd', hidden_low, out_grad, preferred_element_type=jn...]
    ppermute x29 -> x0, waiting for transfers between devices: 90 us -> none  [shifted(): return lax.ppermute(block, axis, route)]
    unnamed x1 -> x0, blocking collectives: 49 us -> none
    ppermute x29 -> x0, starting transfers between devices: 24.4 us -> none  [shifted(): return lax.ppermute(block, axis, route)]
    while x65 -> x0, local copies, waits for them, and re-layouts: 24.1 us -> none
    convert_element_type x11 -> x0, other arithmetic: 16.7 us -> none  [the longest x4 7.5 us: key_step(): shifted(keys_next.astype(jnp.bfloat16), 'blk', 1).astype(keys_next.dtype)]
  transfers between devices with their start and end apart: 33 -> 0, of which waited for: 19 -> 0; matrix products, arithmetic and copies ran while one was open for 12% -> 0% of each run, Pallas kernels for 0% -> 0%
where the time goes in v3:
time: 183 us; the launch traced here: 181 us
  Pallas kernels  160 us (87%)
  local copies, waits for them, and re-layouts  20.2 us (11%)
    pallas_call x1, Pallas kernels, rest(): pl.pallas_call(rest_kernel, out_shape=(jax.ShapeDtypeStruct((count, width...  116 us
    pallas_call x1, Pallas kernels, attend(): pl.pallas_call(attend_kernel, out_shape=(jax.ShapeDtypeStruct((width, row...  44.1 us
    unnamed x32, local copies, waits for them, and re-layouts  16.2 us

profile of v3, /device:TPU:0, one launch (start us, length us, event | category | flops | bytes accessed | tf_op | source)
XLA Modules:
  0.0 181.1 jit_solution(1754120642263148319)
XLA Ops:
  0.6 0.7 broadcast_in_dim.19.gain_ref.gain1_ref
  1.3 0.0 copy-start.2
  1.3 0.7 broadcast_in_dim.20.shift_ref
  2.1 0.0 copy-start
  2.1 1.0 copy-done
  3.0 0.0 copy-start.1
  3.0 1.0 copy-done.1
  4.0 0.0 copy-start.3
  4.0 0.7 copy-done.3
  4.7 0.0 copy-start.11
  4.7 0.0 copy-start.12
  4.7 44.1 %shard_map.202 = (bf16[1280,512]{1,0:T(8,128)(2,1)S(1)}, bf16[3,512,384]{2,1,0:T(8,128)(2,1)S(1)}, f32[3,512,128]{2,1,0:T(8,128)S(1)}, bf16[1280,512]{1,0:T(8,12...) custom-call(s32[1,4]{1,0:T(1,128)S(1)} %copy-done.3, bf16[128,1280]{1,0:T(8,128)(2,1)S(1)} %bitcast.19, ...), custom_call_target="tpu_custom_call" | custom-call | flops 1509949440 | bytes 8388608 | tf_op jit(solution)/shard_map/pallas_call | solution.py:496
  48.8 0.0 copy-done.2
  48.8 0.0 copy-start.4
  48.8 1.1 copy-done.4
  49.9 0.0 copy-start.5
  49.9 1.1 copy-done.5
  50.9 0.0 copy-start.6
  50.9 1.0 copy-done.6
  52.0 0.0 copy-start.7
  52.0 0.9 copy-done.7
  52.8 0.0 copy-start.8
  52.8 0.7 copy-done.8
  53.6 0.0 copy-done.11
  53.6 0.6 broadcast_in_dim.21.gain2_ref
  54.2 0.0 copy-done.12
  54.2 0.6 broadcast_in_dim.22.shift2_ref
  54.8 115.5 %shard_map.203 = (bf16[128,1280]{1,0:T(8,128)(2,1)}, bf16[128,1280]{1,0:T(8,128)(2,1)}, f32[40,3840]{1,0:T(8,128)}, f32[40,1280]{1,0:T(8,128)}, f32[40,5120]{1,0...) custom-call(s32[1,4]{1,0:T(1,128)} %cls_ref.3, bf16[128,1280]{1,0:T(8,128)(2,1)} %bitcast.18, ...), custom_call_target="tpu_custom_call" | custom-call | flops 42949672960 | bytes 52428800 | tf_op jit(solution)/shard_map/pallas_call | solution.py:907
  170.3 0.0 copy-start.10
  170.3 0.0 copy-start.9
  170.3 0.9 constant_dynamic-slice_fusion
  171.2 0.5 slice_bitcast_fusion
  171.8 0.5 bitcast_subtract_fusion
  172.3 1.7 copy.29
  174.0 1.7 copy.30
  175.7 1.9 %copy.31 = f32[40,3840]{1,0:T(8,128)} copy(f32[40,3840]{1,0:T(8,128)} %get-tuple-element.58) | data formatting | bytes 1228800
  177.6 1.6 copy.32
  179.3 0.0 copy-done.10
  179.3 0.9 copy.33
  180.2 0.0 copy-done.9
  180.2 0.9 copy.34
Async XLA Ops:
  1.3 47.4 %copy-start.2 = (f32[1,1280]{1,0:T(1,128)}, f32[1,1280]{1,0:T(1,128)S(1)}, u32[]{:S(2)}) copy-start(f32[1,1280]{1,0:T(1,128)S(1)} %broadcast_in_dim.19.gain_ref.gain1_ref) | copy-start | bytes 15364
  2.1 1.0 copy-start
  3.0 1.0 copy-start.1
  4.0 0.7 copy-start.3
  4.7 48.9 %copy-start.11 = (f32[1280]{0:T(1024)S(1)}, f32[1280]{0:T(1024)}, u32[]{:S(2)}) copy-start(f32[1280]{0:T(1024)} %param.17) | copy-start | bytes 15364
  4.7 49.5 %copy-start.12 = (f32[1280]{0:T(1024)S(1)}, f32[1280]{0:T(1024)}, u32[]{:S(2)}) copy-start(f32[1280]{0:T(1024)} %param.18) | copy-start | bytes 15364
  48.8 1.1 copy-start.4
  49.9 1.1 copy-start.5
  50.9 1.0 copy-start.6
  52.0 0.9 copy-start.7
  52.8 0.7 copy-start.8
  170.3 9.0 %copy-start.10 = (f32[40,5120]{1,0:T(8,128)S(1)}, f32[40,5120]{1,0:T(8,128)}, u32[]{:S(2)}) copy-start(f32[40,5120]{1,0:T(8,128)} %get-tuple-element.60) | copy-start | bytes 2457604
  170.3 9.8 %copy-start.9 = (f32[160,1280]{1,0:T(8,128)S(1)}, f32[160,1280]{1,0:T(8,128)}, u32[]{:S(2)}) copy-start(f32[160,1280]{1,0:T(8,128)} %get-tuple-element.61) | copy-start | bytes 2457604

commit v4 on v3

--- a/solution.py
+++ b/solution.py
@@ -1,3 +1,5 @@
+import functools
+
 import jax
 import jax.numpy as jnp
 from jax import lax
@@ -372,72 +374,114 @@
     return cdf, cdf + pre * (0.3989422804014327 * jnp.exp(-0.5 * pre * pre))
 
 
-def attend_kernel(
-    cls_ref, tok_ref, grad_ref, gain_ref, shift_ref, wqkv_ref,
-    turned_ref, qkv_ref, att_ref, aturned_ref, own_ref, grads_ref,
-    rows, normed, wbuf, low, wsem, gsend, grecv, asend, arecv, dsend, drecv,
+def as_row(ref):
+    return ref[...].reshape(1, ref.shape[0])
+
+
+def layer_kernel(
+    cls_ref, tok_hbm, grad_hbm, gain1_ref, shift1_ref, gain2_ref, shift2_ref, wqkv_ref, wout_ref, win_ref, wdown_ref,
+    layer_out, tgrad_out, gqkv_out, gout_out, in_out, down_out, sums_ref,
+    gg, rows_all, qkv_ref, att_ref, turned_ref, aturned_ref, attlow, abox, arow,
+    layer_ref, tgrad_ref, gqkv_ref, gout_ref, in_ref, down_ref,
+    st_in, st_dn, wi, wd, wo, gx, gp, ht, part_in, part_dn, sib_in, sib_dn, ysend_in, ysend_dn, yrecv_in, yrecv_dn,
+    slab, slab_in, residual, unit, gnorm, grow, gatt, low, keys, values, part, xin, zout, zin, full, fin, landing,
+    sums, sbuf, sbox, tbox,
+    isem, lsem, rsend, rrecv, ogsend, ogrecv, bsend, brecv, arsend, arrecv, outsem,
+    wsem, ssem, osem, gsend, grecv, dsend, drecv, sibs, sibr, ysend, yrecv, qsend, qrecv,
+    xsend, xrecv, zsend, zrecv, fsend, frecv, asend, arecv, usend, urecv, tsend, trecv,
 ):
     dp, blk, z, x, y, c = place()
-    tokens, width = tok_ref.shape
-    row_len = 4 * tokens
-    first = 5 * y + 3 * c
-    pairs = 3 - c
-    both = 2 * tokens
+    tokens, width = tok_hbm.shape
+    row_len, both = 4 * tokens, 2 * tokens
+    first, pairs = 5 * y + 3 * c, 3 - c
+    cut, owned, rows = wi.shape[1], down_ref.shape[0], in_ref.shape[0]
+    share = width // 8
+    block = st_in.shape[2]
+    steps = win_ref.shape[1] // block
+    depth = st_in.shape[0]
+    sibling, ypeer, diag = (dp, 2 * y + 1 - c), (dp, 2 * (1 - y) + c), (dp, 2 * (1 - y) + 1 - c)
+    xpeer = (2 * z + 1 - x, blk)
+    zpeers = [(2 * lax.rem(z + k, 4) + x, blk) for k in range(1, 4)]
+    others = ((1, sibling), (2, ypeer), (3, diag))
+    received = ((1, sibling, 2 + c), (2, ypeer, pairs), (3, diag, 2 + c))
+
+    tok_in = pltpu.make_async_copy(tok_hbm, rows_all.at[y, piece(c, tokens), :], isem.at[0])
+    grad_in = pltpu.make_async_copy(grad_hbm, gg.at[x, z], isem.at[1])
+    tok_in.start()
+    grad_in.start()
 
     def load(j, t):
         source = wqkv_ref.at[:, pl.ds(pl.multiple_of(t * width + (first + j) * 128, 128), 128)]
-        return pltpu.make_async_copy(source, wbuf.at[j, :, pl.ds(t * 128, 128)], wsem.at[j, t])
+        return pltpu.make_async_copy(source, st_in.at[j, :, pl.ds(t * 128, 128)], lsem.at[j, t])
 
     @pl.loop(0, pairs)
     def _(j):
         for t in range(3):
             load(j, t).start()
 
-    rows[y, piece(c, tokens), :] = tok_ref[...]
-    grads_ref[x, z] = grad_ref[...]
-    sibling, ypeer, diag = (dp, 2 * y + 1 - c), (dp, 2 * (1 - y) + c), (dp, 2 * (1 - y) + 1 - c)
-    greet([sibling, ypeer, diag] + [(2 * lax.rem(z + k, 4) + x, blk) for k in (1, 3)] + [(2 * z + 1 - x, blk)])
-    row = RowGather(rows, tokens, y, c, sibling, ypeer, gsend, grecv)
-    row.start()
-    grads = DpGather(grads_ref, z, x, blk, dsend, drecv)
+    def stream_in(i):
+        slot = lax.rem(i, depth)
+        return pltpu.make_async_copy(win_ref.at[:, piece(i, block)], st_in.at[slot], ssem.at[0, slot])
+
+    def stream_dn(i):
+        slot = lax.rem(i, depth)
+        return pltpu.make_async_copy(wdown_ref.at[piece(i, block), :], st_dn.at[slot], ssem.at[1, slot])
+
+    tails = ((0, block), (1, block), (2, width - 2 * block))
+
+    def load_out(i, size):
+        return pltpu.make_async_copy(
+            wout_ref.at[pl.ds(i * block, size), :], st_dn.at[i, pl.ds(0, size), :], ssem.at[1, i]
+        )
+
+    def load_rows(j):
+        return pltpu.make_async_copy(wout_ref.at[piece(first + j, 128), :], wo.at[j], osem.at[j])
+
+    greet([sibling, ypeer, diag] + [(lax.rem(dp + k, 8), blk) for k in range(1, 8)])
+    row_tok = RowGather(rows_all, tokens, y, c, sibling, ypeer, rsend, rrecv)
+    grads = DpGather(gg, z, x, blk, ogsend, ogrecv)
+    tok_in.wait()
+    row_tok.start()
+    grad_in.wait()
     grads.start()
+    for i, size in tails:
+        load_out(i, size).start()
 
     @pl.loop(0, pairs)
     def _(j):
+        load_rows(j).start()
         for t in range(3):
             load(j, t).wait()
+
+    normed_rows = wd
 
     @pl.loop(0, 2)
     def _(step):
         @pl.when(step == 0)
         def _():
-            row.core.wait_recv()
+            row_tok.core.wait_recv()
 
         @pl.when(step == 1)
         def _():
-            row.forward()
-            row.last.wait_recv()
+            row_tok.forward()
+            row_tok.last.wait_recv()
             grads.forward(1)
 
         chip = flip(y, step)
         at = piece(chip, both)
-        normed[at, :] = (centered(rows[chip].astype(F32))[0] * gain_ref[...] + shift_ref[...]).astype(BF16)
+        normed_rows[at, :] = (centered(rows_all[chip].astype(F32))[0] * as_row(gain1_ref) + as_row(shift1_ref)).astype(BF16)
 
         @pl.loop(0, pairs)
         def _(j):
-            made = mm(normed[at, :], wbuf[j])
+            made = mm(normed_rows[at, :], st_in[j, :, 0:384])
             qkv_ref[j, at, 0:128] = (made[:, 0:128] * 0.125).astype(BF16)
             qkv_ref[j, at, 128:384] = made[:, 128:384].astype(BF16)
 
-    @pl.when(c == 1)
-    def _():
-        qkv_ref[2] = jnp.zeros_like(qkv_ref[2])
-        att_ref[2] = jnp.zeros_like(att_ref[2])
-
-    def to_blk(j, r, target):
-        return remote(low.at[0, j], low.at[r, j], asend.at[r, j], arecv.at[r, j], target)
-
-    others = ((1, sibling), (2, ypeer), (3, diag))
+    for i in range(depth - 1):
+        stream_in(i).start()
+
+    def to_own(j, r, target):
+        return remote(attlow.at[j, piece(target[1], tokens), :], abox.at[r, j], bsend.at[r, j], brecv.at[r, j], target)
 
     @pl.loop(0, pairs)
     def _(j):
@@ -452,136 +496,43 @@
                 total = jnp.sum(weigh, axis=-1, keepdims=True)
                 pair = pair + half_of(mm(weigh.astype(BF16), qkv_ref[j, :, 256:384]) / total, head)
             att_ref[j, at, :] = pair
-            low[0, j, at, :] = pair.astype(BF16)
+            attlow[j, at, :] = pair.astype(BF16)
 
         for r, target in others:
-            to_blk(j, r, target).start()
-
-        @pl.when(j == 0)
-        def _():
-            grads.forward(2)
-
+            to_own(j, r, target).start()
+        abox[0, j] = attlow[j, piece(blk, tokens), :]
+
+    grads.forward(2)
     for b in range(4):
         at = slice(b * tokens, (b + 1) * tokens)
-        turned_ref[:, at] = normed[at, :].T
-    grads.forward(3)
-
-    @pl.loop(0, pairs)
-    def _(j):
-        for r, target in others:
-            to_blk(j, r, target).wait_send()
-
-    for r, target, count in ((1, sibling, 2 + c), (2, ypeer, pairs), (3, diag, 2 + c)):
+        turned_ref[:, at] = normed_rows[at, :].T
+
+    for r, target, count in received:
 
         @pl.loop(0, count)
         def _(j):
-            to_blk(j, r, target).wait_recv()
-
+            to_own(j, r, target).wait_recv()
+
+    own_at = (y, piece(c, tokens))
     for p in range(10):
         yy, cc = p // 5, (p % 5) // 3
-        j = p % 5 - 3 * cc
         slot = 2 * flip(y, yy) + flip(c, cc)
-        aturned_ref[128 * p : 128 * p + 128, :] = low[slot, j].T
-        own_ref[:, 128 * p : 128 * p + 128] = low[slot, j, piece(blk, tokens), :]
-    row.drain()
-    grads.arrive()
-    grads.drain()
-
-
-def attend(cls_positions, tokens, grad, gain, shift, w_qkv):
-    count, width = tokens.shape
-    row_len = 4 * count
-    v = pltpu.VMEM
-    dma = pltpu.SemaphoreType.DMA
-    return pl.pallas_call(
-        attend_kernel,
-        out_shape=(
-            jax.ShapeDtypeStruct((width, row_len), BF16),
-            jax.ShapeDtypeStruct((3, row_len, 384), BF16),
-            jax.ShapeDtypeStruct((3, row_len, 128), F32),
-            jax.ShapeDtypeStruct((width, row_len), BF16),
-            jax.ShapeDtypeStruct((count, width), BF16),
-            jax.ShapeDtypeStruct((2, 4, count, width), BF16),
-        ),
-        in_specs=[pl.BlockSpec(memory_space=pltpu.SMEM)]
-        + [pl.BlockSpec(memory_space=v)] * 4
-        + [pl.BlockSpec(memory_space=pl.ANY)],
-        out_specs=(pl.BlockSpec(memory_space=v),) * 6,
-        scratch_shapes=[
-            v((2, 2 * count, width), BF16), v((row_len, width), BF16), v((3, width, 384), BF16),
-            v((4, 3, row_len, 128), BF16),
-            dma((3, 3)), dma((3,)), dma((3,)), dma((4, 3)), dma((4, 3)), dma((3, 4)), dma((2, 4)),
-        ],
-        compiler_params=pltpu.CompilerParams(collective_id=1, has_side_effects=True, vmem_limit_bytes=48 * 2**20),
-        cost_estimate=pl.CostEstimate(flops=2 * row_len * width * 1152, bytes_accessed=8 * 2**20, transcendentals=0),
-    )(cls_positions, tokens, grad, gain, shift, w_qkv)
-
-
-def rest_kernel(
-    cls_ref, tok_ref, own_ref, qkv_ref, att_ref, turned_ref, aturned_ref, gg,
-    gain1_ref, gain2_ref, shift2_ref, wout_ref, win_ref, wdown_ref, wqkv_ref,
-    layer_ref, tgrad_ref, gqkv_ref, gout_ref, in_ref, down_ref, sums_ref,
-    st_in, st_dn, wi, wd, wo, gx, gp, ht, part_in, part_dn, sib_in, sib_dn, ysend_in, ysend_dn, yrecv_in, yrecv_dn,
-    slab, slab_in, residual, unit, gnorm, grow, gatt, low, keys, values, part, xin, zout, zin, full, fin, landing,
-    sums, sbuf, sbox, tbox,
-    wsem, ssem, osem, gsend, grecv, dsend, drecv, sibs, sibr, ysend, yrecv, qsend, qrecv,
-    xsend, xrecv, zsend, zrecv, fsend, frecv, asend, arecv, usend, urecv, tsend, trecv,
-):
-    dp, blk, z, x, y, c = place()
-    tokens, width = tok_ref.shape
-    row_len, both = 4 * tokens, 2 * tokens
-    first, pairs = 5 * y + 3 * c, 3 - c
-    cut, owned, rows = wi.shape[1], down_ref.shape[0], in_ref.shape[0]
-    share = width // 8
-    block = st_in.shape[2]
-    steps = win_ref.shape[1] // block
-    depth = st_in.shape[0]
-    sibling, ypeer, diag = (dp, 2 * y + 1 - c), (dp, 2 * (1 - y) + c), (dp, 2 * (1 - y) + 1 - c)
-    xpeer = (2 * z + 1 - x, blk)
-    zpeers = [(2 * lax.rem(z + k, 4) + x, blk) for k in range(1, 4)]
-    others = ((1, sibling), (2, ypeer), (3, diag))
-
-    def stream_in(i):
-        slot = lax.rem(i, depth)
-        return pltpu.make_async_copy(win_ref.at[:, piece(i, block)], st_in.at[slot], ssem.at[0, slot])
-
-    def stream_dn(i):
-        slot = lax.rem(i, depth)
-        return pltpu.make_async_copy(wdown_ref.at[piece(i, block), :], st_dn.at[slot], ssem.at[1, slot])
-
-    tails = ((0, block), (1, block), (2, width - 2 * block))
-
-    def load_out(i, size):
-        return pltpu.make_async_copy(
-            wout_ref.at[pl.ds(i * block, size), :], st_dn.at[i, pl.ds(0, size), :], ssem.at[1, i]
-        )
-
-    for i, size in tails:
-        load_out(i, size).start()
-    for i in range(depth - 1):
-        stream_in(i).start()
-
-    def load_rows(j):
-        return pltpu.make_async_copy(wout_ref.at[piece(first + j, 128), :], wo.at[j], osem.at[j])
-
-    @pl.loop(0, pairs)
-    def _(j):
-        load_rows(j).start()
-
-    greet([sibling, ypeer, diag] + [(lax.rem(dp + k, 8), blk) for k in range(1, 8)])
-
-    made = tok_ref[...].astype(F32)
+        arow[y, piece(c, tokens), 128 * p : 128 * p + 128] = abox[slot, p % 5 - 3 * cc]
+    row_att = RowGather(arow, tokens, y, c, sibling, ypeer, arsend, arrecv)
+
+    made = rows_all[y, piece(c, tokens), :].astype(F32)
     for i, size in tails:
         load_out(i, size).wait()
-        made = made + mm(own_ref[:, i * block : i * block + size], st_dn[i, :size, :])
+        made = made + mm(arow[y, piece(c, tokens), i * block : i * block + size], st_dn[i, :size, :])
     for i in range(depth - 1):
         stream_dn(i).start()
     residual[...] = made
     made, scale2 = centered(made)
     unit[...] = made
-    gx[x, z] = (made * gain2_ref[...] + shift2_ref[...]).astype(BF16)
+    gx[x, z] = (made * as_row(gain2_ref) + as_row(shift2_ref)).astype(BF16)
     normed = DpGather(gx, z, x, blk, dsend, drecv)
     normed.start()
+    row_att.start()
     gnorm[...] = jnp.zeros_like(gnorm)
 
     @pl.loop(0, steps)
@@ -601,8 +552,13 @@
         residual[...] += mm((pre * cdf).astype(BF16), st_dn[slot])
         gnorm[...] += mm(grad, st_in[slot], NT)
 
+        @pl.when(i == 1)
+        def _():
+            grads.forward(3)
+
         @pl.when(i == 4)
         def _():
+            row_att.forward()
             normed.forward(1)
 
         @pl.when(i == 8)
@@ -615,6 +571,8 @@
     load_dn.start()
     layer = residual[...]
     layer_ref[...] = layer.astype(BF16)
+    outs = [pltpu.make_async_copy(layer_ref, layer_out, outsem.at[0])]
+    outs[0].start()
     sums[...] = jnp.zeros_like(sums)
     spots = lax.broadcasted_iota(jnp.int32, (tokens, 1), 0) + blk * tokens
     chosen = jnp.zeros((tokens, 1), F32)
@@ -625,7 +583,7 @@
     grad = gnorm[...]
     sums[2:3, :] = jnp.sum(grad * unit[...], axis=0, keepdims=True)
     sums[3:4, :] = jnp.sum(grad, axis=0, keepdims=True)
-    made = gg[x, z].astype(F32) + norm_back(grad * gain2_ref[...], unit[...], scale2)
+    made = gg[x, z].astype(F32) + norm_back(grad * as_row(gain2_ref), unit[...], scale2)
     residual[...] = made
     grow[y, piece(c, tokens), :] = made.astype(BF16)
     row = RowGather(grow, tokens, y, c, sibling, ypeer, gsend, grecv)
@@ -645,6 +603,9 @@
     normed.forward(3)
     row.forward()
     make(x)
+    row_att.arrive()
+    for b in range(4):
+        aturned_ref[:, b * tokens : (b + 1) * tokens] = arow[b // 2, (b % 2) * tokens : (b % 2 + 1) * tokens, :].T
     row.arrive()
 
     @pl.loop(0, pairs)
@@ -747,6 +708,7 @@
         @pl.when(j == 0)
         def _():
             normed.arrive()
+            grads.arrive()
             make(1 - x)
 
             @pl.loop(0, 2)
@@ -791,7 +753,7 @@
         for r, target in others:
             to_low(j, r, target).wait_send()
 
-    for r, target, count in ((1, sibling, 2 + c), (2, ypeer, pairs), (3, diag, 2 + c)):
+    for r, target, count in received:
 
         @pl.loop(0, count)
         def _(j):
@@ -840,7 +802,7 @@
             slab_in[dp] = slab[dp]
 
     grad = gnorm[...]
-    made, scale1 = centered(tok_ref[...].astype(F32))
+    made, scale1 = centered(rows_all[y, piece(c, tokens), :].astype(F32))
     sums[0:1, :] = jnp.sum(grad * made, axis=0, keepdims=True)
     sums[1:2, :] = jnp.sum(grad, axis=0, keepdims=True)
     sbuf[...] = jnp.zeros_like(sbuf)
@@ -852,7 +814,9 @@
         to_u.append(remote(sbuf.at[target], sbox.at[dp], usend.at[k], urecv.at[k], (target, blk)))
         to_u[-1].start()
     sbox[dp] = sbuf[dp]
-    tgrad_ref[...] = (residual[...] + norm_back(grad * gain1_ref[...], made, scale1)).astype(BF16)
+    tgrad_ref[...] = (residual[...] + norm_back(grad * as_row(gain1_ref), made, scale1)).astype(BF16)
+    outs.append(pltpu.make_async_copy(tgrad_ref, tgrad_out, outsem.at[1]))
+    outs[-1].start()
     add_z(pairs - 1)
     for copy in to_u:
         copy.wait()
@@ -862,21 +826,29 @@
         copy.start()
     to_y[1].wait()
     down_ref[...] = part_dn[mine].astype(F32) + sib_dn[y].astype(F32) + yrecv_dn[...].astype(F32)
+    outs.append(pltpu.make_async_copy(down_ref, down_out, outsem.at[2]))
+    outs[-1].start()
     for copy in to_q:
         copy.wait()
     for s in range(8):
         in_ref[:, s * cut : (s + 1) * cut] = slab_in[s].astype(F32)
+    outs.append(pltpu.make_async_copy(in_ref, in_out, outsem.at[3]))
+    outs[-1].start()
     add_z(pairs)
     for copy in to_t:
         copy.wait()
-    sums_ref[...] = (tbox[0] + tbox[1]) + (tbox[2] + tbox[3])
+    total = (tbox[0] + tbox[1]) + (tbox[2] + tbox[3])
+    for b in range(4):
+        @pl.when(blk == b)
+        def _():
+            sums_ref[...] = total[:, b * rows : (b + 1) * rows]
 
     @pl.loop(0, pairs + 1)
     def _(s):
         for r, target in others:
             to_blk(s, r, target).wait_send()
 
-    for r, target, count in ((1, sibling, 2 + c), (2, ypeer, pairs), (3, diag, 2 + c)):
+    for r, target, count in received:
 
         @pl.loop(0, count + 1)
         def _(s):
@@ -892,11 +864,57 @@
                 for t in range(3):
                     at = t * width + 128 * (p + j)
                     gqkv_ref[:, at : at + 128] = fin[slot, j + 1, :, 128 * t : 128 * t + 128]
-    row.drain()
-    normed.drain()
-
-
-def rest(cls_positions, tokens, own, qkv, att, turned, aturned, grads, gain1, gain2, shift2, w_out, w_in, w_down, w_qkv):
+    outs.append(pltpu.make_async_copy(gqkv_ref, gqkv_out, outsem.at[4]))
+    outs[-1].start()
+    outs.append(pltpu.make_async_copy(gout_ref, gout_out, outsem.at[5]))
+    outs[-1].start()
+
+    @pl.loop(0, pairs)
+    def _(j):
+        for r, target in others:
+            to_own(j, r, target).wait_send()
+
+    for gather in (row_tok, row_att, row, grads, normed):
+        gather.drain()
+    for copy in outs:
+        copy.wait()
+
+
+def finish_kernel(cells, sums_ref, *refs):
+    count = 6
+    arrays, (mean_ref, variance_ref, *grads), outs = refs[:count], refs[count : count + 6], refs[count + 6 : 2 * count + 6]
+    held, isem, osem = refs[2 * count + 6 : -2], refs[-2], refs[-1]
+    loads = [pltpu.make_async_copy(arrays[i], held[i], isem.at[i]) for i in range(count)]
+    stores = [pltpu.make_async_copy(held[i], outs[i], osem.at[i]) for i in range(count)]
+    for load in loads:
+        load.start()
+    for load, store in zip(loads, stores):
+        load.wait()
+        store.start()
+    mean = sums_ref[4:5, :] / cells
+    mean_ref[...] = mean
+    variance_ref[...] = sums_ref[5:6, :] / cells - mean * mean
+    for i in range(4):
+        grads[i][...] = sums_ref[i : i + 1, :]
+    for store in stores:
+        store.wait()
+
+
+def finish(cells, sums, *arrays):
+    anywhere, v = pl.BlockSpec(memory_space=pl.ANY), pl.BlockSpec(memory_space=pltpu.VMEM)
+    count = len(arrays)
+    small = jax.ShapeDtypeStruct((1, sums.shape[1]), F32)
+    return pl.pallas_call(
+        functools.partial(finish_kernel, cells),
+        out_shape=(small,) * 6 + tuple(jax.ShapeDtypeStruct(a.shape, a.dtype) for a in arrays),
+        in_specs=[v] + [anywhere] * count,
+        out_specs=(v,) * 6 + (anywhere,) * count,
+        scratch_shapes=[pltpu.VMEM(a.shape, a.dtype) for a in arrays]
+        + [pltpu.SemaphoreType.DMA((count,)), pltpu.SemaphoreType.DMA((count,))],
+    )(sums, *arrays)
+
+
+def whole_layer(cls_positions, tokens, grad, gain1, shift1, gain2, shift2, w_qkv, w_out, w_in, w_down):
     count, width = tokens.shape
     inner = w_in.shape[1]
     row_len, share = 4 * count, width // 8
@@ -904,8 +922,9 @@
     block, depth = 512, 3
     v = pltpu.VMEM
     dma = pltpu.SemaphoreType.DMA
+    anywhere = pl.BlockSpec(memory_space=pl.ANY)
     return pl.pallas_call(
-        rest_kernel,
+        layer_kernel,
         out_shape=(
             jax.ShapeDtypeStruct((count, width), BF16),
             jax.ShapeDtypeStruct((count, width), BF16),
@@ -913,13 +932,19 @@
             jax.ShapeDtypeStruct((rows, width), F32),
             jax.ShapeDtypeStruct((rows, inner), F32),
             jax.ShapeDtypeStruct((owned, width), F32),
-            jax.ShapeDtypeStruct((8, 256), F32),
+            jax.ShapeDtypeStruct((8, rows), F32),
         ),
         in_specs=[pl.BlockSpec(memory_space=pltpu.SMEM)]
-        + [pl.BlockSpec(memory_space=v)] * 10
-        + [pl.BlockSpec(memory_space=pl.ANY)] * 4,
-        out_specs=(pl.BlockSpec(memory_space=v),) * 7,
+        + [anywhere] * 2
+        + [pl.BlockSpec(memory_space=v)] * 4
+        + [anywhere] * 4,
+        out_specs=(anywhere,) * 6 + (pl.BlockSpec(memory_space=v),),
         scratch_shapes=[
+            v((2, 4, count, width), BF16), v((2, 2 * count, width), BF16),
+            v((3, row_len, 384), BF16), v((3, row_len, 128), F32), v((width, row_len), BF16), v((width, row_len), BF16),
+            v((3, row_len, 128), BF16), v((4, 3, count, 128), BF16), v((2, 2 * count, width), BF16),
+            v((count, width), BF16), v((count, width), BF16), v((rows, 3 * width), F32), v((rows, width), F32),
+            v((rows, inner), F32), v((owned, width), F32),
             v((depth, width, block), BF16), v((depth, block, width), BF16),
             v((width, cut), BF16), v((cut, width), BF16), v((3, 128, width), BF16),
             v((2, 4, count, width), BF16), v((8 * count, cut), BF16), v((cut, 8 * count), BF16),
@@ -934,14 +959,16 @@
             v((4, 3, share, 384), BF16), v((4, 4, share // 4, 384), F32), v((4, 4, share // 4, 384), F32),
             v((4, 3, count, 384), BF16),
             v((8, width), F32), v((8, 8, 256), F32), v((8, 8, 256), F32), v((4, 8, 256), F32),
+            dma((2,)), dma((3, 3)), dma((3,)), dma((3,)), dma((3, 4)), dma((2, 4)), dma((4, 3)), dma((4, 3)),
+            dma((3,)), dma((3,)), dma((6,)),
             dma((2 + 3 * depth,)), dma((2, depth)), dma((3,)), dma((3,)), dma((3,)), dma((3, 4)), dma((2, 4)),
             dma((2, 2)), dma((2, 2)), dma((2,)), dma((2,)), dma((8,)), dma((8,)),
             dma((4,)), dma((4,)), dma((4, 3)), dma((4, 3)), dma((4, 4)), dma((4, 4)), dma((4, 3)), dma((4, 3)),
             dma((8,)), dma((8,)), dma((4,)), dma((4,)),
         ],
-        compiler_params=pltpu.CompilerParams(collective_id=2, has_side_effects=True, vmem_limit_bytes=64 * 2**20),
+        compiler_params=pltpu.CompilerParams(collective_id=1, has_side_effects=True, vmem_limit_bytes=64 * 2**20),
         cost_estimate=pl.CostEstimate(flops=40 * 2**30, bytes_accessed=50 * 2**20, transcendentals=0),
-    )(cls_positions, tokens, own, qkv, att, turned, aturned, grads, gain1, gain2, shift2, w_out, w_in, w_down, w_qkv)
+    )(cls_positions, tokens, grad, gain1, shift1, gain2, shift2, w_qkv, w_out, w_in, w_down)
 
 
 def on_device(
@@ -959,31 +986,22 @@
     out_grad,
 ):
     tokens, out_grad = tokens[0], out_grad[0]
-    turned, qkv, att, aturned, own, grads = attend(
-        cls_positions, tokens, out_grad, first_gain[None], first_shift[None], w_qkv
-    )
-    layer, tokens_grad, grad_qkv, grad_out, grad_in, grad_down, sums = rest(
-        cls_positions, tokens, own, qkv, att, turned, aturned, grads,
-        first_gain[None], second_gain[None], second_shift[None], w_out, w_in, w_down, w_qkv,
-    )
-    count = cls_positions.shape[0] * cls_positions.shape[1] * lax.axis_size("dp")
-    share = tokens.shape[1] // (lax.axis_size("dp") * lax.axis_size("blk"))
-    mine = lax.dynamic_slice_in_dim(sums, lax.axis_index("blk") * share, share, axis=1)
-    cls_mean = mine[4] / count
-    cls_variance = mine[5] / count - cls_mean * cls_mean
+    layer, tokens_grad, grad_qkv, grad_out, grad_in, grad_down, sums = whole_layer(
+        cls_positions, tokens, out_grad, first_gain, first_shift, second_gain, second_shift, w_qkv, w_out, w_in, w_down
+    )
+    mean, variance, gain1_grad, shift1_grad, gain2_grad, shift2_grad, *large = finish(
+        cls_positions.size * lax.axis_size("dp"), sums, layer, tokens_grad, grad_qkv, grad_out, grad_in, grad_down
+    )
     return (
-        layer[None],
-        tokens_grad[None],
-        grad_qkv,
-        grad_out,
-        grad_in,
-        grad_down,
-        mine[0],
-        mine[1],
-        mine[2],
-        mine[3],
-        cls_mean,
-        cls_variance,
+        large[0][None],
+        large[1][None],
+        *large[2:],
+        gain1_grad[0],
+        shift1_grad[0],
+        gain2_grad[0],
+        shift2_grad[0],
+        mean[0],
+        variance[0],
     )
 
 

time: 183 us -> 153 us (0.84)
  local copies, waits for them, and re-layouts: 20.2 us -> 0 us
  Pallas kernels: 160 us -> 152 us
    unnamed x32 -> x0, local copies, waits for them, and re-layouts: 16.2 us -> none
    pallas_call x2, Pallas kernels: 160 us -> 152 us  [the longest x1 148 us: whole_layer(): pl.pallas_call(layer_kernel, out_shape=(jax.ShapeDtypeStruct((count, widt...]
    broadcast_in_dim x4 -> x0, local copies, waits for them, and re-layouts: 2.6 us -> none  [the longest x1 0.7 us: on_device(): first_shift[None]]
where the time goes in v4:
time: 153 us
  Pallas kernels  152 us (99%)
    pallas_call x1, Pallas kernels, whole_layer(): pl.pallas_call(layer_kernel, out_shape=(jax.ShapeDtypeStruct((count, widt...  148 us
    pallas_call x1, Pallas kernels, finish(): pl.pallas_call(functools.partial(finish_kernel, cells), out_shape=(small,...  4.07 us

profile of v4, /device:TPU:0, one launch (start us, length us, event | category | flops | bytes accessed | tf_op | source)
XLA Modules:
  0.0 152.6 jit_solution(11243284197893075397)
XLA Ops:
  0.6 147.7 %shard_map.202 = (bf16[128,1280]{1,0:T(8,128)(2,1)}, bf16[128,1280]{1,0:T(8,128)(2,1)}, f32[40,3840]{1,0:T(8,128)}, f32[40,1280]{1,0:T(8,128)}, f32[40,5120]{1,0...) custom-call(s32[1,4]{1,0:T(1,128)} %cls_ref.1, bf16[128,1280]{1,0:T(8,128)(2,1)} %bitcast.10, ...), custom_call_target="tpu_custom_call" | custom-call | flops 42949672960 | bytes 52428800 | tf_op jit(solution)/shard_map/pallas_call | solution.py:926
  148.3 4.1 %shard_map.203 = (f32[1,40]{1,0:T(1,128)}, f32[1,40]{1,0:T(1,128)}, f32[1,40]{1,0:T(1,128)}, f32[1,40]{1,0:T(1,128)}, f32[1,40]{1,0:T(1,128)}, /*index=5*/f32[1,...) custom-call(f32[8,40]{1,0:T(8,128)} %get-tuple-element.31.sums_ref, ...), custom_call_target="tpu_custom_call" | custom-call | tf_op jit(solution)/shard_map/pallas_call | solution.py:907

commit v5 on v4

--- a/solution.py
+++ b/solution.py
@@ -320,10 +320,11 @@
             self.down(above)
             self.hop(2, above).start()
 
-    def arrive(self):
-        for zz in range(4):
-            slot = self.slots.at[1 - self.x, zz]
-            remote(slot, slot, self.send.at[2, zz], self.recv.at[1 - self.x, zz], self.targets[2]).wait_recv()
+    def arrive(self, half):
+        for k in range(2):
+            slot = self.slots.at[1 - self.x, 2 * half + k]
+            done = self.recv.at[1 - self.x, 2 * half + k]
+            remote(slot, slot, self.send.at[2, k], done, self.targets[2]).wait_recv()
 
     def drain(self):
         for zz in range(4):
@@ -384,7 +385,7 @@
     gg, rows_all, qkv_ref, att_ref, turned_ref, aturned_ref, attlow, abox, arow,
     layer_ref, tgrad_ref, gqkv_ref, gout_ref, in_ref, down_ref,
     st_in, st_dn, wi, wd, wo, gx, gp, ht, part_in, part_dn, sib_in, sib_dn, ysend_in, ysend_dn, yrecv_in, yrecv_dn,
-    slab, slab_in, residual, unit, gnorm, grow, gatt, low, keys, values, part, xin, zout, zin, full, fin, landing,
+    slab, slab_in, residual, unit, gnorm, grow, gatt, low, keys, values, part, xin, zout, zin, zlast, zfirst, hfirst, xfirst, full, fin, landing,
     sums, sbuf, sbox, tbox,
     isem, lsem, rsend, rrecv, ogsend, ogrecv, bsend, brecv, arsend, arrecv, outsem,
     wsem, ssem, osem, gsend, grecv, dsend, drecv, sibs, sibr, ysend, yrecv, qsend, qrecv,
@@ -401,7 +402,6 @@
     depth = st_in.shape[0]
     sibling, ypeer, diag = (dp, 2 * y + 1 - c), (dp, 2 * (1 - y) + c), (dp, 2 * (1 - y) + 1 - c)
     xpeer = (2 * z + 1 - x, blk)
-    zpeers = [(2 * lax.rem(z + k, 4) + x, blk) for k in range(1, 4)]
     others = ((1, sibling), (2, ypeer), (3, diag))
     received = ((1, sibling, 2 + c), (2, ypeer, pairs), (3, diag, 2 + c))
 
@@ -502,7 +502,10 @@
             to_own(j, r, target).start()
         abox[0, j] = attlow[j, piece(blk, tokens), :]
 
-    grads.forward(2)
+        @pl.when(j == 1)
+        def _():
+            grads.forward(2)
+
     for b in range(4):
         at = slice(b * tokens, (b + 1) * tokens)
         turned_ref[:, at] = normed_rows[at, :].T
@@ -552,7 +555,7 @@
         residual[...] += mm((pre * cdf).astype(BF16), st_dn[slot])
         gnorm[...] += mm(grad, st_in[slot], NT)
 
-        @pl.when(i == 1)
+        @pl.when(i == 0)
         def _():
             grads.forward(3)
 
@@ -591,21 +594,26 @@
     load_in.wait()
     load_dn.wait()
 
-    def make(xx):
-        @pl.loop(0, 2)
-        def _(half):
-            at = piece(2 * xx + half, both)
-            pre = mm(gx[xx, piece(half, 2)].reshape(both, width), wi[...])
-            cdf, slope = gelu_parts(pre)
-            ht[:, at] = (pre * cdf).astype(BF16).T
-            gp[at, :] = (mm(gg[xx, piece(half, 2)].reshape(both, width), wd[...], NT) * slope).astype(BF16)
-
-    normed.forward(3)
-    row.forward()
-    make(x)
+    near = z // 2
+
+    def make(xx, half):
+        at = piece(2 * xx + half, both)
+        pre = mm(gx[xx, piece(half, 2)].reshape(both, width), wi[...])
+        cdf, slope = gelu_parts(pre)
+        ht[:, at] = (pre * cdf).astype(BF16).T
+        gp[at, :] = (mm(gg[xx, piece(half, 2)].reshape(both, width), wd[...], NT) * slope).astype(BF16)
+
+    def makes(first_step, last_step):
+        @pl.loop(first_step, last_step)
+        def _(step):
+            make(flip(x, lax.rem(step, 2)), flip(near, step // 2))
+
+    makes(0, 1)
     row_att.arrive()
     for b in range(4):
         aturned_ref[:, b * tokens : (b + 1) * tokens] = arow[b // 2, (b % 2) * tokens : (b % 2 + 1) * tokens, :].T
+    row.forward()
+    normed.forward(3)
     row.arrive()
 
     @pl.loop(0, pairs)
@@ -613,12 +621,21 @@
         load_rows(j).wait()
         gatt[j] = mm(grow[...].reshape(row_len, width), wo[j], NT)
 
+    even, pair_z, half_z = lax.rem(z, 2), z + 1 - 2 * lax.rem(z, 2), lax.rem(z + 2, 4)
+
     def to_x(s):
-        return remote(part.at[s, 1 - x], xin.at[s], xsend.at[s], xrecv.at[s], xpeer)
-
-    def to_z(s, k):
-        target = lax.rem(z + k, 4)
-        return remote(zout.at[s, target], zin.at[s, k - 1], zsend.at[s, k - 1], zrecv.at[s, k - 1], zpeers[k - 1])
+        return remote(part.at[s, 1 - x], xin.at[s - 1], xsend.at[s], xrecv.at[s], xpeer)
+
+    def to_pair(s):
+        return remote(zout.at[s - 1, 1 - even], zin.at[s - 1], zsend.at[s, 0], zrecv.at[s, 0], (2 * pair_z + x, blk))
+
+    def to_half(s):
+        return remote(zlast.at[s - 1, 0], zlast.at[s - 1, 1], zsend.at[s, 1], zrecv.at[s, 1], (2 * half_z + x, blk))
+
+    other_half, my_half = 1 - z // 2, z // 2
+    first_pair = remote(part.at[0, :, 1 - even], zfirst, zsend.at[0, 0], zrecv.at[0, 0], (2 * pair_z + x, blk))
+    first_half = remote(hfirst.at[0], hfirst.at[1], zsend.at[0, 1], zrecv.at[0, 1], (2 * half_z + x, blk))
+    first_x = remote(xfirst.at[0], xfirst.at[1], xsend.at[0], xrecv.at[0], xpeer)
 
     def to_blk(s, r, target):
         return remote(full.at[s, target[1]], fin.at[r, s], fsend.at[r, s], frecv.at[r, s], target)
@@ -629,28 +646,52 @@
     def add_x(s):
         to_x(s).wait()
         for k in range(4):
-            zout[s, k] = (part[s, x, k].astype(F32) + xin[s, k].astype(F32)).astype(BF16)
-        for k in range(1, 4):
-            to_z(s, k).start()
-
-    def add_z(s):
-        for k in range(1, 4):
-            to_z(s, k).wait()
-        total = zout[s, z].astype(F32)
-        for k in range(3):
-            total = total + zin[s, k].astype(F32)
+            zout[s - 1, k // 2, k % 2] = (part[s, x, k // 2, k % 2].astype(F32) + xin[s - 1, k // 2, k % 2].astype(F32)).astype(BF16)
+        to_pair(s).start()
+
+    def add_pair(s):
+        to_pair(s).wait()
+        away = 1 - z // 2
+        zlast[s - 1, 0] = (zout[s - 1, even, away].astype(F32) + zin[s - 1, away].astype(F32)).astype(BF16)
+        to_half(s).start()
+
+    def add_half(s):
+        to_half(s).wait()
+        mine = z // 2
+        total = zout[s - 1, even, mine].astype(F32) + zin[s - 1, mine].astype(F32) + zlast[s - 1, 1].astype(F32)
+        to_owners(s, total)
+
+    def to_owners(s, total):
         for b in range(4):
             full[s, b] = total[b * rows : (b + 1) * rows]
         for r, target in others:
             to_blk(s, r, target).start()
         fin[0, s] = full[s, blk]
 
+    def first_a():
+        first_pair.wait()
+        for xx in range(2):
+            hfirst[0, xx] = (part[0, xx, even, other_half].astype(F32) + zfirst[xx, other_half].astype(F32)).astype(BF16)
+        first_half.start()
+
+    def first_sum(xx):
+        return part[0, xx, even, my_half].astype(F32) + zfirst[xx, my_half].astype(F32) + hfirst[1, xx].astype(F32)
+
+    def first_b():
+        first_half.wait()
+        xfirst[0] = first_sum(1 - x).astype(BF16)
+        first_x.start()
+
+    def first_c():
+        first_x.wait()
+        to_owners(0, first_sum(x) + xfirst[1].astype(F32))
+
     def weight_part(s, left, right):
         @pl.loop(0, 4)
         def _(zz):
             made = mm(left[piece(zz, 2 * share), :], right)
-            part[s, 0, zz] = made[:share].astype(BF16)
-            part[s, 1, zz] = made[share:].astype(BF16)
+            part[s, 0, lax.rem(zz, 2), zz // 2] = made[:share].astype(BF16)
+            part[s, 1, lax.rem(zz, 2), zz // 2] = made[share:].astype(BF16)
 
     @pl.when(c == 0)
     def _():
@@ -661,8 +702,7 @@
         right = grow[:, :, pl.ds(pl.multiple_of(first * 128, 128), 256)].reshape(row_len, 256)
         weight_part(0, aturned_ref, jnp.concatenate([right, jnp.zeros((row_len, 128), BF16)], axis=1))
 
-    to_x(0).start()
-
+    first_pair.start()
     to_sibling = []
     for kind, source, box in ((0, part_in, sib_in), (1, part_dn, sib_dn)):
         for yy in range(2):
@@ -672,6 +712,8 @@
         remote(ysend_in, yrecv_in, ysend.at[0], yrecv.at[0], ypeer),
         remote(ysend_dn, yrecv_dn, ysend.at[1], yrecv.at[1], ypeer),
     )
+
+    over = 2 * (1 - y) + c
 
     @pl.loop(0, pairs)
     def _(j):
@@ -705,11 +747,18 @@
         weight_part(j + 1, turned_ref, low[j])
         to_x(j + 1).start()
 
-        @pl.when(j == 0)
-        def _():
-            normed.arrive()
-            grads.arrive()
-            make(1 - x)
+        @pl.when(j == 2)
+        def _():
+            add_pair(1)
+            first_c()
+
+        @pl.when(j == 1)
+        def _():
+            for half in range(2):
+                normed.arrive(half)
+                grads.arrive(half)
+            makes(1, 4)
+            first_a()
 
             @pl.loop(0, 2)
             def _(half):
@@ -730,22 +779,37 @@
 
             to_sibling[2].start()
             to_sibling[3].start()
-
-        add_x(j)
-
-        @pl.when(j > 0)
-        def _():
-            add_z(j - 1)
-
-        @pl.when(j == 1)
-        def _():
-            for copy in to_sibling:
-                copy.wait()
-            over = 2 * (1 - y) + c
+            to_sibling[0].wait()
+            to_sibling[1].wait()
             ysend_in[...] = (part_in[over].astype(F32) + sib_in[1 - y].astype(F32)).astype(BF16)
             to_y[0].start()
+            to_sibling[2].wait()
+            to_sibling[3].wait()
             ysend_dn[...] = (part_dn[over].astype(F32) + sib_dn[1 - y].astype(F32)).astype(BF16)
-            to_y[1].start()
+            first_b()
+            add_x(1)
+
+    @pl.when(c == 1)
+    def _():
+        add_pair(1)
+        first_c()
+
+    mine = 2 * y + c
+    to_q = []
+    for k in range(1, 8):
+        target = lax.rem(dp + k, 8)
+        to_q.append(remote(slab.at[target], slab_in.at[dp], qsend.at[k], qrecv.at[k], (target, blk)))
+
+    def start_q():
+        to_y[0].wait()
+        to_y[1].start()
+        total = part_in[mine].astype(F32) + sib_in[y].astype(F32) + yrecv_in[...].astype(F32)
+        slab[...] = total.astype(BF16)
+        for copy in to_q:
+            copy.start()
+        slab_in[dp] = slab[dp]
+
+    start_q()
 
     @pl.loop(0, pairs)
     def _(j):
@@ -768,11 +832,7 @@
         for t in range(3):
             stream_qkv(p, t).start()
     gnorm[...] = jnp.zeros_like(gnorm)
-    mine = 2 * y + c
-    to_q = []
-    for k in range(1, 8):
-        target = lax.rem(dp + k, 8)
-        to_q.append(remote(slab.at[target], slab_in.at[dp], qsend.at[k], qrecv.at[k], (target, blk)))
+    add_x(2)
 
     @pl.loop(0, 10)
     def _(p):
@@ -787,19 +847,6 @@
         cc = pp // 3
         slot = 2 * flip(y, yy) + flip(c, cc)
         gnorm[...] += mm(landing[slot, pp - 3 * cc], st_in[lax.rem(p, depth), :, 0:384], NT)
-
-        @pl.when(p == 3)
-        def _():
-            add_x(pairs)
-
-        @pl.when(p == 6)
-        def _():
-            to_y[0].wait()
-            total = part_in[mine].astype(F32) + sib_in[y].astype(F32) + yrecv_in[...].astype(F32)
-            slab[...] = total.astype(BF16)
-            for copy in to_q:
-                copy.start()
-            slab_in[dp] = slab[dp]
 
     grad = gnorm[...]
     made, scale1 = centered(rows_all[y, piece(c, tokens), :].astype(F32))
@@ -817,31 +864,61 @@
     tgrad_ref[...] = (residual[...] + norm_back(grad * as_row(gain1_ref), made, scale1)).astype(BF16)
     outs.append(pltpu.make_async_copy(tgrad_ref, tgrad_out, outsem.at[1]))
     outs[-1].start()
-    add_z(pairs - 1)
-    for copy in to_u:
-        copy.wait()
-    tbox[0] = jnp.sum(sbox[...], axis=0)
+
+    def end_down():
+        to_y[1].wait()
+        down_ref[...] = part_dn[mine].astype(F32) + sib_dn[y].astype(F32) + yrecv_dn[...].astype(F32)
+        outs.append(pltpu.make_async_copy(down_ref, down_out, outsem.at[2]))
+        outs[-1].start()
+
+    def end_q():
+        for copy in to_q:
+            copy.wait()
+        for s in range(8):
+            in_ref[:, s * cut : (s + 1) * cut] = slab_in[s].astype(F32)
+        outs.append(pltpu.make_async_copy(in_ref, in_out, outsem.at[3]))
+        outs[-1].start()
+
     to_t = [remote(tbox.at[0], tbox.at[r], tsend.at[r], trecv.at[r], target) for r, target in others]
-    for copy in to_t:
-        copy.start()
-    to_y[1].wait()
-    down_ref[...] = part_dn[mine].astype(F32) + sib_dn[y].astype(F32) + yrecv_dn[...].astype(F32)
-    outs.append(pltpu.make_async_copy(down_ref, down_out, outsem.at[2]))
-    outs[-1].start()
-    for copy in to_q:
-        copy.wait()
-    for s in range(8):
-        in_ref[:, s * cut : (s + 1) * cut] = slab_in[s].astype(F32)
-    outs.append(pltpu.make_async_copy(in_ref, in_out, outsem.at[3]))
-    outs[-1].start()
-    add_z(pairs)
-    for copy in to_t:
-        copy.wait()
-    total = (tbox[0] + tbox[1]) + (tbox[2] + tbox[3])
-    for b in range(4):
-        @pl.when(blk == b)
-        def _():
-            sums_ref[...] = total[:, b * rows : (b + 1) * rows]
+
+    def start_t():
+        for copy in to_u:
+            copy.wait()
+        tbox[0] = jnp.sum(sbox[...], axis=0)
+        for copy in to_t:
+            copy.start()
+
+    def end_t():
+        for copy in to_t:
+            copy.wait()
+        total = (tbox[0] + tbox[1]) + (tbox[2] + tbox[3])
+        for b in range(4):
+
+            @pl.when(blk == b)
+            def _():
+                sums_ref[...] = total[:, b * rows : (b + 1) * rows]
+
+    add_pair(2)
+
+    @pl.when(c == 0)
+    def _():
+        add_x(3)
+
+    add_half(1)
+    start_t()
+
+    @pl.when(c == 0)
+    def _():
+        add_pair(3)
+
+    add_half(2)
+    end_down()
+    end_t()
+    end_q()
+
+    @pl.when(c == 0)
+    def _():
+        add_half(3)
 
     @pl.loop(0, pairs + 1)
     def _(s):
@@ -955,8 +1032,10 @@
             v((count, width), F32), v((count, width), F32), v((count, width), F32),
             v((2, 2 * count, width), BF16), v((3, row_len, 128), F32), v((3, row_len, 384), BF16),
             v((row_len, 128), F32), v((row_len, 128), F32),
-            v((4, 2, 4, share, 384), BF16), v((4, 4, share, 384), BF16), v((4, 4, share, 384), BF16),
-            v((4, 3, share, 384), BF16), v((4, 4, share // 4, 384), F32), v((4, 4, share // 4, 384), F32),
+            v((4, 2, 2, 2, share, 384), BF16), v((3, 2, 2, share, 384), BF16), v((3, 2, 2, share, 384), BF16),
+            v((3, 2, share, 384), BF16), v((3, 2, share, 384), BF16),
+            v((2, 2, share, 384), BF16), v((2, 2, share, 384), BF16), v((2, share, 384), BF16),
+            v((4, 4, share // 4, 384), F32), v((4, 4, share // 4, 384), F32),
             v((4, 3, count, 384), BF16),
             v((8, width), F32), v((8, 8, 256), F32), v((8, 8, 256), F32), v((4, 8, 256), F32),
             dma((2,)), dma((3, 3)), dma((3,)), dma((3,)), dma((3, 4)), dma((2, 4)), dma((4, 3)), dma((4, 3)),

time: 153 us -> 137 us (0.90)
  Pallas kernels: 152 us -> 136 us
    pallas_call x1, Pallas kernels: 148 us -> 132 us  [whole_layer(): pl.pallas_call(layer_kernel, out_shape=(jax.ShapeDtypeStruct((count, widt...]
where the time goes in v5:
time: 137 us
  Pallas kernels  136 us (99%)
    pallas_call x1, Pallas kernels, whole_layer(): pl.pallas_call(layer_kernel, out_shape=(jax.ShapeDtypeStruct((count, widt...  132 us
    pallas_call x1, Pallas kernels, finish(): pl.pallas_call(functools.partial(finish_kernel, cells), out_shape=(small,...  4.07 us

profile of v5, /device:TPU:0, one launch (start us, length us, event | category | flops | bytes accessed | tf_op | source)
XLA Modules:
  0.0 137.0 jit_solution(15088082706095805644)
XLA Ops:
  0.6 132.1 %shard_map.202 = (bf16[128,1280]{1,0:T(8,128)(2,1)}, bf16[128,1280]{1,0:T(8,128)(2,1)}, f32[40,3840]{1,0:T(8,128)}, f32[40,1280]{1,0:T(8,128)}, f32[40,5120]{1,0...) custom-call(s32[1,4]{1,0:T(1,128)} %cls_ref.1, bf16[128,1280]{1,0:T(8,128)(2,1)} %bitcast.10, ...), custom_call_target="tpu_custom_call" | custom-call | flops 42949672960 | bytes 52428800 | tf_op jit(solution)/shard_map/pallas_call | solution.py:1003
  132.8 4.1 %shard_map.203 = (f32[1,40]{1,0:T(1,128)}, f32[1,40]{1,0:T(1,128)}, f32[1,40]{1,0:T(1,128)}, f32[1,40]{1,0:T(1,128)}, f32[1,40]{1,0:T(1,128)}, /*index=5*/f32[1,...) custom-call(f32[8,40]{1,0:T(8,128)} %get-tuple-element.31.sums_ref, ...), custom_call_target="tpu_custom_call" | custom-call | tf_op jit(solution)/shard_map/pallas_call | solution.py:984

commit v6 on v5

--- a/solution.py
+++ b/solution.py
@@ -555,18 +555,14 @@
         residual[...] += mm((pre * cdf).astype(BF16), st_dn[slot])
         gnorm[...] += mm(grad, st_in[slot], NT)
 
-        @pl.when(i == 0)
+        @pl.when(i == 2)
         def _():
             grads.forward(3)
 
-        @pl.when(i == 4)
+        @pl.when(i == 6)
         def _():
             row_att.forward()
             normed.forward(1)
-
-        @pl.when(i == 8)
-        def _():
-            normed.forward(2)
 
     load_in = pltpu.make_async_copy(win_ref.at[:, piece(dp, cut)], wi, wsem.at[0])
     load_dn = pltpu.make_async_copy(wdown_ref.at[piece(dp, cut), :], wd, wsem.at[1])
@@ -591,9 +587,18 @@
     grow[y, piece(c, tokens), :] = made.astype(BF16)
     row = RowGather(grow, tokens, y, c, sibling, ypeer, gsend, grecv)
     row.start()
+    normed.forward(2)
     load_in.wait()
     load_dn.wait()
 
+    def stream_qkv(p, t):
+        slot = lax.rem(p, depth)
+        source = wqkv_ref.at[:, pl.ds(pl.multiple_of(t * width + p * 128, 128), 128)]
+        return pltpu.make_async_copy(source, st_in.at[slot, :, pl.ds(t * 128, 128)], wsem.at[2 + 3 * slot + t])
+
+    for p in range(depth):
+        for t in range(3):
+            stream_qkv(p, t).start()
     near = z // 2
 
     def make(xx, half):
@@ -613,7 +618,6 @@
     for b in range(4):
         aturned_ref[:, b * tokens : (b + 1) * tokens] = arow[b // 2, (b % 2) * tokens : (b % 2 + 1) * tokens, :].T
     row.forward()
-    normed.forward(3)
     row.arrive()
 
     @pl.loop(0, pairs)
@@ -703,6 +707,7 @@
         weight_part(0, aturned_ref, jnp.concatenate([right, jnp.zeros((row_len, 128), BF16)], axis=1))
 
     first_pair.start()
+    normed.forward(3)
     to_sibling = []
     for kind, source, box in ((0, part_in, sib_in), (1, part_dn, sib_dn)):
         for yy in range(2):
@@ -747,12 +752,7 @@
         weight_part(j + 1, turned_ref, low[j])
         to_x(j + 1).start()
 
-        @pl.when(j == 2)
-        def _():
-            add_pair(1)
-            first_c()
-
-        @pl.when(j == 1)
+        @pl.when(j == pairs - 1)
         def _():
             for half in range(2):
                 normed.arrive(half)
@@ -789,10 +789,8 @@
             first_b()
             add_x(1)
 
-    @pl.when(c == 1)
-    def _():
-        add_pair(1)
-        first_c()
+    add_x(2)
+    add_pair(1)
 
     mine = 2 * y + c
     to_q = []
@@ -810,6 +808,11 @@
         slab_in[dp] = slab[dp]
 
     start_q()
+    @pl.when(c == 0)
+    def _():
+        add_x(3)
+
+    first_c()
 
     @pl.loop(0, pairs)
     def _(j):
@@ -823,20 +826,10 @@
         def _(j):
             to_low(j, r, target).wait_recv()
 
-    def stream_qkv(p, t):
-        slot = lax.rem(p, depth)
-        source = wqkv_ref.at[:, pl.ds(pl.multiple_of(t * width + p * 128, 128), 128)]
-        return pltpu.make_async_copy(source, st_in.at[slot, :, pl.ds(t * 128, 128)], wsem.at[2 + 3 * slot + t])
-
-    for p in range(depth - 1):
-        for t in range(3):
-            stream_qkv(p, t).start()
     gnorm[...] = jnp.zeros_like(gnorm)
-    add_x(2)
-
     @pl.loop(0, 10)
     def _(p):
-        @pl.when(p + depth - 1 < 10)
+        @pl.when((p > 0) & (p + depth - 1 < 10))
         def _():
             for t in range(3):
                 stream_qkv(p + depth - 1, t).start()
@@ -899,26 +892,22 @@
                 sums_ref[...] = total[:, b * rows : (b + 1) * rows]
 
     add_pair(2)
-
-    @pl.when(c == 0)
-    def _():
-        add_x(3)
-
     add_half(1)
-    start_t()
 
     @pl.when(c == 0)
     def _():
         add_pair(3)
 
+    start_t()
     add_half(2)
+
+    @pl.when(c == 0)
+    def _():
+        add_half(3)
+
     end_down()
     end_t()
     end_q()
-
-    @pl.when(c == 0)
-    def _():
-        add_half(3)
 
     @pl.loop(0, pairs + 1)
     def _(s):

time: 137 us -> 128 us (0.934)
  Pallas kernels: 136 us -> 126 us
    pallas_call x1, Pallas kernels: 132 us -> 122 us  [whole_layer(): pl.pallas_call(layer_kernel, out_shape=(jax.ShapeDtypeStruct((count, widt...]
where the time goes in v6:
time: 128 us; the launch traced here: 127 us
  Pallas kernels  126 us (98%)
    pallas_call x1, Pallas kernels, whole_layer(): pl.pallas_call(layer_kernel, out_shape=(jax.ShapeDtypeStruct((count, widt...  122 us
    pallas_call x1, Pallas kernels, finish(): pl.pallas_call(functools.partial(finish_kernel, cells), out_shape=(small,...  4.07 us

profile of v6, /device:TPU:0, one launch (start us, length us, event | category | flops | bytes accessed | tf_op | source)
XLA Modules:
  0.0 127.2 jit_solution(5773351126145501850)
XLA Ops:
  0.6 122.3 %shard_map.202 = (bf16[128,1280]{1,0:T(8,128)(2,1)}, bf16[128,1280]{1,0:T(8,128)(2,1)}, f32[40,3840]{1,0:T(8,128)}, f32[40,1280]{1,0:T(8,128)}, f32[40,5120]{1,0...) custom-call(s32[1,4]{1,0:T(1,128)} %cls_ref.1, bf16[128,1280]{1,0:T(8,128)(2,1)} %bitcast.10, ...), custom_call_target="tpu_custom_call" | custom-call | flops 42949672960 | bytes 52428800 | tf_op jit(solution)/shard_map/pallas_call | solution.py:992
  123.0 4.1 %shard_map.203 = (f32[1,40]{1,0:T(1,128)}, f32[1,40]{1,0:T(1,128)}, f32[1,40]{1,0:T(1,128)}, f32[1,40]{1,0:T(1,128)}, f32[1,40]{1,0:T(1,128)}, /*index=5*/f32[1,...) custom-call(f32[8,40]{1,0:T(8,128)} %get-tuple-element.31.sums_ref, ...), custom_call_target="tpu_custom_call" | custom-call | tf_op jit(solution)/shard_map/pallas_call | solution.py:973

commit v7 on v6

--- a/solution.py
+++ b/solution.py
@@ -258,10 +258,11 @@
 
 
 class RowGather:
-    def __init__(self, rows, size, y, c, sibling, ypeer, send, recv):
+    def __init__(self, rows, size, y, c, sibling, ypeer, send, recv, source=None):
         near, far = rows.at[y, piece(c, size)], rows.at[1 - y, piece(c, size)]
-        self.core = remote(near, near, send.at[0], recv.at[0], sibling)
-        self.over = remote(near, near, send.at[1], recv.at[1], ypeer)
+        source = near if source is None else source
+        self.core = remote(source, near, send.at[0], recv.at[0], sibling)
+        self.over = remote(source, near, send.at[1], recv.at[1], ypeer)
         self.last = remote(far, far, send.at[2], recv.at[2], sibling)
 
     def start(self):
@@ -284,7 +285,8 @@
 class DpGather:
     def __init__(self, slots, z, x, blk, send, recv):
         self.slots, self.z, self.x, self.send, self.recv = slots, z, x, send, recv
-        self.targets = ((2 * (z + 1) + x, blk), (2 * (z - 1) + x, blk), (2 * z + 1 - x, blk))
+        above, below = lax.rem(z + 1, 4), lax.rem(z + 3, 4)
+        self.targets = ((2 * above + x, blk), (2 * below + x, blk), (2 * z + 1 - x, blk))
 
     def hop(self, kind, zz):
         slot = self.slots.at[self.x, zz]
@@ -438,10 +440,10 @@
         return pltpu.make_async_copy(wout_ref.at[piece(first + j, 128), :], wo.at[j], osem.at[j])
 
     greet([sibling, ypeer, diag] + [(lax.rem(dp + k, 8), blk) for k in range(1, 8)])
-    row_tok = RowGather(rows_all, tokens, y, c, sibling, ypeer, rsend, rrecv)
+    row_tok = RowGather(rows_all, tokens, y, c, sibling, ypeer, rsend, rrecv, tok_hbm)
     grads = DpGather(gg, z, x, blk, ogsend, ogrecv)
+    row_tok.start()
     tok_in.wait()
-    row_tok.start()
     grad_in.wait()
     grads.start()
     for i, size in tails:
@@ -667,7 +669,7 @@
 
     def to_owners(s, total):
         for b in range(4):
-            full[s, b] = total[b * rows : (b + 1) * rows]
+            full[s, b] = total[b * rows : (b + 1) * rows].astype(BF16)
         for r, target in others:
             to_blk(s, r, target).start()
         fin[0, s] = full[s, blk]
@@ -750,13 +752,22 @@
         for r, target in others:
             to_low(j, r, target).start()
         weight_part(j + 1, turned_ref, low[j])
-        to_x(j + 1).start()
+
+        @pl.when(j == 0)
+        def _():
+            to_x(1).start()
 
         @pl.when(j == pairs - 1)
         def _():
             for half in range(2):
                 normed.arrive(half)
                 grads.arrive(half)
+            to_x(2).start()
+
+            @pl.when(c == 0)
+            def _():
+                to_x(3).start()
+
             makes(1, 4)
             first_a()
 
@@ -925,11 +936,11 @@
             slot = 2 * flip(y, yy) + flip(c, cc)
             p = 5 * yy + 3 * cc
             wide = 128 * (3 - cc)
-            gout_ref[:, 128 * p : 128 * p + wide] = fin[slot, 0, :, :wide]
+            gout_ref[:, 128 * p : 128 * p + wide] = fin[slot, 0, :, :wide].astype(F32)
             for j in range(3 - cc):
                 for t in range(3):
                     at = t * width + 128 * (p + j)
-                    gqkv_ref[:, at : at + 128] = fin[slot, j + 1, :, 128 * t : 128 * t + 128]
+                    gqkv_ref[:, at : at + 128] = fin[slot, j + 1, :, 128 * t : 128 * t + 128].astype(F32)
     outs.append(pltpu.make_async_copy(gqkv_ref, gqkv_out, outsem.at[4]))
     outs[-1].start()
     outs.append(pltpu.make_async_copy(gout_ref, gout_out, outsem.at[5]))
@@ -1024,7 +1035,7 @@
             v((4, 2, 2, 2, share, 384), BF16), v((3, 2, 2, share, 384), BF16), v((3, 2, 2, share, 384), BF16),
             v((3, 2, share, 384), BF16), v((3, 2, share, 384), BF16),
             v((2, 2, share, 384), BF16), v((2, 2, share, 384), BF16), v((2, share, 384), BF16),
-            v((4, 4, share // 4, 384), F32), v((4, 4, share // 4, 384), F32),
+            v((4, 4, share // 4, 384), BF16), v((4, 4, share // 4, 384), BF16),
             v((4, 3, count, 384), BF16),
             v((8, width), F32), v((8, 8, 256), F32), v((8, 8, 256), F32), v((4, 8, 256), F32),
             dma((2,)), dma((3, 3)), dma((3,)), dma((3,)), dma((3, 4)), dma((2, 4)), dma((4, 3)), dma((4, 3)),

time: 128 us -> 127 us (level)
  no operation moved by 1% of the time
where the time goes in v7:
time: 127 us
  Pallas kernels  126 us (99%)
    pallas_call x1, Pallas kernels, whole_layer(): pl.pallas_call(layer_kernel, out_shape=(jax.ShapeDtypeStruct((count, widt...  122 us
    pallas_call x1, Pallas kernels, finish(): pl.pallas_call(functools.partial(finish_kernel, cells), out_shape=(small,...  4.07 us

profile of v7, /device:TPU:0, one launch (start us, length us, event | category | flops | bytes accessed | tf_op | source)
XLA Modules:
  0.0 126.9 jit_solution(11408044669239724128)
XLA Ops:
  0.6 122.0 %shard_map.202 = (bf16[128,1280]{1,0:T(8,128)(2,1)}, bf16[128,1280]{1,0:T(8,128)(2,1)}, f32[40,3840]{1,0:T(8,128)}, f32[40,1280]{1,0:T(8,128)}, f32[40,5120]{1,0...) custom-call(s32[1,4]{1,0:T(1,128)} %cls_ref.1, bf16[128,1280]{1,0:T(8,128)(2,1)} %bitcast.10, ...), custom_call_target="tpu_custom_call" | custom-call | flops 42949672960 | bytes 52428800 | tf_op jit(solution)/shard_map/pallas_call | solution.py:1003
  122.7 4.1 %shard_map.203 = (f32[1,40]{1,0:T(1,128)}, f32[1,40]{1,0:T(1,128)}, f32[1,40]{1,0:T(1,128)}, f32[1,40]{1,0:T(1,128)}, f32[1,40]{1,0:T(1,128)}, /*index=5*/f32[1,...) custom-call(f32[8,40]{1,0:T(8,128)} %get-tuple-element.31.sums_ref, ...), custom_call_target="tpu_custom_call" | custom-call | tf_op jit(solution)/shard_map/pallas_call | solution.py:984

commit v8 on v7

--- a/solution.py
+++ b/solution.py
@@ -639,9 +639,32 @@
         return remote(zlast.at[s - 1, 0], zlast.at[s - 1, 1], zsend.at[s, 1], zrecv.at[s, 1], (2 * half_z + x, blk))
 
     other_half, my_half = 1 - z // 2, z // 2
-    first_pair = remote(part.at[0, :, 1 - even], zfirst, zsend.at[0, 0], zrecv.at[0, 0], (2 * pair_z + x, blk))
-    first_half = remote(hfirst.at[0], hfirst.at[1], zsend.at[0, 1], zrecv.at[0, 1], (2 * half_z + x, blk))
-    first_x = remote(xfirst.at[0], xfirst.at[1], xsend.at[0], xrecv.at[0], xpeer)
+    def first_moves(wide):
+        lanes = pl.ds(0, wide)
+        return (
+            lambda: remote(
+                part.at[0, :, 1 - even, :, :, lanes], zfirst.at[:, :, :, lanes], zsend.at[0, 0], zrecv.at[0, 0],
+                (2 * pair_z + x, blk),
+            ),
+            lambda: remote(
+                hfirst.at[0, :, :, lanes], hfirst.at[1, :, :, lanes], zsend.at[0, 1], zrecv.at[0, 1],
+                (2 * half_z + x, blk),
+            ),
+            lambda: remote(xfirst.at[0, :, lanes], xfirst.at[1, :, lanes], xsend.at[0], xrecv.at[0], xpeer),
+        )
+
+    def first_move(stage, act):
+        for core in range(2):
+
+            @pl.when(c == core)
+            def _():
+                act(first_moves(128 * (3 - core))[stage]())
+
+    def begin(copy):
+        copy.start()
+
+    def finish_copy(copy):
+        copy.wait()
 
     def to_blk(s, r, target):
         return remote(full.at[s, target[1]], fin.at[r, s], fsend.at[r, s], frecv.at[r, s], target)
@@ -675,21 +698,21 @@
         fin[0, s] = full[s, blk]
 
     def first_a():
-        first_pair.wait()
+        first_move(0, finish_copy)
         for xx in range(2):
             hfirst[0, xx] = (part[0, xx, even, other_half].astype(F32) + zfirst[xx, other_half].astype(F32)).astype(BF16)
-        first_half.start()
+        first_move(1, begin)
 
     def first_sum(xx):
         return part[0, xx, even, my_half].astype(F32) + zfirst[xx, my_half].astype(F32) + hfirst[1, xx].astype(F32)
 
     def first_b():
-        first_half.wait()
+        first_move(1, finish_copy)
         xfirst[0] = first_sum(1 - x).astype(BF16)
-        first_x.start()
+        first_move(2, begin)
 
     def first_c():
-        first_x.wait()
+        first_move(2, finish_copy)
         to_owners(0, first_sum(x) + xfirst[1].astype(F32))
 
     def weight_part(s, left, right):
@@ -708,7 +731,7 @@
         right = grow[:, :, pl.ds(pl.multiple_of(first * 128, 128), 256)].reshape(row_len, 256)
         weight_part(0, aturned_ref, jnp.concatenate([right, jnp.zeros((row_len, 128), BF16)], axis=1))
 
-    first_pair.start()
+    first_move(0, begin)
     normed.forward(3)
     to_sibling = []
     for kind, source, box in ((0, part_in, sib_in), (1, part_dn, sib_dn)):

time: 127 us -> 127 us (level)
  no operation moved by 1% of the time
where the time goes in v8:
time: 127 us
  Pallas kernels  126 us (99%)
    pallas_call x1, Pallas kernels, whole_layer(): pl.pallas_call(layer_kernel, out_shape=(jax.ShapeDtypeStruct((count, widt...  122 us
    pallas_call x1, Pallas kernels, finish(): pl.pallas_call(functools.partial(finish_kernel, cells), out_shape=(small,...  4.07 us

profile of v8, /device:TPU:0, one launch (start us, length us, event | category | flops | bytes accessed | tf_op | source)
XLA Modules:
  0.0 126.9 jit_solution(14908835868405888734)
XLA Ops:
  0.6 122.0 %shard_map.202 = (bf16[128,1280]{1,0:T(8,128)(2,1)}, bf16[128,1280]{1,0:T(8,128)(2,1)}, f32[40,3840]{1,0:T(8,128)}, f32[40,1280]{1,0:T(8,128)}, f32[40,5120]{1,0...) custom-call(s32[1,4]{1,0:T(1,128)} %cls_ref.1, bf16[128,1280]{1,0:T(8,128)(2,1)} %bitcast.10, ...), custom_call_target="tpu_custom_call" | custom-call | flops 42949672960 | bytes 52428800 | tf_op jit(solution)/shard_map/pallas_call | solution.py:1026
  122.7 4.1 %shard_map.203 = (f32[1,40]{1,0:T(1,128)}, f32[1,40]{1,0:T(1,128)}, f32[1,40]{1,0:T(1,128)}, f32[1,40]{1,0:T(1,128)}, f32[1,40]{1,0:T(1,128)}, /*index=5*/f32[1,...) custom-call(f32[8,40]{1,0:T(8,128)} %get-tuple-element.31.sums_ref, ...), custom_call_target="tpu_custom_call" | custom-call | tf_op jit(solution)/shard_map/pallas_call | solution.py:1007

commit v9 on v8

--- a/solution.py
+++ b/solution.py
@@ -939,6 +939,14 @@
     def _():
         add_half(3)
 
+    for r, target in others:
+        to_blk(0, r, target).wait_recv()
+    for yy in range(2):
+        for cc in range(2):
+            p, wide = 5 * yy + 3 * cc, 128 * (3 - cc)
+            gout_ref[:, 128 * p : 128 * p + wide] = fin[2 * flip(y, yy) + flip(c, cc), 0, :, :wide].astype(F32)
+    outs.append(pltpu.make_async_copy(gout_ref, gout_out, outsem.at[5]))
+    outs[-1].start()
     end_down()
     end_t()
     end_q()
@@ -950,7 +958,7 @@
 
     for r, target, count in received:
 
-        @pl.loop(0, count + 1)
+        @pl.loop(1, count + 1)
         def _(s):
             to_blk(s, r, target).wait_recv()
 
@@ -958,15 +966,11 @@
         for cc in range(2):
             slot = 2 * flip(y, yy) + flip(c, cc)
             p = 5 * yy + 3 * cc
-            wide = 128 * (3 - cc)
-            gout_ref[:, 128 * p : 128 * p + wide] = fin[slot, 0, :, :wide].astype(F32)
             for j in range(3 - cc):
                 for t in range(3):
                     at = t * width + 128 * (p + j)
                     gqkv_ref[:, at : at + 128] = fin[slot, j + 1, :, 128 * t : 128 * t + 128].astype(F32)
     outs.append(pltpu.make_async_copy(gqkv_ref, gqkv_out, outsem.at[4]))
-    outs[-1].start()
-    outs.append(pltpu.make_async_copy(gout_ref, gout_out, outsem.at[5]))
     outs[-1].start()
 
     @pl.loop(0, pairs)

time: 127 us -> 127 us (level)
  no operation moved by 1% of the time
where the time goes in v9:
time: 127 us
  Pallas kernels  126 us (99%)
    pallas_call x1, Pallas kernels, whole_layer(): pl.pallas_call(layer_kernel, out_shape=(jax.ShapeDtypeStruct((count, widt...  122 us
    pallas_call x1, Pallas kernels, finish(): pl.pallas_call(functools.partial(finish_kernel, cells), out_shape=(small,...  4.07 us

profile of v9, /device:TPU:0, one launch (start us, length us, event | category | flops | bytes accessed | tf_op | source)
XLA Modules:
  0.0 126.8 jit_solution(7965319026135131248)
XLA Ops:
  0.6 121.9 %shard_map.202 = (bf16[128,1280]{1,0:T(8,128)(2,1)}, bf16[128,1280]{1,0:T(8,128)(2,1)}, f32[40,3840]{1,0:T(8,128)}, f32[40,1280]{1,0:T(8,128)}, f32[40,5120]{1,0...) custom-call(s32[1,4]{1,0:T(1,128)} %cls_ref.1, bf16[128,1280]{1,0:T(8,128)(2,1)} %bitcast.10, ...), custom_call_target="tpu_custom_call" | custom-call | flops 42949672960 | bytes 52428800 | tf_op jit(solution)/shard_map/pallas_call | solution.py:1030
  122.5 4.1 %shard_map.203 = (f32[1,40]{1,0:T(1,128)}, f32[1,40]{1,0:T(1,128)}, f32[1,40]{1,0:T(1,128)}, f32[1,40]{1,0:T(1,128)}, f32[1,40]{1,0:T(1,128)}, /*index=5*/f32[1,...) custom-call(f32[8,40]{1,0:T(8,128)} %get-tuple-element.31.sums_ref, ...), custom_call_target="tpu_custom_call" | custom-call | tf_op jit(solution)/shard_map/pallas_call | solution.py:1011
